TPU v7x, 32 devices: a whole 2x2x4 slice. The times are simulated.
32 devices in a mesh: dp: 8 (over z, core), tensor: 4 (over y, x).
Axes of the slice: x: 2, y: 2, z: 4, core: 2. Of those that a mesh axis runs over, the one named last changes fastest.
Arguments:
- inputs: bfloat16 [49152, 512], P(('dp', 'tensor')), may hold values from -6 to 6
- w_qkv: bfloat16 [2, 3, 512, 512], P(None, None, 'dp', 'tensor'), may hold values from -0.25 to 0.25
- w_out: bfloat16 [2, 512, 512], P(None, 'tensor', 'dp'), may hold values from -0.75 to 0.75
- w_up: bfloat16 [2, 512, 2048], P(None, 'dp', 'tensor'), may hold values from -0.25 to 0.25
- w_down: bfloat16 [2, 2048, 512], P(None, 'tensor', 'dp'), may hold values from -0.125 to 0.125
- ln_gain: float32 [2, 2, 512], replicated, may hold values from 0.5 to 1.5
- ln_bias: float32 [2, 2, 512], replicated, may hold values from -3 to 3
- bias_qv: float32 [2, 2, 512], P(None, None, 'tensor'), may hold values from -3 to 3
- bias_up: float32 [2, 2048], P(None, 'tensor'), may hold values from -3 to 3
- branch_bias: float32 [2, 2, 512], replicated, may hold values from -3 to 3
- cotangent: float32 [49152, 512], P(('dp', 'tensor')), may hold values from -6 to 6
Outputs:
- outputs: bfloat16 [49152, 512], P(('dp', 'tensor'))
- input_grad: float32 [49152, 512], P(('dp', 'tensor'))
- grad_qkv: float32 [2, 3, 512, 512], P(None, None, 'dp', 'tensor')
- grad_out: float32 [2, 512, 512], P(None, 'tensor', 'dp')
- grad_up: float32 [2, 512, 2048], P(None, 'dp', 'tensor')
- grad_down: float32 [2, 2048, 512], P(None, 'tensor', 'dp')
- grad_ln_gain: float32 [2, 2, 512], replicated
- grad_ln_bias: float32 [2, 2, 512], replicated
- grad_bias_qv: float32 [2, 2, 512], P(None, None, 'tensor')
- grad_bias_up: float32 [2, 2048], P(None, 'tensor')
- grad_branch_bias: float32 [2, 2, 512], replicated
All inputs are finite; a program needn't handle non-finite values.
Results may differ from a plain program's by a relative error of at most 0.025.
Values may be sent and summed in bfloat16 or wider, within the bound.
A program may use at most 320 MiB of HBM per device.

v0:
```python
import math

import jax
import jax.numpy as jnp
from jax import lax
from jax.sharding import PartitionSpec as P

HD = 64
SPAN = 128
LEN = 2048
LAYERS = 2


highest = lax.Precision.HIGHEST
epsilon = 1e-05
masked_score = -1e30


def normalize(rows, gain, shift):
    centre = rows - jnp.mean(rows, -1, keepdims=True)
    spread = jnp.mean(centre * centre, -1, keepdims=True)
    return centre * lax.rsqrt(spread + epsilon) * gain + shift


def gelu_exact(values):
    return jax.nn.gelu(values, approximate=False)


def to_heads(rows):
    return rows.reshape(-1, LEN // SPAN, SPAN, rows.shape[1] // HD, HD)


def score_blocks(head_queries, head_keys, key_mean):
    scale = HD ** (-0.5)
    blocks = LEN // SPAN
    direct = (
        jnp.einsum(
            "gbihe,gbjhe->gbhij", head_queries, head_keys, preferred_element_type=jnp.float32
        )
        * scale
    )
    summary = jnp.einsum(
        "gbihe,gche->gbhic", head_queries.astype(jnp.float32), key_mean, precision=highest
    ) * scale + math.log(SPAN)
    inside = lax.broadcasted_iota(jnp.int32, (SPAN, SPAN), 0) >= lax.broadcasted_iota(
        jnp.int32, (SPAN, SPAN), 1
    )
    earlier = lax.broadcasted_iota(jnp.int32, (blocks, 1, 1, blocks), 0) > lax.broadcasted_iota(
        jnp.int32, (blocks, 1, 1, blocks), 3
    )
    return (jnp.where(inside, direct, masked_score), jnp.where(earlier, summary, masked_score))


def attend(query_rows, key_rows, value_rows):
    head_queries, head_keys, head_values = (
        to_heads(query_rows),
        to_heads(key_rows),
        to_heads(value_rows),
    )
    key_mean = jnp.mean(head_keys.astype(jnp.float32), 2)
    value_mean = jnp.mean(head_values.astype(jnp.float32), 2)
    direct, summary = score_blocks(head_queries, head_keys, key_mean)
    top = jnp.maximum(jnp.max(direct, -1), jnp.max(summary, -1))[..., None]
    direct_weight = jnp.exp(direct - top)
    summary_weight = jnp.exp(summary - top)
    total = jnp.sum(direct_weight, -1, keepdims=True) + jnp.sum(summary_weight, -1, keepdims=True)
    direct_prob = direct_weight / total
    summary_prob = summary_weight / total
    mixed = jnp.einsum(
        "gbhij,gbjhe->gbihe",
        direct_prob.astype(jnp.bfloat16),
        head_values,
        preferred_element_type=jnp.float32,
    )
    mixed = mixed + jnp.einsum("gbhic,gche->gbihe", summary_prob, value_mean, precision=highest)
    log_total = (top + jnp.log(total))[..., 0]
    return (mixed.reshape(query_rows.shape), log_total)


def attend_back(query_rows, key_rows, value_rows, log_total, grad_rows):
    scale = HD ** (-0.5)
    head_queries, head_keys, head_values = (
        to_heads(query_rows),
        to_heads(key_rows),
        to_heads(value_rows),
    )
    head_grads = to_heads(grad_rows)
    key_mean = jnp.mean(head_keys.astype(jnp.float32), 2)
    value_mean = jnp.mean(head_values.astype(jnp.float32), 2)
    direct, summary = score_blocks(head_queries, head_keys, key_mean)
    direct_prob = jnp.exp(direct - log_total[..., None])
    summary_prob = jnp.exp(summary - log_total[..., None])
    grad_float = head_grads.astype(jnp.float32)
    query_float = head_queries.astype(jnp.float32)
    direct_grad = jnp.einsum(
        "gbihe,gbjhe->gbhij", head_grads, head_values, preferred_element_type=jnp.float32
    )
    summary_grad = jnp.einsum("gbihe,gche->gbhic", grad_float, value_mean, precision=highest)
    centre = jnp.sum(direct_prob * direct_grad, -1, keepdims=True) + jnp.sum(
        summary_prob * summary_grad, -1, keepdims=True
    )
    direct_score = (direct_prob * (direct_grad - centre)).astype(jnp.bfloat16)
    summary_score = summary_prob * (summary_grad - centre)
    grad_query = jnp.einsum(
        "gbhij,gbjhe->gbihe", direct_score, head_keys, preferred_element_type=jnp.float32
    )
    grad_query = (
        grad_query + jnp.einsum("gbhic,gche->gbihe", summary_score, key_mean, precision=highest)
    ) * scale
    key_block = jnp.einsum("gbhic,gbihe->gche", summary_score, query_float, precision=highest) * (
        scale / SPAN
    )
    grad_key = (
        jnp.einsum(
            "gbhij,gbihe->gbjhe", direct_score, head_queries, preferred_element_type=jnp.float32
        )
        * scale
        + key_block[:, :, None]
    )
    value_block = (
        jnp.einsum("gbhic,gbihe->gche", summary_prob, grad_float, precision=highest) / SPAN
    )
    grad_value = (
        jnp.einsum(
            "gbhij,gbihe->gbjhe",
            direct_prob.astype(jnp.bfloat16),
            head_grads,
            preferred_element_type=jnp.float32,
        )
        + value_block[:, :, None]
    )
    shape = query_rows.shape
    return (grad_query.reshape(shape), grad_key.reshape(shape), grad_value.reshape(shape))


def fetch(first, second, third, fourth):
    return (
        lax.all_gather(first, "dp", axis=2, tiled=True),
        lax.all_gather(second, "dp", axis=2, tiled=True),
        lax.all_gather(third, "dp", axis=1, tiled=True),
        lax.all_gather(fourth, "dp", axis=2, tiled=True),
    )


def return_grads(first, second, third, fourth):
    return (
        lax.psum_scatter(first.astype(jnp.bfloat16), "dp", scatter_dimension=2, tiled=True).astype(
            jnp.float32
        ),
        lax.psum_scatter(second.astype(jnp.bfloat16), "dp", scatter_dimension=2, tiled=True).astype(
            jnp.float32
        ),
        lax.psum_scatter(third.astype(jnp.bfloat16), "dp", scatter_dimension=1, tiled=True).astype(
            jnp.float32
        ),
        lax.psum_scatter(fourth.astype(jnp.bfloat16), "dp", scatter_dimension=2, tiled=True).astype(
            jnp.float32
        ),
    )


def layer_weights(w_qkv, w_out, w_up, w_down, layer):
    gathered = fetch(
        w_qkv[layer : layer + 1],
        w_out[layer : layer + 1],
        w_up[layer : layer + 1],
        w_down[layer : layer + 1],
    )
    return tuple((part[0] for part in gathered))


def spread_only(rows, project):
    return project(lax.all_gather(rows, "tensor", axis=0, tiled=True))


def fold_again(rows, grads):
    return jnp.einsum(
        "td,tc->dc",
        lax.all_gather(rows, "tensor", axis=0, tiled=True),
        grads,
        preferred_element_type=jnp.float32,
    )


def spread_grads(rows, project):
    piece = lax.all_gather(rows, "tensor", axis=0, tiled=True)
    return (piece, project(piece))


def slice_term(source, weight, form):
    return jnp.einsum(form, source, weight, preferred_element_type=jnp.float32)


def rows_sum(source, weight, form):
    return lax.psum_scatter(
        slice_term(source, weight, form).astype(jnp.bfloat16),
        "tensor",
        scatter_dimension=0,
        tiled=True,
    ).astype(jnp.float32)


def grads_sum(source, weight, form):
    return lax.psum_scatter(
        slice_term(source, weight, form).astype(jnp.bfloat16),
        "tensor",
        scatter_dimension=0,
        tiled=True,
    ).astype(jnp.float32)


def group_rows(token_att, out_whole):
    groups = lax.axis_size("tensor")
    parts = token_att.reshape(token_att.shape[0], groups, -1)
    grouped = out_whole.reshape(groups, -1, out_whole.shape[1])
    partial_value = jnp.einsum("tgc,gcd->tgd", parts, grouped, preferred_element_type=jnp.float32)
    return jnp.sum(partial_value.astype(jnp.bfloat16), 1, dtype=jnp.float32)


def group_grads(token_grads, qkv_whole):
    groups = lax.axis_size("tensor")
    parts = token_grads.reshape(token_grads.shape[0], 3, groups, -1)
    grouped = qkv_whole.reshape(3, qkv_whole.shape[1], groups, -1)
    partial_value = jnp.einsum("tsgc,sdgc->tgd", parts, grouped, preferred_element_type=jnp.float32)
    return jnp.sum(partial_value.astype(jnp.bfloat16), 1, dtype=jnp.float32)


def forward_layer(residual, matrices, gains, shifts, bias_pair, bias_hidden, branch_pair):
    w_qkv, w_out, w_up, w_down = matrices
    attn_in = normalize(residual, gains[0], shifts[0]).astype(jnp.bfloat16)

    def project_qkv(piece):
        return jnp.einsum("td,sdc->tsc", piece, w_qkv, preferred_element_type=jnp.float32)

    def project_up(piece):
        return jnp.dot(piece, w_up, preferred_element_type=jnp.float32)

    mixed_qkv = spread_only(attn_in, project_qkv)
    queries = (mixed_qkv[:, 0] + bias_pair[0]).astype(jnp.bfloat16)
    keys_now = mixed_qkv[:, 1].astype(jnp.bfloat16)
    values_now = (mixed_qkv[:, 2] + bias_pair[1]).astype(jnp.bfloat16)
    mixed, log_total = attend(queries, keys_now, values_now)
    attended = mixed.astype(jnp.bfloat16)
    qkv_whole, out_whole = (
        lax.all_gather(w_qkv, "tensor", axis=2, tiled=True),
        lax.all_gather(w_out, "tensor", axis=0, tiled=True),
    )
    token_att = lax.all_to_all(attended, "tensor", split_axis=0, concat_axis=1, tiled=True)
    attn_branch = group_rows(token_att, out_whole)
    middle = residual + attn_branch + branch_pair[0]
    mlp_in = normalize(middle, gains[1], shifts[1]).astype(jnp.bfloat16)
    raised = spread_only(mlp_in, project_up)
    hidden = raised + bias_hidden
    activated = gelu_exact(hidden).astype(jnp.bfloat16)
    result = middle + rows_sum(activated, w_down, "tc,cd->td") + branch_pair[1]
    saved = (
        residual,
        middle,
        attn_in,
        mlp_in,
        None,
        None,
        queries,
        keys_now,
        values_now,
        log_total,
        attended,
        hidden,
        activated,
        qkv_whole,
    )
    return (result, saved)


def backward_layer(grad_residual, saved, matrices, gains, shifts):
    w_qkv, w_out, w_up, w_down = matrices
    (
        residual,
        middle,
        attn_in,
        mlp_in,
        attn_rows,
        mlp_rows,
        queries,
        keys_now,
        values_now,
        log_total,
        attended,
        hidden,
        activated,
        qkv_whole,
    ) = saved
    down_bias_grad = jnp.sum(grad_residual, 0)

    def back_down(piece):
        return jnp.einsum("td,fd->tf", piece, w_down, preferred_element_type=jnp.float32)

    gathered_out, grad_act = spread_grads(grad_residual.astype(jnp.bfloat16), back_down)
    down_grad = jnp.einsum("tf,td->fd", activated, gathered_out, preferred_element_type=jnp.float32)
    grad_hidden = jax.vjp(gelu_exact, hidden)[1](grad_act)[0].astype(jnp.bfloat16)
    up_bias_grad = jnp.sum(grad_hidden, 0, dtype=jnp.float32)
    up_grad = fold_again(mlp_in, grad_hidden)
    grad_mlp_in = grads_sum(grad_hidden, w_up, "tf,df->td")
    norm_back = jax.vjp(normalize, middle, gains[1], shifts[1])[1]
    grad_norm, gain_second, shift_second = norm_back(grad_mlp_in)
    grad_middle = grad_residual + grad_norm
    attn_bias_grad = jnp.sum(grad_middle, 0)

    def back_out(piece):
        return jnp.einsum("td,cd->tc", piece, w_out, preferred_element_type=jnp.float32)

    gathered_mid, grad_attended = spread_grads(grad_middle.astype(jnp.bfloat16), back_out)
    out_grad = jnp.einsum("tc,td->cd", attended, gathered_mid, preferred_element_type=jnp.float32)
    grad_query, grad_key, grad_value = attend_back(
        queries, keys_now, values_now, log_total, grad_attended.astype(jnp.bfloat16)
    )
    grad_query = grad_query.astype(jnp.bfloat16)
    grad_key = grad_key.astype(jnp.bfloat16)
    grad_value = grad_value.astype(jnp.bfloat16)
    pair_grad = jnp.stack(
        [jnp.sum(grad_query, 0, dtype=jnp.float32), jnp.sum(grad_value, 0, dtype=jnp.float32)]
    )
    stacked = jnp.stack([grad_query, grad_key, grad_value], 1)
    flat_grad = fold_again(attn_in, stacked.reshape(stacked.shape[0], -1))
    qkv_grad = jnp.transpose(flat_grad.reshape(flat_grad.shape[0], 3, -1), (1, 0, 2))
    token_grads = lax.all_to_all(stacked, "tensor", split_axis=0, concat_axis=2, tiled=True)
    grad_attn_in = group_grads(token_grads, qkv_whole)
    first_back = jax.vjp(normalize, residual, gains[0], shifts[0])[1]
    grad_first, gain_first, shift_first = first_back(grad_attn_in)
    grad_input = grad_middle + grad_first
    matrix_part = (qkv_grad[None], out_grad[None], up_grad[None], down_grad[None])
    shared_part = (
        jnp.stack([gain_first, gain_second]),
        jnp.stack([shift_first, shift_second]),
        jnp.stack([attn_bias_grad, down_bias_grad]),
    )
    head_part = (pair_grad, up_bias_grad)
    return (grad_input, matrix_part, shared_part, head_part)


def body(
    inputs, w_qkv, w_out, w_up, w_down, ln_gain, ln_bias, bias_qv, bias_up, branch_bias, cotangent
):
    residual = inputs.astype(jnp.float32)
    saved_all = []
    for layer in range(LAYERS):
        matrices = layer_weights(w_qkv, w_out, w_up, w_down, layer)
        residual, saved = forward_layer(
            residual,
            matrices,
            ln_gain[layer],
            ln_bias[layer],
            bias_qv[layer],
            bias_up[layer],
            branch_bias[layer],
        )
        saved_all.append(saved)
    outputs = residual.astype(jnp.bfloat16)
    grad_residual = cotangent
    matrix_grads = [None] * LAYERS
    shared_grads = [None] * LAYERS
    head_grads = [None] * LAYERS
    for layer in reversed(range(LAYERS)):
        matrices = layer_weights(w_qkv, w_out, w_up, w_down, layer)
        grad_residual, matrix_part, shared_part, head_part = backward_layer(
            grad_residual, saved_all[layer], matrices, ln_gain[layer], ln_bias[layer]
        )
        matrix_grads[layer] = return_grads(
            matrix_part[0], matrix_part[1], matrix_part[2], matrix_part[3]
        )
        shared_grads[layer] = shared_part
        head_grads[layer] = head_part
    joined = [jnp.concatenate([grads[index] for grads in matrix_grads], 0) for index in range(4)]
    gain_total = jnp.stack([grads[0] for grads in shared_grads])
    shift_total = jnp.stack([grads[1] for grads in shared_grads])
    branch_total = jnp.stack([grads[2] for grads in shared_grads])
    gain_sum, shift_sum, branch_sum = lax.psum(
        (gain_total, shift_total, branch_total), ("dp", "tensor")
    )
    pair_total = jnp.stack([grads[0] for grads in head_grads])
    hidden_total = jnp.stack([grads[1] for grads in head_grads])
    pair_sum, hidden_sum = lax.psum((pair_total, hidden_total), "dp")
    return (
        outputs,
        grad_residual,
        joined[0],
        joined[1],
        joined[2],
        joined[3],
        gain_sum,
        shift_sum,
        pair_sum,
        hidden_sum,
        branch_sum,
    )


def solution(mesh):
    return jax.shard_map(
        body,
        mesh=mesh,
        in_specs=(
            P(("dp", "tensor"), None),
            P(None, None, "dp", "tensor"),
            P(None, "tensor", "dp"),
            P(None, "dp", "tensor"),
            P(None, "tensor", "dp"),
            P(),
            P(),
            P(None, None, "tensor"),
            P(None, "tensor"),
            P(),
            P(("dp", "tensor"), None),
        ),
        out_specs=(
            P(("dp", "tensor"), None),
            P(("dp", "tensor"), None),
            P(None, None, "dp", "tensor"),
            P(None, "tensor", "dp"),
            P(None, "dp", "tensor"),
            P(None, "tensor", "dp"),
            P(),
            P(),
            P(None, None, "tensor"),
            P(None, "tensor"),
            P(),
        ),
        check_vma=False,
    )
```

profile of v0, /device:TPU:0, one launch (start us, length us, event | category | flops | bytes accessed | tf_op | source)
XLA Modules:
  0.0 1674.3 jit_solution(17339127591960681586)
XLA Ops:
  16.2 16.2 all_gather.71
  32.4 55.4 %all-gather.15.cloned.1.call-done = bf16[6144,512]{1,0:T(8,128)(2,1)} async-done(((bf16[1536,512]{1,0:T(8,128)(2,1)}), bf16[6144,512]{1,0:T(8,128)(2,1)}) %all-gather.15.cloned.1.call-update) | async-done | bytes 6291472 | tf_op jit(solution)/shard_map/all_gather | solution.py:173
  180.8 15.9 all_gather.75
  196.7 16.0 all_gather.76
  212.7 36.4 %all-gather.17.cloned.1.call-done = bf16[6144,512]{1,0:T(8,128)(2,1)} async-done(((bf16[1536,512]{1,0:T(8,128)(2,1)}), bf16[6144,512]{1,0:T(8,128)(2,1)}) %all-gather.17.cloned.1.call-update) | async-done | bytes 6291472 | tf_op jit(solution)/shard_map/all_gather | solution.py:173
  249.1 33.3 %multiply_convert_fusion.1 = (bf16[6144,512]{1,0:T(8,128)(2,1)S(1)}, f32[6144,512]{1,0:T(8,128)}, f32[6144,512]{1,0:T(8,128)}) fusion(f32[512]{0:T(512)S(1)} %bitcast.514, bf16[6144,512]{1,0:T(8,128)(2,1)} %all-gather.17.cloned.1.call-done, bf16[1,512,512]{2,1,0:T(8,128)(2,1)} %all_gather.75), kind=kOutput, calls=%fused_computation.28 | convolution fusion | flops 3428843520 | bytes 38275072 | tf_op jit(solution)/shard_map/dot_general | solution.py:236
  290.6 70.3 %reduce-scatter.21.cloned.1.call-done = bf16[1536,512]{1,0:T(8,128)(2,1)} async-done(((bf16[6144,512]{1,0:T(8,128)(2,1)}), bf16[1536,512]{1,0:T(8,128)(2,1)}) %reduce-scatter.21.cloned.1.call-update) | async-done | bytes 1572880 | tf_op jit(solution)/shard_map/reduce_scatter | solution.py:195
  381.1 55.4 %all-gather.19.cloned.1.call-done = bf16[6144,512]{1,0:T(8,128)(2,1)} async-done(((bf16[1536,512]{1,0:T(8,128)(2,1)}), bf16[6144,512]{1,0:T(8,128)(2,1)}) %all-gather.19.cloned.1.call-update) | async-done | bytes 6291472 | tf_op jit(solution)/shard_map/all_gather | solution.py:173
  533.6 15.0 all_gather.82
  563.4 37.6 %all-gather.21.cloned.1.call-done = bf16[6144,512]{1,0:T(8,128)(2,1)} async-done(((bf16[1536,512]{1,0:T(8,128)(2,1)}), bf16[6144,512]{1,0:T(8,128)(2,1)}) %all-gather.21.cloned.1.call-update) | async-done | bytes 6291472 | tf_op jit(solution)/shard_map/all_gather | solution.py:173
  601.0 33.1 %multiply_convert_fusion = (bf16[6144,512]{1,0:T(8,128)(2,1)}, f32[6144,512]{1,0:T(8,128)}, f32[6144,512]{1,0:T(8,128)}) fusion(f32[512]{0:T(512)S(1)} %bitcast.517, bf16[6144,512]{1,0:T(8,128)(2,1)} %all-gather.21.cloned.1.call-done, bf16[1,512,512]{2,1,0:T(8,128)(2,1)S(1)} %all_gather.82), kind=kOutput, calls=%fused_computation.14 | convolution fusion | flops 3428843520 | bytes 38275072 | tf_op jit(solution)/shard_map/dot_general | solution.py:236
  634.0 38.8 %all-gather.23.cloned.1.call-done = bf16[6144,512]{1,0:T(8,128)(2,1)} async-done(((bf16[1536,512]{1,0:T(8,128)(2,1)}), bf16[6144,512]{1,0:T(8,128)(2,1)}) %all-gather.23.cloned.1.call-update) | async-done | bytes 6291472 | tf_op jit(solution)/shard_map/all_gather | solution.py:186
  703.6 61.8 %reduce-scatter.25.cloned.1.call-done = bf16[1536,512]{1,0:T(8,128)(2,1)} async-done(((bf16[6144,512]{1,0:T(8,128)(2,1)}), bf16[1536,512]{1,0:T(8,128)(2,1)}) %reduce-scatter.25.cloned.1.call-update) | async-done | bytes 1572880 | tf_op jit(solution)/shard_map/reduce_scatter | solution.py:204
  771.2 67.4 %reduce-scatter.23.cloned.1.call-done = bf16[1536,512]{1,0:T(8,128)(2,1)} async-done(((bf16[6144,512]{1,0:T(8,128)(2,1)}), bf16[1536,512]{1,0:T(8,128)(2,1)}) %reduce-scatter.23.cloned.1.call-update) | async-done | bytes 1572880 | tf_op jit(solution)/shard_map/reduce_scatter | solution.py:195
  846.8 70.3 %all-gather.25.cloned.1.call-done = bf16[6144,512]{1,0:T(8,128)(2,1)} async-done(((bf16[1536,512]{1,0:T(8,128)(2,1)}), bf16[6144,512]{1,0:T(8,128)(2,1)}) %all-gather.25.cloned.1.call-update) | async-done | bytes 6291472 | tf_op jit(solution)/shard_map/all_gather | solution.py:186
  994.4 69.0 %all-gather.31.cloned.1.call-done = bf16[1,3,512,512]{3,2,1,0:T(8,128)(2,1)} async-done(((bf16[1,3,512,128]{3,2,1,0:T(8,128)(2,1)}), bf16[1,3,512,512]{3,2,1,0:T(8,128)(2,1)}) %all-gather.31.cloned.1.call-update) | async-done | bytes 1572880 | tf_op jit(solution)/shard_map/all_gather | solution.py:245
  1092.6 72.9 %all-gather.27.cloned.1.call-done = bf16[6144,512]{1,0:T(8,128)(2,1)} async-done(((bf16[1536,512]{1,0:T(8,128)(2,1)}), bf16[6144,512]{1,0:T(8,128)(2,1)}) %all-gather.27.cloned.1.call-update) | async-done | bytes 6291472 | tf_op jit(solution)/shard_map/all_gather | solution.py:186
  1202.8 54.5 %reduce-scatter.27.cloned.1.call-done = bf16[1536,512]{1,0:T(8,128)(2,1)} async-done(((bf16[6144,512]{1,0:T(8,128)(2,1)}), bf16[1536,512]{1,0:T(8,128)(2,1)}) %reduce-scatter.27.cloned.1.call-update) | async-done | bytes 1572880 | tf_op jit(solution)/shard_map/reduce_scatter | solution.py:204
  1305.1 18.0 %reduce-scatter.43.cloned.1.call-done = bf16[64,512]{1,0:T(8,128)(2,1)} async-done(((bf16[512,512]{1,0:T(8,128)(2,1)}), bf16[64,512]{1,0:T(8,128)(2,1)}) %reduce-scatter.43.cloned.1.call-update) | async-done | bytes 65552
  1333.1 60.3 %all-gather.29.cloned.1.call-done = bf16[6144,512]{1,0:T(8,128)(2,1)} async-done(((bf16[1536,512]{1,0:T(8,128)(2,1)}), bf16[6144,512]{1,0:T(8,128)(2,1)}) %all-gather.29.cloned.1.call-update) | async-done | bytes 6291472 | tf_op jit(solution)/shard_map/all_gather | solution.py:186
  1488.9 31.4 %reduce-scatter.33.cloned.1.call-done = bf16[1,64,512]{2,1,0:T(8,128)(2,1)} async-done(((bf16[1,512,512]{2,1,0:T(8,128)(2,1)}), bf16[1,64,512]{2,1,0:T(8,128)(2,1)}) %reduce-scatter.33.cloned.1.call-update) | async-done | bytes 65552 | tf_op jit(solution)/shard_map/reduce_scatter | solution.py:153
  1552.4 29.4 %reduce-scatter.31.cloned.1.call-done = bf16[1,3,64,128]{3,2,1,0:T(8,128)(2,1)} async-done(((bf16[1,3,512,128]{3,2,1,0:T(8,128)(2,1)}), bf16[1,3,64,128]{3,2,1,0:T(8,128)(2,1)}) %reduce-scatter.31.cloned.1.call-update) | async-done | bytes 49168 | tf_op jit(solution)/shard_map/reduce_scatter | solution.py:147
  1581.8 31.2 %reduce-scatter.29.cloned.1.call-done = bf16[1,3,64,128]{3,2,1,0:T(8,128)(2,1)} async-done(((bf16[1,3,512,128]{3,2,1,0:T(8,128)(2,1)}), bf16[1,3,64,128]{3,2,1,0:T(8,128)(2,1)}) %reduce-scatter.29.cloned.1.call-update) | async-done | bytes 49168 | tf_op jit(solution)/shard_map/reduce_scatter | solution.py:147
  1628.6 38.4 %all-reduce = (f32[2,2,512]{2,1,0:T(2,128)}, f32[2,2,512]{2,1,0:T(2,128)}, f32[2,2,512]{2,1,0:T(2,128)}) all-reduce(f32[2,2,512]{2,1,0:T(2,128)S(1)} %pad_maximum_fusion, f32[2,2,512]{2,1,0:T(2,128)S(1)} %pad_maximum_fusion.1, f32[2,2,512]{2,1,0:T(2,128)S(1)} %pad_maximum_fusion.2), channel_id=1, replica_groups=mesh['dp'=8,'tensor'=4] {'dp','tensor'}, use_global_device_ids=true, to_apply=%region_52.53 | all-reduce | flops 6144 | bytes 49152 | tf_op jit(solution)/shard_map/psum | solution.py:377
  (560 shorter events, 629.6 us)
Async XLA Ops:
  7.2 80.7 %all-gather.15.cloned.1.call-start = ((), (), s32[]{:S(2)}) async-start(), calls=%async_computation.16 | async-start | bytes 7864320 | tf_op jit(solution)/shard_map/all_gather | solution.py:173
  144.8 104.3 %all-gather.17.cloned.1.call-start = ((), (), s32[]{:S(2)}) async-start(), calls=%async_computation.17 | async-start | bytes 7864320 | tf_op jit(solution)/shard_map/all_gather | solution.py:173
  178.9 182.1 %reduce-scatter.21.cloned.1.call-start = ((), (), s32[]{:S(2)}) async-start(), calls=%async_computation.18 | async-start | bytes 7864320 | tf_op jit(solution)/shard_map/reduce_scatter | solution.py:195
  290.6 146.0 %all-gather.19.cloned.1.call-start = ((), (), s32[]{:S(2)}) async-start(), calls=%async_computation.19 | async-start | bytes 7864320 | tf_op jit(solution)/shard_map/all_gather | solution.py:173
  494.1 106.8 %all-gather.21.cloned.1.call-start = ((), (), s32[]{:S(2)}) async-start(), calls=%async_computation.20 | async-start | bytes 7864320 | tf_op jit(solution)/shard_map/all_gather | solution.py:173
  530.8 142.1 %all-gather.23.cloned.1.call-start = ((), (), s32[]{:S(2)}) async-start(), calls=%async_computation.22 | async-start | bytes 7864320 | tf_op jit(solution)/shard_map/all_gather | solution.py:186
  533.6 231.8 %reduce-scatter.25.cloned.1.call-start = ((), (), s32[]{:S(2)}) async-start(), calls=%async_computation.23 | async-start | bytes 7864320 | tf_op jit(solution)/shard_map/reduce_scatter | solution.py:204
  695.0 143.6 %reduce-scatter.23.cloned.1.call-start = ((), (), s32[]{:S(2)}) async-start(), calls=%async_computation.21 | async-start | bytes 7864320 | tf_op jit(solution)/shard_map/reduce_scatter | solution.py:195
  703.3 213.7 %all-gather.25.cloned.1.call-start = ((), (), s32[]{:S(2)}) async-start(), calls=%async_computation.24 | async-start | bytes 7864320 | tf_op jit(solution)/shard_map/all_gather | solution.py:186
  988.6 88.0 %all-to-all-start.2 = ((bf16[6144,3,128]{2,1,0:T(4,128)(2,1)}), bf16[6144,3,128]{2,1,0:T(4,128)(2,1)}, u32[]{:S(2)}, u32[]{:S(2)}) async-start(bf16[6144,3,128]{2,1,0:T(4,128)(2,1)} %copy.393), calls=%async_computation.5 | async-start | bytes 12582912 | tf_op jit(solution)/shard_map/all_to_all | solution.py:326
  993.8 69.6 %all-gather.31.cloned.1.call-start = ((), (), s32[]{:S(2)}) async-start(), calls=%async_computation.32 | async-start | bytes 1966080 | tf_op jit(solution)/shard_map/all_gather | solution.py:245
  994.4 171.1 %all-gather.27.cloned.1.call-start = ((), (), s32[]{:S(2)}) async-start(), calls=%async_computation.25 | async-start | bytes 7864320 | tf_op jit(solution)/shard_map/all_gather | solution.py:186
  1092.6 164.7 %reduce-scatter.27.cloned.1.call-start = ((), (), s32[]{:S(2)}) async-start(), calls=%async_computation.26 | async-start | bytes 7864320 | tf_op jit(solution)/shard_map/reduce_scatter | solution.py:204
  1187.0 103.1 %all-gather.33.cloned.1.call-start = ((), (), s32[]{:S(2)}) async-start(), calls=%async_computation.33 | async-start | bytes 1966080 | tf_op jit(solution)/shard_map/all_gather | solution.py:245
  1187.7 135.4 %reduce-scatter.43.cloned.1.call-start = ((), (), s32[]{:S(2)}) async-start(), calls=%async_computation.37 | async-start | bytes 589824
  1202.7 190.7 %all-gather.29.cloned.1.call-start = ((), (), s32[]{:S(2)}) async-start(), calls=%async_computation.27 | async-start | bytes 7864320 | tf_op jit(solution)/shard_map/all_gather | solution.py:186
  1266.7 208.4 %reduce-scatter.39.cloned.1.call-start = ((), (), s32[]{:S(2)}) async-start(), calls=%async_computation.35 | async-start | bytes 147456
  1273.7 202.2 %reduce-scatter.41.cloned.1.call-start = ((), (), s32[]{:S(2)}) async-start(), calls=%async_computation.36 | async-start | bytes 589824
  1283.7 205.1 %reduce-scatter.35.cloned.1.call-start = ((), (), s32[]{:S(2)}) async-start(), calls=%async_computation.31 | async-start | bytes 589824 | tf_op jit(solution)/shard_map/reduce_scatter | solution.py:153
  1305.1 215.2 %reduce-scatter.33.cloned.1.call-start = ((), (), s32[]{:S(2)}) async-start(), calls=%async_computation.30 | async-start | bytes 589824 | tf_op jit(solution)/shard_map/reduce_scatter | solution.py:153
  1456.8 157.7 %all-to-all-start.3 = ((bf16[6144,3,128]{2,1,0:T(4,128)(2,1)}), bf16[6144,3,128]{2,1,0:T(4,128)(2,1)}, u32[]{:S(2)}, u32[]{:S(2)}) async-start(bf16[6144,3,128]{2,1,0:T(4,128)(2,1)} %copy.417), calls=%async_computation.7 | async-start | bytes 12582912 | tf_op jit(solution)/shard_map/all_to_all | solution.py:326
  1462.2 88.5 %reduce-scatter.37.cloned.1.call-start = ((), (), s32[]{:S(2)}) async-start(), calls=%async_computation.34 | async-start | bytes 147456
  1467.0 114.8 %reduce-scatter.31.cloned.1.call-start = ((), (), s32[]{:S(2)}) async-start(), calls=%async_computation.29 | async-start | bytes 442368 | tf_op jit(solution)/shard_map/reduce_scatter | solution.py:147
  1475.0 138.0 %reduce-scatter.29.cloned.1.call-start = ((), (), s32[]{:S(2)}) async-start(), calls=%async_computation.28 | async-start | bytes 442368 | tf_op jit(solution)/shard_map/reduce_scatter | solution.py:147
  (135 other events, 2149.7 us)
Sparse Core Ops, SparseCore 0:
  15.0 72.8 all-gather.14
  179.0 70.0 all-gather.16
  290.7 70.2 reduce-scatter.20
  366.4 70.1 all-gather.18
  530.9 70.0 all-gather.20
  602.7 70.1 all-gather.22
  695.2 70.2 reduce-scatter.24
  768.4 70.1 reduce-scatter.22
  846.9 70.1 all-gather.24
  996.2 67.2 all-gather.30
  1092.7 72.7 all-gather.26
  1187.1 70.2 reduce-scatter.26
  1259.1 30.8 all-gather.32
  1292.1 30.9 reduce-scatter.42
  1325.0 68.4 all-gather.28
  1396.2 30.1 reduce-scatter.38
  1428.5 29.0 reduce-scatter.40
  1459.8 29.0 reduce-scatter.34
  1491.1 29.0 reduce-scatter.32
  1522.4 28.2 reduce-scatter.36
  1553.0 28.7 reduce-scatter.30
  1584.1 28.7 reduce-scatter.28
where the time goes:
time: 1690 us; the launch traced here: 1670 us
  waiting for transfers between devices  895 us (53%)
  matrix products  278 us (16%)
  blocking collectives  197 us (12%)
  local copies, waits for them, and re-layouts  189 us (11%)
  other arithmetic  78.1 us (5%)
  starting transfers between devices  20.4 us (1%)
    all_gather x4, waiting for transfers between devices, spread_grads(): piece = lax.all_gather(rows, 'tensor', axis=0, tiled=True)  242 us
    all_gather x4, waiting for transfers between devices, spread_only(): return project(lax.all_gather(rows, 'tensor', axis=0, tiled=True))  185 us
    reduce_scatter x2, waiting for transfers between devices, rows_sum(): lax.psum_scatter(slice_term(source, weight, form).astype(jnp.bfloat16), '...  138 us
    reduce_scatter x2, waiting for transfers between devices, grads_sum(): lax.psum_scatter(slice_term(source, weight, form).astype(jnp.bfloat16), '...  116 us
    all_gather x2, waiting for transfers between devices, forward_layer(): lax.all_gather(w_qkv, 'tensor', axis=2, tiled=True)  74.8 us
    dot_general x2, matrix products, project_up(): return jnp.dot(piece, w_up, preferred_element_type=jnp.float32)  66.4 us
    reduce_scatter x2, waiting for transfers between devices, return_grads(): lax.psum_scatter(first.astype(jnp.bfloat16), 'dp', scatter_dimension=2, t...  60.6 us
    unnamed x296, local copies, waits for them, and re-layouts  59.1 us
  transfers between devices with their start and end apart: 26, of which 21 were waited for; matrix products, arithmetic and copies ran while one was open for 13% of the time, Pallas kernels for 0%

commit v1 on v0

v1 whole, which is shorter than its diff:
```python
import functools
import math

import jax
import jax.numpy as jnp
from jax import lax
from jax.experimental import pallas as pl
from jax.experimental.pallas import tpu as pltpu
from jax.sharding import PartitionSpec as P

HD = 64
SPAN = 128
LEN = 2048
LAYERS = 2
SEQ_BLOCKS = LEN // SPAN
LANES = 128
EPS = 1e-05
MASKED = -1e30
LOG_SPAN = math.log(SPAN)
SCALE = HD**-0.5

bf16 = jnp.bfloat16
f32 = jnp.float32
VMEM_LIMIT = 62 << 20


def dot_nn(a, b):
    return lax.dot_general(a, b, (((1,), (0,)), ((), ())), preferred_element_type=f32)


def dot_nt(a, b):
    return lax.dot_general(a, b, (((1,), (1,)), ((), ())), preferred_element_type=f32)


def dot_tn(a, b):
    return lax.dot_general(a, b, (((0,), (0,)), ((), ())), preferred_element_type=f32)


def normalized(rows):
    centre = rows - jnp.mean(rows, -1, keepdims=True)
    rate = lax.rsqrt(jnp.mean(centre * centre, -1, keepdims=True) + EPS)
    return centre * rate, rate


def normalized_back(grad, gain, unit, rate):
    scaled = grad * gain
    mean_first = jnp.mean(scaled, -1, keepdims=True)
    mean_second = jnp.mean(scaled * unit, -1, keepdims=True)
    return rate * (scaled - mean_first - unit * mean_second)


def row_sums(rows):
    return jnp.sum(rows.reshape(-1, 8, rows.shape[1]), 0)


def lane_blocks(ref, blocks, at):
    return jnp.concatenate([ref[j, at] for j in range(blocks)], 1)


def gelu_pair(hidden):
    cdf = 0.5 + 0.5 * lax.erf(hidden * (0.5**0.5))
    density = jnp.exp(hidden * hidden * -0.5) * (1.0 / math.sqrt(2.0 * math.pi))
    return hidden * cdf, cdf + hidden * density


def pair_masks():
    lane = lax.broadcasted_iota(jnp.int32, (1, LANES), 1)
    low = (lane < HD).astype(f32).astype(bf16)
    high = (lane >= HD).astype(f32).astype(bf16)
    return low, high


def pair_split(rows, masks):
    return jnp.concatenate([rows * masks[0], rows * masks[1]], 0)


def pair_join(columns):
    return jnp.concatenate([columns[:HD, :SPAN], columns[HD:, SPAN:]], 0)


def masked_scores(keys, split_queries, before):
    scores = dot_nt(keys, split_queries)
    key_at = lax.broadcasted_iota(jnp.int32, (SPAN, 2 * SPAN), 0)
    query_at = lax.broadcasted_iota(jnp.int32, (SPAN, 2 * SPAN), 1) % SPAN
    block_at = lax.broadcasted_iota(jnp.int32, (SEQ_BLOCKS, 2 * SPAN), 0)
    direct = jnp.where(key_at <= query_at, scores[:SPAN], MASKED)
    summary = jnp.where(block_at < before, scores[SPAN:] + LOG_SPAN, MASKED)
    return direct, summary


def pair_forward(queries, keys, values, before, masks):
    direct, summary = masked_scores(keys, pair_split(queries, masks), before)
    top = jnp.maximum(jnp.max(direct, 0, keepdims=True), jnp.max(summary, 0, keepdims=True))
    direct = jnp.exp(direct - top)
    summary = jnp.exp(summary - top)
    total = jnp.sum(direct, 0, keepdims=True) + jnp.sum(summary, 0, keepdims=True)
    weights = jnp.concatenate([direct, summary], 0).astype(bf16)
    mixed = dot_tn(values, weights) * (1.0 / total)
    return pair_join(mixed).astype(bf16).T, top + jnp.log(total)


def pair_backward(queries, keys, values, grads, mixed, log_total, before, masks):
    split_queries = pair_split(queries, masks)
    split_grads = pair_split(grads, masks)
    product = (grads.astype(f32) * mixed.astype(f32)).astype(bf16)
    split_product = pair_split(product, masks)
    direct, summary = masked_scores(keys, split_queries, before)
    prob = jnp.concatenate([jnp.exp(direct - log_total), jnp.exp(summary - log_total)], 0)
    minus = jnp.full(values.shape, -1.0, bf16)
    centred = dot_nt(
        jnp.concatenate([values, minus], 1), jnp.concatenate([split_grads, split_product], 1)
    )
    score_grads = (prob * centred).astype(bf16)
    grad_keys = dot_nn(score_grads, split_queries)
    grad_values = dot_nn(prob.astype(bf16), split_grads)
    grad_queries = pair_join(dot_tn(keys, score_grads)) * SCALE
    return grad_queries.astype(bf16).T, grad_keys, grad_values


def block_place(base, at):
    place = base + at
    return place // SEQ_BLOCKS * SEQ_BLOCKS, place % SEQ_BLOCKS


def with_summary(rows, summaries, start, lanes):
    return jnp.concatenate([rows, summaries[pl.ds(start, SEQ_BLOCKS), lanes]], 0)


def attend_tile(base, q_ref, k_ref, v_ref, sum_ref, att_ref, log_ref):
    width = q_ref.shape[1]
    masks = pair_masks()
    for at in range(q_ref.shape[0] // SPAN):
        start, before = block_place(base, at)
        start = pl.multiple_of(start, SEQ_BLOCKS)
        rows = pl.ds(at * SPAN, SPAN)
        for pair in range(width // LANES):
            lanes = pl.ds(pair * LANES, LANES)
            value_lanes = pl.ds(width + pair * LANES, LANES)
            keys = with_summary(k_ref[rows, lanes], sum_ref, start, lanes)
            values = with_summary(v_ref[rows, lanes], sum_ref, start, value_lanes)
            mixed, log_total = pair_forward(q_ref[rows, lanes], keys, values, before, masks)
            att_ref[rows, lanes] = mixed
            log_ref[at, pl.ds(pair, 1), :] = log_total


def attend_back_tile(
    base, q_ref, k_ref, v_ref, sum_ref, datt_ref, att_ref, log_ref, dq_ref, dk_ref, dv_ref, dsum_ref
):
    width = q_ref.shape[1]
    masks = pair_masks()
    for at in range(q_ref.shape[0] // SPAN):
        start, before = block_place(base, at)
        start = pl.multiple_of(start, SEQ_BLOCKS)
        rows = pl.ds(at * SPAN, SPAN)
        for pair in range(width // LANES):
            lanes = pl.ds(pair * LANES, LANES)
            value_lanes = pl.ds(width + pair * LANES, LANES)
            keys = with_summary(k_ref[rows, lanes], sum_ref, start, lanes)
            values = with_summary(v_ref[rows, lanes], sum_ref, start, value_lanes)
            dq, dk, dv = pair_backward(
                q_ref[rows, lanes],
                keys,
                values,
                datt_ref[rows, lanes],
                att_ref[rows, lanes],
                log_ref[at, pl.ds(pair, 1), :],
                before,
                masks,
            )
            dq_ref[rows, lanes] = dq
            dk_ref[rows, lanes] = dk[:SPAN]
            dv_ref[rows, lanes] = dv[:SPAN]
            dsum_ref[pl.ds(start, SEQ_BLOCKS), lanes] += dk[SPAN:]
            dsum_ref[pl.ds(start, SEQ_BLOCKS), value_lanes] += dv[SPAN:]


def project_tile(rows, w_ref, gain, shift, bias, q_ref, k_ref, v_ref, sum_ref):
    blocks = w_ref.shape[0]
    unit, _ = normalized(rows)
    attn_in = (unit * gain + shift).astype(bf16)
    queries = dot_nn(attn_in, lane_blocks(w_ref, blocks, 0)) + bias[0:1]
    q_ref[...] = queries.astype(bf16) * jnp.asarray(SCALE, bf16)
    keys = dot_nn(attn_in, lane_blocks(w_ref, blocks, 1)).astype(bf16)
    values = (dot_nn(attn_in, lane_blocks(w_ref, blocks, 2)) + bias[1:2]).astype(bf16)
    k_ref[...] = keys
    v_ref[...] = values
    width = keys.shape[1]
    for at in range(keys.shape[0] // SPAN):
        part = slice(at * SPAN, (at + 1) * SPAN)
        sum_ref[0, pl.ds(at, 1), pl.ds(0, width)] = jnp.mean(
            keys[part].astype(f32), 0, keepdims=True
        )
        sum_ref[0, pl.ds(at, 1), pl.ds(width, width)] = jnp.mean(
            values[part].astype(f32), 0, keepdims=True
        )


def middle_of(rows, att, w_ref, branch_bias):
    out_turned = lane_blocks(w_ref, w_ref.shape[0], 0)
    return rows + dot_nt(att, out_turned) + branch_bias[0:1]


def wide(ref, j, first, count):
    return jnp.concatenate([ref[j, first + at] for at in range(count)], 1)


def mlp_tile(middle, w_ref, gain, shift, bias_up, branch_bias, act_ref, slope_ref):
    blocks = w_ref.shape[0]
    count = (w_ref.shape[1] - 1) // 2
    unit, _ = normalized(middle)
    mlp_in = (unit * gain + shift).astype(bf16)
    total = middle + branch_bias[1:2]
    span = count * LANES
    for j in range(blocks):
        hidden = dot_nn(mlp_in, wide(w_ref, j, 1, count)) + bias_up[:, j * span : (j + 1) * span]
        act, slope = gelu_pair(hidden)
        act = act.astype(bf16)
        act_ref[:, j * span : (j + 1) * span] = act
        slope_ref[:, j * span : (j + 1) * span] = slope.astype(bf16)
        total = total + dot_nt(act, wide(w_ref, j, 1 + count, count))
    return total


def accumulate(acc_ref, j, first, value):
    for at in range(value.shape[1] // LANES):
        acc_ref[j, first + at] += value[:, at * LANES : (at + 1) * LANES]


def mlp_back_tile(dy, middle, att, w_ref, gain, shift, act_ref, slope_ref, acc_ref, small_ref, datt_ref):
    blocks = w_ref.shape[0]
    count = (w_ref.shape[1] - 1) // 2
    span = count * LANES
    unit, rate = normalized(middle)
    mlp_in = (unit * gain + shift).astype(bf16)
    turned_in = mlp_in.T
    dyb = dy.astype(bf16)
    turned_dy = dyb.T
    grad_in = None
    for j in range(blocks):
        part = slice(j * span, (j + 1) * span)
        grad_act = dot_nn(dyb, wide(w_ref, j, 1 + count, count))
        grad_hidden = (grad_act * slope_ref[:, part].astype(f32)).astype(bf16)
        small_ref[4 + j] += row_sums(grad_hidden.astype(f32))
        accumulate(acc_ref, j, 1 + count, dot_nn(turned_dy, act_ref[:, part]))
        accumulate(acc_ref, j, 1, dot_nn(turned_in, grad_hidden))
        term = dot_nt(grad_hidden, wide(w_ref, j, 1, count))
        grad_in = term if grad_in is None else grad_in + term
    small_ref[0] += row_sums(grad_in * unit)
    small_ref[1] += row_sums(grad_in)
    grad_middle = dy + normalized_back(grad_in, gain, unit, rate)
    small_ref[2] += row_sums(grad_middle)
    small_ref[3] += row_sums(dy)
    dmb = grad_middle.astype(bf16)
    grad_out = dot_tn(dmb, att)
    for j in range(blocks):
        acc_ref[j, 0] += grad_out[:, j * LANES : (j + 1) * LANES]
    datt_ref[...] = dot_nn(dmb, lane_blocks(w_ref, blocks, 0)).astype(bf16)
    return grad_middle


def project_back_tile(
    rows, grad_middle, dq_ref, dk_ref, dv_ref, dsum_ref, w_ref, gain, shift, acc_ref, small_ref
):
    blocks = w_ref.shape[0]
    width = rows.shape[1]
    unit, rate = normalized(rows)
    turned = (unit * gain + shift).astype(bf16).T
    count = rows.shape[0] // SPAN

    def spread(ref, first):
        parts = []
        for at in range(count):
            share = dsum_ref[0, pl.ds(at, 1), pl.ds(first, width)] * (1.0 / SPAN)
            parts.append(ref[pl.ds(at * SPAN, SPAN), :] + share)
        return jnp.concatenate(parts, 0).astype(bf16)

    grads = (dq_ref[...], spread(dk_ref, 0), spread(dv_ref, width))
    grad_in = None
    for at, grad in enumerate(grads):
        piece = dot_nn(turned, grad)
        for j in range(blocks):
            acc_ref[j, at] += piece[:, j * LANES : (j + 1) * LANES]
        term = dot_nt(grad, lane_blocks(w_ref, blocks, at))
        grad_in = term if grad_in is None else grad_in + term
    small_ref[0] += row_sums(grad_in * unit)
    small_ref[1] += row_sums(grad_in)
    small_ref[2] += row_sums(grads[0].astype(f32))
    small_ref[3] += row_sums(grads[2].astype(f32))
    return grad_middle + normalized_back(grad_in, gain, unit, rate)


def first_block(tile):
    per_device = pl.num_programs(0) * (tile // SPAN)
    return lax.axis_index("tensor") * per_device + pl.program_id(0) * (tile // SPAN)


def start_kernel(x_ref, w_ref, gain_ref, shift_ref, bias_ref, q_ref, k_ref, v_ref, sum_ref):
    project_tile(
        x_ref[...].astype(f32),
        w_ref,
        gain_ref[0:1],
        shift_ref[0:1],
        bias_ref,
        q_ref,
        k_ref,
        v_ref,
        sum_ref,
    )


def forward_kernel(
    x_ref, q_in, k_in, v_in, sums, w_ref, gain_ref, shift_ref, bias_up, branch_bias,
    next_w, next_gain, next_shift, next_bias,
    att_ref, log_ref, middle_ref, act_ref, slope_ref, y_ref, q_ref, k_ref, v_ref, sum_ref,
):
    base = first_block(x_ref.shape[0])
    attend_tile(base, q_in, k_in, v_in, sums, att_ref, log_ref)
    middle = middle_of(x_ref[...].astype(f32), att_ref[...], w_ref, branch_bias)
    middle_ref[...] = middle
    result = mlp_tile(
        middle, w_ref, gain_ref[1:2], shift_ref[1:2], bias_up, branch_bias, act_ref, slope_ref
    )
    y_ref[...] = result
    project_tile(
        result, next_w, next_gain[0:1], next_shift[0:1], next_bias, q_ref, k_ref, v_ref, sum_ref
    )


def zero_first(*refs):
    @pl.when(pl.program_id(0) == 0)
    def _():
        for ref in refs:
            ref[...] = jnp.zeros_like(ref)


def store_last(*pairs):
    @pl.when(pl.program_id(0) == pl.num_programs(0) - 1)
    def _():
        for source, target in pairs:
            for j in range(source.shape[0]):
                for at in range(source.shape[1]):
                    target[j, at] = source[j, at].astype(target.dtype)


def turn_kernel(
    x_ref, q_in, k_in, v_in, sums, w_ref, gain_ref, shift_ref, bias_up, branch_bias, dy_ref,
    out_ref, dmid_ref, dq_ref, dk_ref, dv_ref, dsum_ref, grad_ref, small_ref,
    att_ref, log_ref, act_ref, slope_ref, datt_ref, acc_ref,
):
    base = first_block(x_ref.shape[0])
    zero_first(acc_ref, dsum_ref, small_ref)
    attend_tile(base, q_in, k_in, v_in, sums, att_ref, log_ref)
    middle = middle_of(x_ref[...], att_ref[...], w_ref, branch_bias)
    gain, shift = gain_ref[1:2], shift_ref[1:2]
    result = mlp_tile(middle, w_ref, gain, shift, bias_up, branch_bias, act_ref, slope_ref)
    out_ref[...] = result.astype(bf16)
    dmid_ref[...] = mlp_back_tile(
        dy_ref[...], middle, att_ref[...], w_ref, gain, shift, act_ref, slope_ref, acc_ref,
        small_ref, datt_ref,
    )
    attend_back_tile(
        base, q_in, k_in, v_in, sums, datt_ref, att_ref, log_ref, dq_ref, dk_ref, dv_ref, dsum_ref
    )
    store_last((acc_ref, grad_ref))


def backward_kernel(
    x_ref, dmid_in, dq_in, dk_in, dv_in, dsum_in, w_ref, gain_ref, shift_ref,
    low_w, low_gain, low_shift, middle_ref, att_ref, log_ref, act_ref, slope_ref,
    q_in, k_in, v_in, sums,
    high_grad, high_small, dmid_ref, dq_ref, dk_ref, dv_ref, dsum_ref, grad_ref, small_ref,
    high_acc, acc_ref, datt_ref,
):
    base = first_block(x_ref.shape[0])
    zero_first(high_acc, acc_ref, dsum_ref, small_ref, high_small)
    dy = project_back_tile(
        x_ref[...], dmid_in[...], dq_in, dk_in, dv_in, dsum_in, w_ref, gain_ref[0:1],
        shift_ref[0:1], high_acc, high_small,
    )
    dmid_ref[...] = mlp_back_tile(
        dy, middle_ref[...], att_ref[...], low_w, low_gain[1:2], low_shift[1:2], act_ref,
        slope_ref, acc_ref, small_ref, datt_ref,
    )
    attend_back_tile(
        base, q_in, k_in, v_in, sums, datt_ref, att_ref, log_ref, dq_ref, dk_ref, dv_ref, dsum_ref
    )
    store_last((high_acc, high_grad), (acc_ref, grad_ref))


def finish_kernel(
    x_ref, dmid_in, dq_in, dk_in, dv_in, dsum_in, w_ref, gain_ref, shift_ref,
    dx_ref, grad_ref, small_ref, acc_ref,
):
    zero_first(acc_ref, small_ref)
    dx_ref[...] = project_back_tile(
        x_ref[...].astype(f32), dmid_in[...], dq_in, dk_in, dv_in, dsum_in, w_ref, gain_ref[0:1],
        shift_ref[0:1], acc_ref, small_ref,
    )
    store_last((acc_ref, grad_ref))


def tile_of(rows):
    return next(tile for tile in (256, 128) if rows % tile == 0)


def tiled(array_like, tile):
    return pl.BlockSpec((tile, array_like.shape[1]), lambda i: (i, 0))


def whole(array_like):
    rank = len(array_like.shape)
    return pl.BlockSpec(array_like.shape, lambda i: (0,) * rank, pipeline_mode=pl.Buffered(1))


def stepped(array_like, count):
    rank = len(array_like.shape)
    return pl.BlockSpec((count,) + array_like.shape[1:], lambda i: (i,) + (0,) * (rank - 1))


def spec(kind, array_like, tile):
    if kind == "t":
        return tiled(array_like, tile)
    if kind == "w":
        return whole(array_like)
    if kind == "s":
        return stepped(array_like, 1)
    return stepped(array_like, tile // SPAN)


def call(kernel, name, tile, steps, ins, outs, scratch=()):
    kinds = [kind for kind, _ in ins]
    args = [arg for _, arg in ins]
    shapes = [jax.ShapeDtypeStruct(shape, dtype) for _, shape, dtype in outs]
    return pl.pallas_call(
        kernel,
        name=name,
        grid=(steps,),
        in_specs=[spec(kind, arg, tile) for kind, arg in zip(kinds, args)],
        out_specs=[spec(out[0], shape, tile) for out, shape in zip(outs, shapes)],
        out_shape=shapes,
        scratch_shapes=list(scratch),
        compiler_params=pltpu.CompilerParams(
            dimension_semantics=("arbitrary",), vmem_limit_bytes=VMEM_LIMIT
        ),
    )(*args)


def to_blocks(whole_matrix, lead):
    rows = whole_matrix.shape[-2]
    parts = whole_matrix.reshape(lead, rows, -1, LANES)
    return jnp.transpose(parts, (2, 0, 1, 3))


def gather_weights(w_qkv, w_out, w_up, w_down):
    def both(piece, dp_axis, tensor_axis):
        piece = lax.all_gather(piece, "dp", axis=dp_axis, tiled=True)
        return lax.all_gather(piece, "tensor", axis=tensor_axis, tiled=True)

    qkv = both(w_qkv, 1, 2)
    out_turned = both(w_out, 1, 0).T
    up = both(w_up, 0, 1)
    down_turned = both(w_down, 1, 0).T
    d = up.shape[0]
    blocks = d // LANES
    first = to_blocks(qkv, 3)

    def spread(matrix):
        return to_blocks(matrix, 1)[:, 0].reshape(blocks, -1, d, LANES)

    rest = jnp.concatenate([spread(out_turned), spread(up), spread(down_turned)], 1)
    return first, rest


def scatter_grads(first, rest):
    blocks, _, d, _ = first.shape
    count = (rest.shape[1] - 1) // 2

    def natural(part):
        return jnp.transpose(part, (2, 0, 1, 3)).reshape(d, -1)

    def both(matrix, dp_axis, tensor_axis):
        matrix = lax.psum_scatter(matrix, "dp", scatter_dimension=dp_axis, tiled=True)
        matrix = lax.psum_scatter(matrix, "tensor", scatter_dimension=tensor_axis, tiled=True)
        return matrix.astype(f32)

    qkv = jnp.transpose(first, (1, 2, 0, 3)).reshape(3, d, -1)
    return (
        both(qkv, 1, 2),
        both(natural(rest[:, 0:1]).T, 1, 0),
        both(natural(rest[:, 1 : 1 + count]), 0, 1),
        both(natural(rest[:, 1 + count :]).T, 1, 0),
    )


def share_sums(sums):
    flat = sums.reshape(-1, sums.shape[-1]).astype(bf16)
    return lax.all_gather(flat, "tensor", axis=0, tiled=True)


def return_sums(dsums, like):
    own = lax.psum_scatter(dsums, "tensor", scatter_dimension=0, tiled=True)
    return own.reshape(like)


def body(
    inputs, w_qkv, w_out, w_up, w_down, ln_gain, ln_bias, bias_qv, bias_up, branch_bias, cotangent
):
    rows, d = inputs.shape
    tile = tile_of(rows)
    steps = rows // tile
    per_tile = tile // SPAN
    own_blocks = rows // SPAN
    groups = lax.axis_size("tensor")
    ff = bias_up.shape[1] * groups
    blocks = d // LANES
    count = ff // d
    all_blocks = own_blocks * groups
    bias_qv_all = lax.all_gather(bias_qv, "tensor", axis=2, tiled=True)
    bias_up_all = lax.all_gather(bias_up, "tensor", axis=1, tiled=True)
    firsts, rests = zip(
        *(gather_weights(w_qkv[l], w_out[l], w_up[l], w_down[l]) for l in range(LAYERS))
    )
    sums_shape = (steps, per_tile, 2 * d)
    triple = [("t", (rows, d), bf16)] * 3 + [("s", sums_shape, f32)]
    back = [
        ("t", (rows, d), f32),
        ("t", (rows, d), bf16),
        ("t", (rows, d), f32),
        ("t", (rows, d), f32),
        ("w", (all_blocks, 2 * d), f32),
        ("w", rests[0].shape, bf16),
        ("w", (4 + blocks, 8, d), f32),
    ]
    first_out = [("w", firsts[0].shape, bf16), ("w", (4, 8, d), f32)]
    acc = pltpu.VMEM(rests[0].shape, f32)
    first_acc = pltpu.VMEM(firsts[0].shape, f32)
    tile_bf16 = pltpu.VMEM((tile, d), bf16)

    q0, k0, v0, sums0 = call(
        start_kernel, "start", tile, steps,
        [("t", inputs), ("w", firsts[0]), ("w", ln_gain[0]), ("w", ln_bias[0]), ("w", bias_qv_all[0])],
        triple,
    )
    sums0 = share_sums(sums0)
    att0, log0, middle0, act0, slope0, x1, q1, k1, v1, sums1 = call(
        forward_kernel, "forward", tile, steps,
        [("t", inputs), ("t", q0), ("t", k0), ("t", v0), ("w", sums0), ("w", rests[0]),
         ("w", ln_gain[0]), ("w", ln_bias[0]), ("w", bias_up_all[0:1]), ("w", branch_bias[0]),
         ("w", firsts[1]), ("w", ln_gain[1]), ("w", ln_bias[1]), ("w", bias_qv_all[1])],
        [("t", (rows, d), bf16), ("b", (own_blocks, blocks, 2 * SPAN), f32), ("t", (rows, d), f32),
         ("t", (rows, ff), bf16), ("t", (rows, ff), bf16), ("t", (rows, d), f32)] + triple,
    )
    sums1 = share_sums(sums1)
    outputs, dmid1, dq1, dk1, dv1, dsum1, rest1, small1 = call(
        turn_kernel, "turn", tile, steps,
        [("t", x1), ("t", q1), ("t", k1), ("t", v1), ("w", sums1), ("w", rests[1]),
         ("w", ln_gain[1]), ("w", ln_bias[1]), ("w", bias_up_all[1:2]), ("w", branch_bias[1]),
         ("t", cotangent)],
        [("t", (rows, d), bf16)] + back,
        [tile_bf16, pltpu.VMEM((per_tile, blocks, 2 * SPAN), f32), pltpu.VMEM((tile, ff), bf16),
         pltpu.VMEM((tile, ff), bf16), tile_bf16, acc],
    )
    dsum1 = return_sums(dsum1, sums_shape)
    first1, small1_first, dmid0, dq0, dk0, dv0, dsum0, rest0, small0 = call(
        backward_kernel, "backward", tile, steps,
        [("t", x1), ("t", dmid1), ("t", dq1), ("t", dk1), ("t", dv1), ("s", dsum1), ("w", firsts[1]),
         ("w", ln_gain[1]), ("w", ln_bias[1]), ("w", rests[0]), ("w", ln_gain[0]), ("w", ln_bias[0]),
         ("t", middle0), ("t", att0), ("b", log0), ("t", act0), ("t", slope0),
         ("t", q0), ("t", k0), ("t", v0), ("w", sums0)],
        first_out + back,
        [first_acc, acc, tile_bf16],
    )
    dsum0 = return_sums(dsum0, sums_shape)
    dx, first0, small0_first = call(
        finish_kernel, "finish", tile, steps,
        [("t", inputs), ("t", dmid0), ("t", dq0), ("t", dk0), ("t", dv0), ("s", dsum0),
         ("w", firsts[0]), ("w", ln_gain[0]), ("w", ln_bias[0])],
        [("t", (rows, d), f32)] + first_out,
        [first_acc],
    )
    weight_grads = [scatter_grads(first0, rest0), scatter_grads(first1, rest1)]
    joined = [jnp.stack([grads[at] for grads in weight_grads]) for at in range(4)]
    late = jnp.sum(jnp.stack([small0, small1]), 2)
    early = jnp.sum(jnp.stack([small0_first, small1_first]), 2)
    late, early = lax.psum((late, early), ("dp", "tensor"))
    place = lax.axis_index("tensor")

    def own(array):
        size = array.shape[-1] // groups
        return lax.dynamic_slice_in_dim(array, place * size, size, array.ndim - 1)

    gain_grad = jnp.stack([early[:, 0], late[:, 0]], 1)
    shift_grad = jnp.stack([early[:, 1], late[:, 1]], 1)
    branch_grad = late[:, 2:4]
    pair_grad = own(early[:, 2:4])
    up_grad = own(late[:, 4:].reshape(LAYERS, -1))
    return (outputs, dx, *joined, gain_grad, shift_grad, pair_grad, up_grad, branch_grad)


def solution(mesh):
    return jax.shard_map(
        body,
        mesh=mesh,
        in_specs=(
            P(("dp", "tensor"), None),
            P(None, None, "dp", "tensor"),
            P(None, "tensor", "dp"),
            P(None, "dp", "tensor"),
            P(None, "tensor", "dp"),
            P(),
            P(),
            P(None, None, "tensor"),
            P(None, "tensor"),
            P(),
            P(("dp", "tensor"), None),
        ),
        out_specs=(
            P(("dp", "tensor"), None),
            P(("dp", "tensor"), None),
            P(None, None, "dp", "tensor"),
            P(None, "tensor", "dp"),
            P(None, "dp", "tensor"),
            P(None, "tensor", "dp"),
            P(),
            P(),
            P(None, None, "tensor"),
            P(None, "tensor"),
            P(),
        ),
        check_vma=False,
    )
```

time: 1690 us -> 930 us (0.55)
  waiting for transfers between devices: 895 us -> 301 us
  matrix products: 278 us -> 0 us
  Pallas kernels: 0 us -> 159 us
  blocking collectives: 197 us -> 269 us
  other arithmetic: 78.1 us -> 10.8 us
  local copies, waits for them, and re-layouts: 189 us -> 159 us
    all_gather x10 -> x6, waiting for transfers between devices: 502 us -> 0.03 us  [both(): return lax.all_gather(piece, 'tensor', axis=tensor_axis, tiled=True)]
    dot_general x48 -> x0, matrix products: 278 us -> none  [the longest x2 66.4 us: project_up(): return jnp.dot(piece, w_up, preferred_element_type=jnp.float32)]
    reduce_scatter x8 -> x6, waiting for transfers between devices: 349 us -> 149 us  [both(): lax.psum_scatter(matrix, 'tensor', scatter_dimension=tensor_axis, tiled=T...]
    pallas_call x0 -> x5, Pallas kernels: none -> 159 us  [call(): pl.pallas_call(kernel, name=name, grid=(steps,), in_specs=[spec(kind, arg...]
    unnamed x26 -> x32, waiting for transfers between devices: 33.3 us -> 152 us
    convert_element_type x22 -> x0, local copies, waits for them, and re-layouts: 60.1 us -> none  [the longest x8 28.3 us: forward_layer(): attended = mixed.astype(jnp.bfloat16)]
    unnamed x0 -> x2, blocking collectives: none -> 47.8 us
    unnamed x296 -> x78, local copies, waits for them, and re-layouts: 59.1 us -> 106 us
  transfers between devices with their start and end apart: 26 -> 23, of which waited for: 21 -> 12; matrix products, arithmetic and copies ran while one was open for 13% -> 22% of each run, Pallas kernels for 0% -> 11%
where the time goes in v1:
time: 930 us; the launch traced here: 922 us
  waiting for transfers between devices  301 us (32%)
  blocking collectives  269 us (29%)
  local copies, waits for them, and re-layouts  159 us (17%)
  Pallas kernels  159 us (17%)
  between operations  16.7 us (2%)
  other arithmetic  10.8 us (1%)
    pallas_call x5, Pallas kernels, call(): pl.pallas_call(kernel, name=name, grid=(steps,), in_specs=[spec(kind, arg...  159 us
    unnamed x32, waiting for transfers between devices  152 us
    reduce_scatter x6, waiting for transfers between devices, both(): lax.psum_scatter(matrix, 'tensor', scatter_dimension=tensor_axis, tiled=T...  149 us
    all_gather x8, blocking collectives, both(): piece = lax.all_gather(piece, 'dp', axis=dp_axis, tiled=True)  122 us
    unnamed x78, local copies, waits for them, and re-layouts  106 us
    unnamed x2, blocking collectives  47.8 us
    psum x1, blocking collectives, body(): late, early = lax.psum((late, early), ('dp', 'tensor'))  38.9 us
    all_gather x2, blocking collectives, both(): return lax.all_gather(piece, 'tensor', axis=tensor_axis, tiled=True)  27.1 us
  transfers between devices with their start and end apart: 23, of which 12 were waited for; matrix products, arithmetic and copies ran while one was open for 22% of the time, Pallas kernels for 11%

profile of v1, /device:TPU:0, one launch (start us, length us, event | category | flops | bytes accessed | tf_op | source)
XLA Modules:
  0.0 922.3 jit_solution(13585028892515002558)
XLA Ops:
  8.1 16.2 %all-gather.8 = bf16[1,3,512,128]{3,2,1,0:T(8,128)(2,1)S(1)} all-gather(bf16[1,3,64,128]{3,2,1,0:T(8,128)(2,1)S(1)} %get-tuple-element.124), channel_id=10, replica_groups=mesh['dp'=8,'tensor'=4] {'dp'}, dimensions={2}, use_global_device_ids=true | all-gather | bytes 442368 | tf_op jit(solution)/shard_map/all_gather | solution.py:456
  25.3 14.4 %all-gather = bf16[1,3,512,128]{3,2,1,0:T(8,128)(2,1)S(1)} all-gather(bf16[1,3,64,128]{3,2,1,0:T(8,128)(2,1)S(1)} %get-tuple-element.125), channel_id=2, replica_groups=mesh['dp'=8,'tensor'=4] {'dp'}, dimensions={2}, use_global_device_ids=true | all-gather | bytes 442368 | tf_op jit(solution)/shard_map/all_gather | solution.py:456
  40.8 15.9 %all-gather.14 = bf16[1,512,512]{1,2,0:T(8,128)(2,1)} all-gather(bf16[1,512,64]{1,2,0:T(8,128)(2,1)S(1)} %get-tuple-element.122), channel_id=16, replica_groups=mesh['dp'=8,'tensor'=4] {'dp'}, dimensions={2}, use_global_device_ids=true | all-gather | bytes 589824 | tf_op jit(solution)/shard_map/all_gather | solution.py:456
  56.8 16.0 %all-gather.6 = bf16[1,512,512]{1,2,0:T(8,128)(2,1)} all-gather(bf16[1,512,64]{1,2,0:T(8,128)(2,1)S(1)} %get-tuple-element.123), channel_id=8, replica_groups=mesh['dp'=8,'tensor'=4] {'dp'}, dimensions={2}, use_global_device_ids=true | all-gather | bytes 589824 | tf_op jit(solution)/shard_map/all_gather | solution.py:456
  72.8 16.0 %all-gather.4 = bf16[1,512,512]{2,1,0:T(8,128)(2,1)} all-gather(bf16[1,64,512]{2,1,0:T(8,128)(2,1)S(1)} %get-tuple-element.121), channel_id=6, replica_groups=mesh['dp'=8,'tensor'=4] {'dp'}, dimensions={1}, use_global_device_ids=true | all-gather | bytes 589824 | tf_op jit(solution)/shard_map/all_gather | solution.py:456
  88.9 16.0 %all-gather.12 = bf16[1,512,512]{2,1,0:T(8,128)(2,1)} all-gather(bf16[1,64,512]{2,1,0:T(8,128)(2,1)S(1)} %get-tuple-element.120), channel_id=14, replica_groups=mesh['dp'=8,'tensor'=4] {'dp'}, dimensions={1}, use_global_device_ids=true | all-gather | bytes 589824 | tf_op jit(solution)/shard_map/all_gather | solution.py:456
  133.2 14.2 %all-gather.3 = bf16[1,512,512]{2,1,0:T(8,128)(2,1)S(1)} all-gather(bf16[1,128,512]{2,1,0:T(8,128)(2,1)S(1)} %copy.78), channel_id=5, replica_groups=mesh['dp'=8,'tensor'=4] {'tensor'}, dimensions={1}, use_global_device_ids=true | all-gather | bytes 655360 | tf_op jit(solution)/shard_map/all_gather | solution.py:457
  212.9 31.2 %forward.1 = (bf16[1536,512]{1,0:T(8,128)(2,1)}, f32[12,4,256]{2,1,0:T(4,128)}, f32[1536,512]{1,0:T(8,128)}, bf16[1536,2048]{1,0:T(8,128)(2,1)}, bf16[1536,2048]...) custom-call(bf16[1536,512]{1,0:T(8,128)(2,1)} %x_ref.5, ...), custom_call_target="tpu_custom_call" | custom-call | tf_op jit(solution)/shard_map/forward/pallas_call | solution.py:434
  259.5 57.6 %turn.1 = (bf16[1536,512]{1,0:T(8,128)(2,1)}, f32[1536,512]{1,0:T(8,128)}, bf16[1536,512]{1,0:T(8,128)(2,1)}, f32[1536,512]{1,0:T(8,128)}, f32[1536,512]{1,0:T(8...) custom-call(f32[1536,512]{1,0:T(8,128)} %get-tuple-element.49.x_ref, ...), custom_call_target="tpu_custom_call" | custom-call | tf_op jit(solution)/shard_map/turn/pallas_call | solution.py:434
  319.5 23.3 %fusion = f32[16,1024]{1,0:T(8,128)S(1)} fusion(f32[48,1024]{1,0:T(8,128)S(1)} %copy-done.3), kind=kCustom, calls=%all-reduce-scatter | all-reduce-scatter fusion | flops 65537 | bytes 262656
  348.0 49.0 %backward.1 = (bf16[4,3,512,128]{3,2,1,0:T(8,128)(2,1)}, f32[4,8,512]{2,1,0:T(8,128)}, f32[1536,512]{1,0:T(8,128)}, bf16[1536,512]{1,0:T(8,128)(2,1)}, f32[1536,...) custom-call(f32[1536,512]{1,0:T(8,128)} %get-tuple-element.49.x_ref,, ...), custom_call_target="tpu_custom_call" | custom-call | tf_op jit(solution)/shard_map/backward/pallas_call | solution.py:434
  399.7 24.5 %fusion.1 = f32[16,1024]{1,0:T(8,128)S(1)} fusion(f32[48,1024]{1,0:T(8,128)S(1)} %copy-done.2), kind=kCustom, calls=%all-reduce-scatter.1 | all-reduce-scatter fusion | flops 65537 | bytes 262656
  485.3 61.2 %all-reduce.10.cloned.1.call-done = (bf16[3,512,512]{2,0,1:T(4,128)(2,1)}, bf16[3,512,512]{2,0,1:T(4,128)(2,1)}) async-done(((bf16[3,512,512]{2,0,1:T(4,128)(2,1)}, bf16[3,512,512]{2,0,1:T(4,128)(2,1)}), (bf16[3,512,512]{2,0,1:T(4,128)(2,1)}, bf16[3,512,512]{2,0,1:T(4,128)(2,1)})) %all-reduce.10.cloned.1.call-update) | async-done | bytes 3145744
  606.5 14.9 %reduce-scatter.59.cloned.1.call-done = bf16[64,2048]{1,0:T(8,128)(2,1)} async-done(((bf16[512,2048]{1,0:T(8,128)(2,1)}), bf16[64,2048]{1,0:T(8,128)(2,1)}) %reduce-scatter.59.cloned.1.call-update) | async-done | bytes 262160
  623.5 38.9 %all-reduce.6 = (f32[2,8,512]{2,1,0:T(8,128)S(1)}, f32[2,4,512]{2,1,0:T(4,128)S(1)}) all-reduce(f32[2,8,512]{2,1,0:T(8,128)S(1)} %maximum_reduce_fusion, f32[2,4,512]{2,1,0:T(4,128)S(1)} %maximum_reduce_fusion.1), channel_id=1, replica_groups=mesh['dp'=8,'tensor'=4] {'dp','tensor'}, use_global_device_ids=true, to_apply=%region_21.0 | all-reduce | flops 12288 | bytes 98304 | tf_op jit(solution)/shard_map/psum | solution.py:585
  666.0 29.2 %reduce-scatter.55.cloned.1.call-done = bf16[64,2048]{1,0:T(8,128)(2,1)} async-done(((bf16[512,2048]{1,0:T(8,128)(2,1)}), bf16[64,2048]{1,0:T(8,128)(2,1)}) %reduce-scatter.55.cloned.1.call-update) | async-done | bytes 262160
  699.0 21.9 %reduce-scatter.37.cloned.1.call-done = bf16[128,64]{1,0:T(8,128)(2,1)} async-done(((bf16[512,64]{1,0:T(8,128)(2,1)}), bf16[128,64]{1,0:T(8,128)(2,1)}) %reduce-scatter.37.cloned.1.call-update) | async-done | bytes 16400 | tf_op jit(solution)/shard_map/reduce_scatter | solution.py:483
  720.9 26.7 %reduce-scatter.35.cloned.1.call-done = bf16[128,64]{1,0:T(8,128)(2,1)} async-done(((bf16[512,64]{1,0:T(8,128)(2,1)}), bf16[128,64]{1,0:T(8,128)(2,1)}) %reduce-scatter.35.cloned.1.call-update) | async-done | bytes 16400 | tf_op jit(solution)/shard_map/reduce_scatter | solution.py:483
  749.1 25.8 %reduce-scatter.47.cloned.1.call-done = bf16[128,192]{1,0:T(8,128)(2,1)} async-done(((bf16[512,192]{1,0:T(8,128)(2,1)}), bf16[128,192]{1,0:T(8,128)(2,1)}) %reduce-scatter.47.cloned.1.call-update) | async-done | bytes 49168
  782.4 20.0 %reduce-scatter.49.cloned.1.call-done = bf16[128,192]{1,0:T(8,128)(2,1)} async-done(((bf16[512,192]{1,0:T(8,128)(2,1)}), bf16[128,192]{1,0:T(8,128)(2,1)}) %reduce-scatter.49.cloned.1.call-update) | async-done | bytes 49168
  810.6 19.2 %reduce-scatter.45.cloned.1.call-done = bf16[512,64]{1,0:T(8,128)(2,1)} async-done(((bf16[2048,64]{1,0:T(8,128)(2,1)}), bf16[512,64]{1,0:T(8,128)(2,1)}) %reduce-scatter.45.cloned.1.call-update) | async-done | bytes 65552 | tf_op jit(solution)/shard_map/reduce_scatter | solution.py:483
  829.9 27.9 %reduce-scatter.43.cloned.1.call-done = bf16[512,64]{1,0:T(8,128)(2,1)} async-done(((bf16[2048,64]{1,0:T(8,128)(2,1)}), bf16[512,64]{1,0:T(8,128)(2,1)}) %reduce-scatter.43.cloned.1.call-update) | async-done | bytes 65552 | tf_op jit(solution)/shard_map/reduce_scatter | solution.py:483
  859.7 25.6 %reduce-scatter.41.cloned.1.call-done = bf16[64,512]{0,1:T(8,128)(2,1)} async-done(((bf16[64,2048]{0,1:T(8,128)(2,1)}), bf16[64,512]{0,1:T(8,128)(2,1)}) %reduce-scatter.41.cloned.1.call-update) | async-done | bytes 65552 | tf_op jit(solution)/shard_map/reduce_scatter | solution.py:483
  885.2 27.9 %reduce-scatter.39.cloned.1.call-done = bf16[64,512]{0,1:T(8,128)(2,1)} async-done(((bf16[64,2048]{0,1:T(8,128)(2,1)}), bf16[64,512]{0,1:T(8,128)(2,1)}) %reduce-scatter.39.cloned.1.call-update) | async-done | bytes 65552 | tf_op jit(solution)/shard_map/reduce_scatter | solution.py:483
  (197 shorter events, 272.2 us)
Async XLA Ops:
  7.2 171.4 %all-gather.31.cloned.1.call-start = ((), (), s32[]{:S(2)}) async-start(), calls=%async_computation.23 | async-start | bytes 1966080 | tf_op jit(solution)/shard_map/all_gather | solution.py:457
  25.2 155.9 %all-gather.25.cloned.1.call-start = ((), (), s32[]{:S(2)}) async-start(), calls=%async_computation.20 | async-start | bytes 1966080 | tf_op jit(solution)/shard_map/all_gather | solution.py:457
  40.7 160.7 %all-gather.35.cloned.1.call-start = ((), (), s32[]{:S(2)}) async-start(), calls=%async_computation.25 | async-start | bytes 2621440 | tf_op jit(solution)/shard_map/all_gather | solution.py:457
  56.7 148.8 %all-gather.29.cloned.1.call-start = ((), (), s32[]{:S(2)}) async-start(), calls=%async_computation.22 | async-start | bytes 2621440 | tf_op jit(solution)/shard_map/all_gather | solution.py:457
  72.8 135.5 %all-gather.27.cloned.1.call-start = ((), (), s32[]{:S(2)}) async-start(), calls=%async_computation.21 | async-start | bytes 2621440 | tf_op jit(solution)/shard_map/all_gather | solution.py:457
  88.8 165.9 %all-gather.33.cloned.1.call-start = ((), (), s32[]{:S(2)}) async-start(), calls=%async_computation.24 | async-start | bytes 2621440 | tf_op jit(solution)/shard_map/all_gather | solution.py:457
  104.9 375.8 %reduce-scatter.53.cloned.1.call-start = ((), (), s32[]{:S(2)}) async-start(), calls=%async_computation.29 | async-start | bytes 589824
  105.0 62.7 %copy-start.14 = (f32[2,512]{1,0:T(2,128)S(1)}, f32[2,512]{1,0:T(2,128)}, u32[]{:S(2)}) copy-start(f32[2,512]{1,0:T(2,128)} %param.19) | copy-start | bytes 12292
  319.5 162.9 %reduce-scatter.51.cloned.1.call-start = ((), (), s32[]{:S(2)}) async-start(), calls=%async_computation.28 | async-start | bytes 589824
  342.8 4.4 collective-permute-start
  399.6 146.9 %all-reduce.10.cloned.1.call-start = ((), (), s32[]{:S(2)}) async-start(), calls=%async_computation.34 | async-start | bytes 8388608
  424.2 6.2 collective-permute-start.1
  449.5 154.9 %reduce-scatter.61.cloned.1.call-start = ((), (), s32[]{:S(2)}) async-start(), calls=%async_computation.33 | async-start | bytes 2359296
  459.8 161.6 %reduce-scatter.59.cloned.1.call-start = ((), (), s32[]{:S(2)}) async-start(), calls=%async_computation.32 | async-start | bytes 2359296
  469.9 193.1 %reduce-scatter.57.cloned.1.call-start = ((), (), s32[]{:S(2)}) async-start(), calls=%async_computation.31 | async-start | bytes 2359296
  475.3 219.9 %reduce-scatter.55.cloned.1.call-start = ((), (), s32[]{:S(2)}) async-start(), calls=%async_computation.30 | async-start | bytes 2359296
  480.6 240.3 %reduce-scatter.37.cloned.1.call-start = ((), (), s32[]{:S(2)}) async-start(), calls=%async_computation.15 | async-start | bytes 163840 | tf_op jit(solution)/shard_map/reduce_scatter | solution.py:483
  482.3 265.2 %reduce-scatter.35.cloned.1.call-start = ((), (), s32[]{:S(2)}) async-start(), calls=%async_computation.14 | async-start | bytes 163840 | tf_op jit(solution)/shard_map/reduce_scatter | solution.py:483
  484.0 290.9 %reduce-scatter.47.cloned.1.call-start = ((), (), s32[]{:S(2)}) async-start(), calls=%async_computation.26 | async-start | bytes 327680
  575.3 227.1 %reduce-scatter.49.cloned.1.call-start = ((), (), s32[]{:S(2)}) async-start(), calls=%async_computation.27 | async-start | bytes 327680
  604.3 225.6 %reduce-scatter.45.cloned.1.call-start = ((), (), s32[]{:S(2)}) async-start(), calls=%async_computation.19 | async-start | bytes 655360 | tf_op jit(solution)/shard_map/reduce_scatter | solution.py:483
  606.4 251.3 %reduce-scatter.43.cloned.1.call-start = ((), (), s32[]{:S(2)}) async-start(), calls=%async_computation.18 | async-start | bytes 655360 | tf_op jit(solution)/shard_map/reduce_scatter | solution.py:483
  623.3 261.9 %reduce-scatter.41.cloned.1.call-start = ((), (), s32[]{:S(2)}) async-start(), calls=%async_computation.17 | async-start | bytes 655360 | tf_op jit(solution)/shard_map/reduce_scatter | solution.py:483
  665.0 248.0 %reduce-scatter.39.cloned.1.call-start = ((), (), s32[]{:S(2)}) async-start(), calls=%async_computation.16 | async-start | bytes 655360 | tf_op jit(solution)/shard_map/reduce_scatter | solution.py:483
  (17 other events, 505.3 us)
Sparse Core Ops, SparseCore 0:
  25.4 32.0 all-gather.30
  59.9 30.9 all-gather.24
  92.7 35.1 all-gather.34
  129.6 39.5 all-gather.28
  170.9 35.6 all-gather.26
  208.3 35.1 all-gather.32
  319.6 31.4 reduce-scatter.52
  399.7 32.7 reduce-scatter.50
  449.6 96.8 all-reduce.9
  548.7 35.8 reduce-scatter.60
  586.8 34.5 reduce-scatter.58
  623.5 34.6 reduce-scatter.56
  660.5 34.6 reduce-scatter.54
  698.4 22.4 reduce-scatter.36
  723.7 23.8 reduce-scatter.34
  750.7 24.0 reduce-scatter.46
  778.3 24.0 reduce-scatter.48
  805.0 24.7 reduce-scatter.44
  832.9 24.7 reduce-scatter.42
  860.4 24.7 reduce-scatter.40
  888.3 24.7 reduce-scatter.38

commit v2 on v1

--- a/solution.py
+++ b/solution.py
@@ -123,7 +123,7 @@
 
 
 def with_summary(rows, summaries, start, lanes):
-    return jnp.concatenate([rows, summaries[pl.ds(start, SEQ_BLOCKS), lanes]], 0)
+    return jnp.concatenate([rows, summaries[pl.ds(start, SEQ_BLOCKS), lanes].astype(bf16)], 0)
 
 
 def attend_tile(base, q_ref, k_ref, v_ref, sum_ref, att_ref, log_ref):
@@ -178,10 +178,10 @@
     blocks = w_ref.shape[0]
     unit, _ = normalized(rows)
     attn_in = (unit * gain + shift).astype(bf16)
-    queries = dot_nn(attn_in, lane_blocks(w_ref, blocks, 0)) + bias[0:1]
+    queries = dot_nn(attn_in, lane_blocks(w_ref, blocks, 0)) + bias[0]
     q_ref[...] = queries.astype(bf16) * jnp.asarray(SCALE, bf16)
     keys = dot_nn(attn_in, lane_blocks(w_ref, blocks, 1)).astype(bf16)
-    values = (dot_nn(attn_in, lane_blocks(w_ref, blocks, 2)) + bias[1:2]).astype(bf16)
+    values = (dot_nn(attn_in, lane_blocks(w_ref, blocks, 2)) + bias[1]).astype(bf16)
     k_ref[...] = keys
     v_ref[...] = values
     width = keys.shape[1]
@@ -197,22 +197,22 @@
 
 def middle_of(rows, att, w_ref, branch_bias):
     out_turned = lane_blocks(w_ref, w_ref.shape[0], 0)
-    return rows + dot_nt(att, out_turned) + branch_bias[0:1]
+    return rows + dot_nt(att, out_turned) + branch_bias
 
 
 def wide(ref, j, first, count):
     return jnp.concatenate([ref[j, first + at] for at in range(count)], 1)
 
 
-def mlp_tile(middle, w_ref, gain, shift, bias_up, branch_bias, act_ref, slope_ref):
+def mlp_tile(middle, w_ref, gain, shift, l, bias_up, branch_bias, act_ref, slope_ref):
     blocks = w_ref.shape[0]
     count = (w_ref.shape[1] - 1) // 2
     unit, _ = normalized(middle)
     mlp_in = (unit * gain + shift).astype(bf16)
-    total = middle + branch_bias[1:2]
+    total = middle + branch_bias
     span = count * LANES
     for j in range(blocks):
-        hidden = dot_nn(mlp_in, wide(w_ref, j, 1, count)) + bias_up[:, j * span : (j + 1) * span]
+        hidden = dot_nn(mlp_in, wide(w_ref, j, 1, count)) + bias_up[j, pl.ds(l, 1)]
         act, slope = gelu_pair(hidden)
         act = act.astype(bf16)
         act_ref[:, j * span : (j + 1) * span] = act
@@ -294,38 +294,6 @@
     return lax.axis_index("tensor") * per_device + pl.program_id(0) * (tile // SPAN)
 
 
-def start_kernel(x_ref, w_ref, gain_ref, shift_ref, bias_ref, q_ref, k_ref, v_ref, sum_ref):
-    project_tile(
-        x_ref[...].astype(f32),
-        w_ref,
-        gain_ref[0:1],
-        shift_ref[0:1],
-        bias_ref,
-        q_ref,
-        k_ref,
-        v_ref,
-        sum_ref,
-    )
-
-
-def forward_kernel(
-    x_ref, q_in, k_in, v_in, sums, w_ref, gain_ref, shift_ref, bias_up, branch_bias,
-    next_w, next_gain, next_shift, next_bias,
-    att_ref, log_ref, middle_ref, act_ref, slope_ref, y_ref, q_ref, k_ref, v_ref, sum_ref,
-):
-    base = first_block(x_ref.shape[0])
-    attend_tile(base, q_in, k_in, v_in, sums, att_ref, log_ref)
-    middle = middle_of(x_ref[...].astype(f32), att_ref[...], w_ref, branch_bias)
-    middle_ref[...] = middle
-    result = mlp_tile(
-        middle, w_ref, gain_ref[1:2], shift_ref[1:2], bias_up, branch_bias, act_ref, slope_ref
-    )
-    y_ref[...] = result
-    project_tile(
-        result, next_w, next_gain[0:1], next_shift[0:1], next_bias, q_ref, k_ref, v_ref, sum_ref
-    )
-
-
 def zero_first(*refs):
     @pl.when(pl.program_id(0) == 0)
     def _():
@@ -333,70 +301,140 @@
             ref[...] = jnp.zeros_like(ref)
 
 
-def store_last(*pairs):
-    @pl.when(pl.program_id(0) == pl.num_programs(0) - 1)
+def lay_out(all_ref, flat_ref):
+    @pl.when(pl.program_id(0) == 0)
     def _():
-        for source, target in pairs:
-            for j in range(source.shape[0]):
-                for at in range(source.shape[1]):
-                    target[j, at] = source[j, at].astype(target.dtype)
+        groups, steps, per_tile, _ = all_ref.shape
+        for group in range(groups):
+            for step in range(steps):
+                at = (group * steps + step) * per_tile
+                flat_ref[pl.ds(at, per_tile)] = all_ref[group, step]
+
+
+def on_last(act):
+    pl.when(pl.program_id(0) == pl.num_programs(0) - 1)(act)
+
+
+def store_grads(*pairs):
+    for source, target in pairs:
+        for j in range(source.shape[0]):
+            for at in range(source.shape[1]):
+                target[j, at] = source[j, at].astype(target.dtype)
+
+
+def store_sums(flat_ref, slab_ref):
+    size = slab_ref.shape[1]
+    for group in range(slab_ref.shape[0]):
+        slab_ref[group] = flat_ref[pl.ds(group * size, size)]
+
+
+def vector(ref, l, at):
+    return ref[l, pl.ds(at, 1)]
+
+
+def pair_bias(ref, l):
+    blocks = ref.shape[0]
+    return [jnp.concatenate([ref[j, l, pl.ds(s, 1)] for j in range(blocks)], 1) for s in range(2)]
+
+
+def start_kernel(l, x_ref, w_ref, gain_ref, shift_ref, bias_ref, q_ref, k_ref, v_ref, sum_ref):
+    project_tile(
+        x_ref[...].astype(f32), w_ref, vector(gain_ref, l, 0), vector(shift_ref, l, 0),
+        pair_bias(bias_ref, l), q_ref, k_ref, v_ref, sum_ref,
+    )
+
+
+def forward_kernel(
+    l, x_ref, q_in, k_in, v_in, sums_all, w_ref, gain_ref, shift_ref, bias_up, branch_bias,
+    next_w, bias_ref,
+    att_ref, log_ref, middle_ref, act_ref, slope_ref, y_ref, q_ref, k_ref, v_ref, sum_ref,
+    sums,
+):
+    lay_out(sums_all, sums)
+    base = first_block(x_ref.shape[0])
+    attend_tile(base, q_in, k_in, v_in, sums, att_ref, log_ref)
+    middle = middle_of(x_ref[...].astype(f32), att_ref[...], w_ref, vector(branch_bias, l, 0))
+    middle_ref[...] = middle
+    result = mlp_tile(
+        middle, w_ref, vector(gain_ref, l, 1), vector(shift_ref, l, 1), l, bias_up,
+        vector(branch_bias, l, 1), act_ref, slope_ref,
+    )
+    y_ref[...] = result
+    project_tile(
+        result, next_w, vector(gain_ref, l + 1, 0), vector(shift_ref, l + 1, 0),
+        pair_bias(bias_ref, l + 1), q_ref, k_ref, v_ref, sum_ref,
+    )
 
 
 def turn_kernel(
-    x_ref, q_in, k_in, v_in, sums, w_ref, gain_ref, shift_ref, bias_up, branch_bias, dy_ref,
+    l, x_ref, q_in, k_in, v_in, sums_all, w_ref, gain_ref, shift_ref, bias_up, branch_bias, dy_ref,
     out_ref, dmid_ref, dq_ref, dk_ref, dv_ref, dsum_ref, grad_ref, small_ref,
-    att_ref, log_ref, act_ref, slope_ref, datt_ref, acc_ref,
+    att_ref, log_ref, act_ref, slope_ref, datt_ref, acc_ref, sums, dsums,
 ):
+    lay_out(sums_all, sums)
     base = first_block(x_ref.shape[0])
-    zero_first(acc_ref, dsum_ref, small_ref)
+    zero_first(acc_ref, dsums, small_ref)
     attend_tile(base, q_in, k_in, v_in, sums, att_ref, log_ref)
-    middle = middle_of(x_ref[...], att_ref[...], w_ref, branch_bias)
-    gain, shift = gain_ref[1:2], shift_ref[1:2]
-    result = mlp_tile(middle, w_ref, gain, shift, bias_up, branch_bias, act_ref, slope_ref)
+    middle = middle_of(x_ref[...], att_ref[...], w_ref, vector(branch_bias, l, 0))
+    gain, shift = vector(gain_ref, l, 1), vector(shift_ref, l, 1)
+    result = mlp_tile(
+        middle, w_ref, gain, shift, l, bias_up, vector(branch_bias, l, 1), act_ref, slope_ref
+    )
     out_ref[...] = result.astype(bf16)
     dmid_ref[...] = mlp_back_tile(
         dy_ref[...], middle, att_ref[...], w_ref, gain, shift, act_ref, slope_ref, acc_ref,
         small_ref, datt_ref,
     )
     attend_back_tile(
-        base, q_in, k_in, v_in, sums, datt_ref, att_ref, log_ref, dq_ref, dk_ref, dv_ref, dsum_ref
-    )
-    store_last((acc_ref, grad_ref))
+        base, q_in, k_in, v_in, sums, datt_ref, att_ref, log_ref, dq_ref, dk_ref, dv_ref, dsums
+    )
+
+    @on_last
+    def _():
+        store_grads((acc_ref, grad_ref))
+        store_sums(dsums, dsum_ref)
 
 
 def backward_kernel(
-    x_ref, dmid_in, dq_in, dk_in, dv_in, dsum_in, w_ref, gain_ref, shift_ref,
-    low_w, low_gain, low_shift, middle_ref, att_ref, log_ref, act_ref, slope_ref,
-    q_in, k_in, v_in, sums,
+    l, x_ref, dmid_in, dq_in, dk_in, dv_in, dsum_in, w_ref, low_w, gain_ref, shift_ref,
+    middle_ref, att_ref, log_ref, act_ref, slope_ref, q_in, k_in, v_in, sums_all,
     high_grad, high_small, dmid_ref, dq_ref, dk_ref, dv_ref, dsum_ref, grad_ref, small_ref,
-    high_acc, acc_ref, datt_ref,
+    high_acc, acc_ref, datt_ref, sums, dsums,
 ):
+    lay_out(sums_all, sums)
     base = first_block(x_ref.shape[0])
-    zero_first(high_acc, acc_ref, dsum_ref, small_ref, high_small)
+    zero_first(high_acc, acc_ref, dsums, small_ref, high_small)
     dy = project_back_tile(
-        x_ref[...], dmid_in[...], dq_in, dk_in, dv_in, dsum_in, w_ref, gain_ref[0:1],
-        shift_ref[0:1], high_acc, high_small,
+        x_ref[...], dmid_in[...], dq_in, dk_in, dv_in, dsum_in, w_ref, vector(gain_ref, l + 1, 0),
+        vector(shift_ref, l + 1, 0), high_acc, high_small,
     )
     dmid_ref[...] = mlp_back_tile(
-        dy, middle_ref[...], att_ref[...], low_w, low_gain[1:2], low_shift[1:2], act_ref,
-        slope_ref, acc_ref, small_ref, datt_ref,
+        dy, middle_ref[...], att_ref[...], low_w, vector(gain_ref, l, 1), vector(shift_ref, l, 1),
+        act_ref, slope_ref, acc_ref, small_ref, datt_ref,
     )
     attend_back_tile(
-        base, q_in, k_in, v_in, sums, datt_ref, att_ref, log_ref, dq_ref, dk_ref, dv_ref, dsum_ref
-    )
-    store_last((high_acc, high_grad), (acc_ref, grad_ref))
+        base, q_in, k_in, v_in, sums, datt_ref, att_ref, log_ref, dq_ref, dk_ref, dv_ref, dsums
+    )
+
+    @on_last
+    def _():
+        store_grads((high_acc, high_grad), (acc_ref, grad_ref))
+        store_sums(dsums, dsum_ref)
 
 
 def finish_kernel(
-    x_ref, dmid_in, dq_in, dk_in, dv_in, dsum_in, w_ref, gain_ref, shift_ref,
+    l, x_ref, dmid_in, dq_in, dk_in, dv_in, dsum_in, w_ref, gain_ref, shift_ref,
     dx_ref, grad_ref, small_ref, acc_ref,
 ):
     zero_first(acc_ref, small_ref)
     dx_ref[...] = project_back_tile(
-        x_ref[...].astype(f32), dmid_in[...], dq_in, dk_in, dv_in, dsum_in, w_ref, gain_ref[0:1],
-        shift_ref[0:1], acc_ref, small_ref,
-    )
-    store_last((acc_ref, grad_ref))
+        x_ref[...].astype(f32), dmid_in[...], dq_in, dk_in, dv_in, dsum_in, w_ref,
+        vector(gain_ref, l, 0), vector(shift_ref, l, 0), acc_ref, small_ref,
+    )
+
+    @on_last
+    def _():
+        store_grads((acc_ref, grad_ref))
 
 
 def tile_of(rows):
@@ -492,14 +530,598 @@
     )
 
 
-def share_sums(sums):
-    flat = sums.reshape(-1, sums.shape[-1]).astype(bf16)
-    return lax.all_gather(flat, "tensor", axis=0, tiled=True)
-
-
-def return_sums(dsums, like):
-    own = lax.psum_scatter(dsums, "tensor", scatter_dimension=0, tiled=True)
-    return own.reshape(like)
+def place():
+    spot = lax.axis_index("dp")
+    return spot // 2, spot % 2, lax.axis_index("tensor")
+
+
+def flip_low(j):
+    return j + 1 - 2 * (j % 2)
+
+
+def flip_high(j):
+    return j + 2 - 4 * (j // 2)
+
+
+def device(line, core, j):
+    return (2 * line + core, j)
+
+
+class Copies:
+    def __init__(self, send_sem, recv_sem):
+        self.send_sem, self.recv_sem = send_sem, recv_sem
+        self.index, self.sent = {}, []
+
+    def slot(self, key):
+        return self.index.setdefault(key, len(self.index))
+
+    def describe(self, key, source, target, where):
+        at = self.slot(key)
+        return pltpu.make_async_remote_copy(
+            src_ref=source,
+            dst_ref=target,
+            send_sem=self.send_sem.at[at],
+            recv_sem=self.recv_sem.at[at],
+            device_id=where,
+            device_id_type=pl.DeviceIdType.MESH,
+        )
+
+    def send(self, key, source, target, where):
+        copy = self.describe(key, source, target, where)
+        copy.start()
+        self.sent.append(copy)
+
+    def receive(self, key, target, where):
+        self.describe(key, target, target, where).wait_recv()
+
+    def finish(self):
+        for copy in self.sent:
+            copy.wait_send()
+        self.sent = []
+
+
+def greet(peers):
+    barrier = pltpu.get_barrier_semaphore()
+    for peer in peers:
+        pl.semaphore_signal(barrier, inc=1, device_id=peer, device_id_type=pl.DeviceIdType.MESH)
+    pl.semaphore_wait(barrier, len(peers))
+
+
+def near_peers(lines):
+    line, core, j = place()
+    peers = [device(lax.rem(line + d, lines), core, j) for d in range(1, lines)]
+    peers += [device(line, core, flip_low(j)), device(line, core, flip_high(j))]
+    peers.append(device(line, 1 - core, j))
+    return peers
+
+
+def piece(ref, j, line, core, half=None):
+    share = ref.shape[2] // lax.axis_size("dp")
+    first = (2 * line + core) * share
+    if half is None:
+        return ref.at[j, :, pl.ds(pl.multiple_of(first, share), share), :]
+    small = share // 2
+    return ref.at[j, :, pl.ds(pl.multiple_of(first + half * small, small), small), :]
+
+
+class Gather:
+    def __init__(self, name, ref, copies, lines):
+        self.name, self.ref, self.copies, self.lines = name, ref, copies, lines
+        self.line, self.core, self.j = place()
+        self.low, self.high = flip_low(self.j), flip_high(self.j)
+        self.far = flip_high(self.low)
+
+    def key(self, *parts):
+        return (self.name,) + parts
+
+    def move(self, key, view, where):
+        self.copies.send(self.key(*key), view, view, where)
+
+    def source_line(self, d):
+        return lax.rem(self.line + self.lines - d, self.lines)
+
+    def out(self, d, view):
+        self.move(("low", d), view, device(self.line, self.core, self.low))
+        self.move(("high", d), view, device(self.line, self.core, self.high))
+        self.partner(("own", d), view)
+
+    def partner(self, key, view):
+        self.move(("partner",) + key, view, device(self.line, 1 - self.core, self.j))
+
+    def view(self, column, d, half=None, core=None):
+        core = self.core if core is None else core
+        return piece(self.ref, column, self.source_line(d), core, half)
+
+    def receive(self, key, view):
+        self.copies.receive(self.key(*key), view, device(self.line, 1 - self.core, self.j))
+
+    def begin(self):
+        own = self.view(self.j, 0)
+        for d in range(1, self.lines):
+            self.move(("line", d), own, device(lax.rem(self.line + d, self.lines), self.core, self.j))
+        self.out(0, own)
+
+    def relay_line(self):
+        for d in range(1, self.lines):
+            view = self.view(self.j, d)
+            self.receive(("line", d), view)
+            self.out(d, view)
+
+    def relay_bits(self):
+        for d in range(self.lines):
+            for name, column, half, other, where in (
+                ("low", self.low, 0, "far_high", self.high),
+                ("high", self.high, 1, "far_low", self.low),
+            ):
+                view = self.view(column, d)
+                self.receive((name, d), view)
+                self.move((other, d), self.view(column, d, half), device(self.line, self.core, where))
+                self.partner((name, d), view)
+
+    def relay_far(self):
+        for d in range(self.lines):
+            for name, half in (("far_high", 0), ("far_low", 1)):
+                view = self.view(self.far, d, half)
+                self.receive((name, d), view)
+                self.partner((name, d), view)
+
+    def collect(self):
+        for d in range(self.lines):
+            for name, column in (("own", self.j), ("low", self.low), ("high", self.high)):
+                self.receive(("partner", name, d), self.view(column, d, None, 1 - self.core))
+            for name, half in (("far_high", 0), ("far_low", 1)):
+                view = self.view(self.far, d, half, 1 - self.core)
+                self.receive(("partner", name, d), view)
+
+
+GATHER_COPIES = 200
+
+
+def gather_kernel(
+    lines, qkv_ref, out_w_ref, up_ref, down_ref, pair_ref, up_bias_ref,
+    first0, first1, rest0, rest1, pair_all, up_all,
+    own_first, own_rest, send_sem, recv_sem, local_sem,
+):
+    line, core, j = place()
+    far = flip_high(flip_low(j))
+    greet(near_peers(lines) + [device(line, core, far)])
+    copies = Copies(send_sem, recv_sem)
+    stores = []
+
+    def store(source, target):
+        copy = pltpu.make_async_copy(source, target, local_sem.at[len(stores)])
+        copy.start()
+        stores.append(copy)
+
+    firsts, rests = (first0, first1), (rest0, rest1)
+    count = up_ref.shape[2] // LANES
+    for l in range(LAYERS):
+        own_first[l] = qkv_ref[l]
+        own_rest[l, 0] = out_w_ref[l].T
+        turned = down_ref[l].T
+        for at in range(count):
+            own_rest[l, 1 + at] = up_ref[l, :, at * LANES : (at + 1) * LANES]
+            own_rest[l, 1 + count + at] = turned[:, at * LANES : (at + 1) * LANES]
+    for l in range(LAYERS):
+        store(own_first.at[l], piece(firsts[l], j, line, core))
+        store(own_rest.at[l], piece(rests[l], j, line, core))
+    store(pair_ref, pair_all.at[j])
+    store(up_bias_ref, up_all.at[j])
+    sections = []
+    for l in range(LAYERS):
+        sections.append(Gather(("first", l), firsts[l], copies, lines))
+        sections.append(Gather(("rest", l), rests[l], copies, lines))
+    stores[0].wait()
+    sections[0].begin()
+    others = (flip_low(j), flip_high(j), far)
+    for at, other in enumerate(others):
+        where = device(line, core, other)
+        copies.send(("pair", at), pair_ref, pair_all.at[j], where)
+        copies.send(("up", at), up_bias_ref, up_all.at[j], where)
+    for at in range(1, len(sections)):
+        stores[at].wait()
+        sections[at].begin()
+        previous = sections[at - 1]
+        previous.relay_line()
+        previous.relay_bits()
+        previous.relay_far()
+    last = sections[-1]
+    last.relay_line()
+    last.relay_bits()
+    last.relay_far()
+    for section in sections:
+        section.collect()
+    for at, other in enumerate(others):
+        where = device(line, core, other)
+        copies.receive(("pair", at), pair_all.at[other], where)
+        copies.receive(("up", at), up_all.at[other], where)
+    for copy in stores[len(sections) :]:
+        copy.wait()
+    copies.finish()
+
+
+def gather_all(w_qkv, w_out, w_up, w_down, bias_qv, bias_up):
+    lines, groups = lax.axis_size("dp") // 2, lax.axis_size("tensor")
+    d = w_up.shape[1] * 2 * lines
+    count = w_up.shape[2] // LANES
+    first = jax.ShapeDtypeStruct((groups, 3, d, LANES), bf16)
+    rest = jax.ShapeDtypeStruct((groups, 1 + 2 * count, d, LANES), bf16)
+    share = d // (2 * lines)
+    pair_all = jax.ShapeDtypeStruct((groups,) + bias_qv.shape, f32)
+    up_all = jax.ShapeDtypeStruct((groups,) + bias_up.shape, f32)
+    vmem = pl.BlockSpec(memory_space=pltpu.VMEM)
+    outs = pl.pallas_call(
+        functools.partial(gather_kernel, lines),
+        name="gather",
+        in_specs=[vmem] * 6,
+        out_specs=[pl.BlockSpec(memory_space=pl.ANY)] * 6,
+        out_shape=[first, first, rest, rest, pair_all, up_all],
+        scratch_shapes=[
+            pltpu.VMEM((LAYERS, 3, share, LANES), bf16),
+            pltpu.VMEM((LAYERS, 1 + 2 * count, share, LANES), bf16),
+            pltpu.SemaphoreType.DMA((GATHER_COPIES,)),
+            pltpu.SemaphoreType.DMA((GATHER_COPIES,)),
+            pltpu.SemaphoreType.DMA((2 * LAYERS + 2,)),
+        ],
+        compiler_params=pltpu.CompilerParams(
+            collective_id=0, has_side_effects=True, vmem_limit_bytes=VMEM_LIMIT
+        ),
+    )(w_qkv, w_out, w_up, w_down, bias_qv, bias_up)
+    return outs[0:2], outs[2:4], outs[4], outs[5]
+
+
+def group_peers(groups):
+    spot, j = lax.axis_index("dp"), lax.axis_index("tensor")
+    return [(spot, lax.rem(j + d, groups)) for d in range(1, groups)]
+
+
+def share_kernel(groups, sums_ref, all_ref, send_sem, recv_sem, local_sem):
+    spot, j = lax.axis_index("dp"), lax.axis_index("tensor")
+    peers = group_peers(groups)
+    own = pltpu.make_async_copy(sums_ref, all_ref.at[j], local_sem)
+    own.start()
+    greet(peers)
+    copies = Copies(send_sem, recv_sem)
+    for d, peer in enumerate(peers):
+        copies.send(d, sums_ref, all_ref.at[j], peer)
+    for d in range(1, groups):
+        other = lax.rem(j + groups - d, groups)
+        copies.receive(d - 1, all_ref.at[other], (spot, other))
+    copies.finish()
+    own.wait()
+
+
+def share_sums(sums, number):
+    groups = lax.axis_size("tensor")
+    return pl.pallas_call(
+        functools.partial(share_kernel, groups),
+        name="share",
+        in_specs=[pl.BlockSpec(memory_space=pltpu.VMEM)],
+        out_specs=pl.BlockSpec(memory_space=pltpu.VMEM),
+        out_shape=jax.ShapeDtypeStruct((groups,) + sums.shape, sums.dtype),
+        scratch_shapes=[
+            pltpu.SemaphoreType.DMA((groups,)),
+            pltpu.SemaphoreType.DMA((groups,)),
+            pltpu.SemaphoreType.DMA,
+        ],
+        compiler_params=pltpu.CompilerParams(collective_id=number, has_side_effects=True),
+    )(sums)
+
+
+def return_kernel(groups, dsum_ref, out_ref, landed, send_sem, recv_sem):
+    spot, j = lax.axis_index("dp"), lax.axis_index("tensor")
+    peers = group_peers(groups)
+    greet(peers)
+    copies = Copies(send_sem, recv_sem)
+    for d, peer in enumerate(peers):
+        copies.send(d, dsum_ref.at[peer[1]], landed.at[d], peer)
+    for d in range(1, groups):
+        copies.receive(d - 1, landed.at[d - 1], (spot, lax.rem(j + groups - d, groups)))
+    total = dsum_ref[j]
+    for d in range(groups - 1):
+        total = total + landed[d]
+    per_tile = out_ref.shape[1]
+    for at in range(out_ref.shape[0]):
+        out_ref[at] = total[at * per_tile : (at + 1) * per_tile]
+    copies.finish()
+
+
+def return_sums(dsums, like, number):
+    groups = lax.axis_size("tensor")
+    return pl.pallas_call(
+        functools.partial(return_kernel, groups),
+        name="return",
+        in_specs=[pl.BlockSpec(memory_space=pltpu.VMEM)],
+        out_specs=pl.BlockSpec(memory_space=pltpu.VMEM),
+        out_shape=jax.ShapeDtypeStruct(like, f32),
+        scratch_shapes=[
+            pltpu.VMEM((groups - 1,) + dsums.shape[1:], f32),
+            pltpu.SemaphoreType.DMA((groups,)),
+            pltpu.SemaphoreType.DMA((groups,)),
+        ],
+        compiler_params=pltpu.CompilerParams(collective_id=number, has_side_effects=True),
+    )(dsums)
+
+
+class Reduce:
+    def __init__(self, name, source, blocks, copies, buffers, lines):
+        self.name, self.source, self.blocks, self.copies, self.lines = name, source, blocks, copies, lines
+        (self.own, self.landed, self.low_one, self.high_one, self.low_two, self.high_two,
+         self.line_sum, self.line_in, self.own_sem) = buffers
+        self.line, self.core, self.j = place()
+        self.low, self.high = flip_low(self.j), flip_high(self.j)
+        self.far = flip_high(self.low)
+        self.share = source.shape[2] // (2 * lines)
+
+    def key(self, *parts):
+        return (self.name,) + parts
+
+    def rows_of(self, line, core):
+        first, size = self.blocks
+        at = pl.ds(pl.multiple_of((2 * line + core) * self.share, self.share), self.share)
+        return self.source.at[:, pl.ds(first, size), at, :]
+
+    def partner(self):
+        return device(self.line, 1 - self.core, self.j)
+
+    def begin(self):
+        for line in range(self.lines):
+            self.copies.send(
+                self.key("partner", line), self.rows_of(line, 1 - self.core), self.landed.at[line],
+                self.partner(),
+            )
+            self.fetch(line).start()
+
+    def fetch(self, line):
+        return pltpu.make_async_copy(self.rows_of(line, self.core), self.own.at[line], self.own_sem.at[line])
+
+    def parts(self):
+        half = self.share // 2
+        return slice(0, half), slice(half, self.share)
+
+    def first_sum(self):
+        for line in range(self.lines):
+            self.copies.receive(self.key("partner", line), self.landed.at[line], self.partner())
+            self.fetch(line).wait()
+
+            def add(j, carry):
+                for at in range(self.blocks[1]):
+                    total = self.own[line, j, at].astype(f32) + self.landed[line, j, at].astype(f32)
+                    self.own[line, j, at] = total.astype(bf16)
+                return carry
+
+            lax.fori_loop(0, self.own.shape[1], add, 0)
+        half = self.share // 2
+        upper, lower = pl.ds(0, half), pl.ds(half, half)
+        for to, (column, rows) in enumerate(((self.low, upper), (self.far, upper))):
+            self.copies.send(
+                self.key("low", to), self.own.at[:, column, :, rows, :], self.low_one.at[to],
+                device(self.line, self.core, self.low),
+            )
+        for to, (column, rows) in enumerate(((self.high, lower), (self.far, lower))):
+            self.copies.send(
+                self.key("high", to), self.own.at[:, column, :, rows, :], self.high_one.at[to],
+                device(self.line, self.core, self.high),
+            )
+
+    def second_sum(self):
+        half = self.share // 2
+        upper, lower = pl.ds(0, half), pl.ds(half, half)
+        for to in range(2):
+            self.copies.receive(self.key("low", to), self.low_one.at[to], self.partner())
+            self.copies.receive(self.key("high", to), self.high_one.at[to], self.partner())
+
+        def add(line, carry):
+            for at in range(self.blocks[1]):
+                for to, column in ((0, self.j), (1, self.high)):
+                    total = self.own[line, column, at, upper].astype(f32)
+                    total = total + self.low_one[to, line, at].astype(f32)
+                    self.low_one[to, line, at] = total.astype(bf16)
+                for to, column in ((0, self.j), (1, self.low)):
+                    total = self.own[line, column, at, lower].astype(f32)
+                    total = total + self.high_one[to, line, at].astype(f32)
+                    self.high_one[to, line, at] = total.astype(bf16)
+            return carry
+
+        lax.fori_loop(0, self.lines, add, 0)
+        self.copies.send(
+            self.key("high_two"), self.low_one.at[1], self.high_two,
+            device(self.line, self.core, self.high),
+        )
+        self.copies.send(
+            self.key("low_two"), self.high_one.at[1], self.low_two,
+            device(self.line, self.core, self.low),
+        )
+
+    def third_sum(self):
+        half = self.share // 2
+        self.copies.receive(self.key("high_two"), self.high_two, self.partner())
+        self.copies.receive(self.key("low_two"), self.low_two, self.partner())
+
+        def add(line, carry):
+            for at in range(self.blocks[1]):
+                upper = self.low_one[0, line, at].astype(f32) + self.high_two[line, at].astype(f32)
+                lower = self.high_one[0, line, at].astype(f32) + self.low_two[line, at].astype(f32)
+                self.line_sum[line, at, pl.ds(0, half)] = upper.astype(bf16)
+                self.line_sum[line, at, pl.ds(half, half)] = lower.astype(bf16)
+            return carry
+
+        lax.fori_loop(0, self.lines, add, 0)
+        for d in range(1, self.lines):
+            to = lax.rem(self.line + d, self.lines)
+            self.copies.send(
+                self.key("line", d), self.line_sum.at[to], self.line_in.at[d - 1],
+                device(to, self.core, self.j),
+            )
+
+    def result(self, at):
+        total = self.line_sum[self.line, at].astype(f32)
+        for d in range(1, self.lines):
+            total = total + self.line_in[d - 1, at].astype(f32)
+        return total
+
+    def end(self):
+        for d in range(1, self.lines):
+            self.copies.receive(self.key("line", d), self.line_in.at[d - 1], self.partner())
+
+    @staticmethod
+    def buffers(lines, groups, size, share):
+        half = share // 2
+        return [
+            pltpu.VMEM((lines, groups, size, share, LANES), bf16),
+            pltpu.VMEM((lines, groups, size, share, LANES), bf16),
+            pltpu.VMEM((2, lines, size, half, LANES), bf16),
+            pltpu.VMEM((2, lines, size, half, LANES), bf16),
+            pltpu.VMEM((lines, size, half, LANES), bf16),
+            pltpu.VMEM((lines, size, half, LANES), bf16),
+            pltpu.VMEM((lines, size, share, LANES), bf16),
+            pltpu.VMEM((lines - 1, size, share, LANES), bf16),
+            pltpu.SemaphoreType.DMA((lines,)),
+        ]
+
+
+REDUCE_COPIES = 160
+SECTION = 3
+BUFFERS = 9
+
+
+def small_sums(small_refs, copies, lines, own, near, far, stage):
+    line, core, j = place()
+    peers = (
+        device(line, 1 - core, j),
+        device(line, core, flip_low(j)),
+        device(line, core, flip_high(j)),
+    )
+    if stage == 0:
+        at = 0
+        for ref in small_refs:
+            for row in range(ref.shape[0]):
+                own[0, pl.ds(at, 1)] = jnp.sum(ref[row], 0, keepdims=True)
+                at += 1
+        copies.send(("small", 0), own.at[0], near.at[0], peers[0])
+    elif stage < 3:
+        copies.receive(("small", stage - 1), near.at[stage - 1], peers[0])
+        own[stage] = own[stage - 1] + near[stage - 1]
+        copies.send(("small", stage), own.at[stage], near.at[stage], peers[stage])
+    elif stage == 3:
+        copies.receive(("small", 2), near.at[2], peers[0])
+        own[3] = own[2] + near[2]
+        for d in range(1, lines):
+            to = lax.rem(line + d, lines)
+            copies.send(("small", 2 + d), own.at[3], far.at[line], device(to, core, j))
+    else:
+        for d in range(1, lines):
+            source = lax.rem(line + lines - d, lines)
+            copies.receive(("small", 2 + d), far.at[source], peers[0])
+        far[line] = own[3]
+        total = far[0]
+        for at in range(1, lines):
+            total = total + far[at]
+        return total
+
+
+def store_vectors(total, outs):
+    gain_out, shift_out, pair_out, up_out, branch_out = outs
+    j = lax.axis_index("tensor")
+    late = total.shape[0] // LAYERS - 4
+    own = pl.ds(pl.multiple_of(j * LANES, LANES), LANES)
+    for l in range(LAYERS):
+        at = l * (total.shape[0] // LAYERS)
+        for row in range(2):
+            gain_out[l, pl.ds(row, 1)] = total[pl.ds(at + (1 - row) * late, 1)]
+            shift_out[l, pl.ds(row, 1)] = total[pl.ds(at + (1 - row) * late + 1, 1)]
+            branch_out[l, pl.ds(row, 1)] = total[pl.ds(at + 2 + row, 1)]
+            pair_out[l, pl.ds(row, 1)] = total[pl.ds(at + late + 2 + row, 1), own]
+        up_out[pl.ds(l, 1)] = total[pl.ds(at + 4 + j, 1)]
+
+
+def reduce_kernel(
+    lines, first0, first1, rest0, rest1, *refs,
+):
+    smalls, refs = refs[:4], refs[4:]
+    (qkv_out, out_out, up_out, down_out), refs = refs[:4], refs[4:]
+    vector_outs, refs = refs[:5], refs[5:]
+    (small_own, small_near, small_far, small_total, send_sem, recv_sem), refs = refs[:6], refs[6:]
+    greet(near_peers(lines))
+    copies = Copies(send_sem, recv_sem)
+    sections = []
+    for l, source in ((1, rest1), (1, first1), (0, rest0), (0, first0)):
+        for first in range(0, source.shape[1], SECTION):
+            at = len(sections)
+            sections.append(
+                (l, source.shape[1] == 3, first,
+                 Reduce((l, at), source, (first, SECTION), copies,
+                        refs[BUFFERS * at : BUFFERS * (at + 1)], lines))
+            )
+    count = up_out.shape[2] // LANES
+
+    def put(l, is_first, first, section):
+        section.end()
+        for at in range(SECTION):
+            value = section.result(at)
+            block = first + at
+            if is_first:
+                qkv_out[l, block] = value
+            elif block == 0:
+                out_out[l] = value.T
+            elif block <= count:
+                up_out[l, :, pl.ds((block - 1) * LANES, LANES)] = value
+            else:
+                down_out[l, pl.ds((block - 1 - count) * LANES, LANES), :] = value.T
+
+    def small(stage):
+        return small_sums(smalls, copies, lines, small_own, small_near, small_far, stage)
+
+    for section in sections:
+        section[3].begin()
+    total = len(sections)
+    for at in range(total + 3):
+        if at < 5:
+            done = small(at)
+            if at == 4:
+                small_total[...] = done
+                store_vectors(small_total, vector_outs)
+        if at < total:
+            sections[at][3].first_sum()
+        if 1 <= at < total + 1:
+            sections[at - 1][3].second_sum()
+        if 2 <= at < total + 2:
+            sections[at - 2][3].third_sum()
+        if 3 <= at:
+            put(*sections[at - 3])
+    copies.finish()
+
+
+def reduce_all(firsts, rests, smalls, shapes):
+    lines, groups = lax.axis_size("dp") // 2, lax.axis_size("tensor")
+    d = firsts[0].shape[2]
+    share = d // (2 * lines)
+    number = 2 * (firsts[0].shape[1] + rests[0].shape[1]) // SECTION
+    rows = sum(small.shape[0] for small in smalls)
+    width = smalls[0].shape[2]
+    vmem = pl.BlockSpec(memory_space=pltpu.VMEM)
+    hbm = pl.BlockSpec(memory_space=pl.ANY)
+    scratch = [
+        pltpu.VMEM((4, rows, width), f32),
+        pltpu.VMEM((3, rows, width), f32),
+        pltpu.VMEM((lines, rows, width), f32),
+        pltpu.VMEM((rows, width), f32),
+        pltpu.SemaphoreType.DMA((REDUCE_COPIES,)),
+        pltpu.SemaphoreType.DMA((REDUCE_COPIES,)),
+    ]
+    for _ in range(number):
+        scratch += Reduce.buffers(lines, groups, SECTION, share)
+    return pl.pallas_call(
+        functools.partial(reduce_kernel, lines),
+        name="reduce",
+        in_specs=[hbm] * 4 + [vmem] * len(smalls),
+        out_specs=[vmem] * len(shapes),
+        out_shape=[jax.ShapeDtypeStruct(shape, f32) for shape in shapes],
+        scratch_shapes=scratch,
+        compiler_params=pltpu.CompilerParams(
+            collective_id=1, has_side_effects=True, vmem_limit_bytes=VMEM_LIMIT
+        ),
+    )(*firsts, *rests, *smalls)
 
 
 def body(
@@ -511,15 +1133,20 @@
     per_tile = tile // SPAN
     own_blocks = rows // SPAN
     groups = lax.axis_size("tensor")
-    ff = bias_up.shape[1] * groups
     blocks = d // LANES
-    count = ff // d
+    ff = w_down.shape[1] * groups
     all_blocks = own_blocks * groups
-    bias_qv_all = lax.all_gather(bias_qv, "tensor", axis=2, tiled=True)
-    bias_up_all = lax.all_gather(bias_up, "tensor", axis=1, tiled=True)
-    firsts, rests = zip(
-        *(gather_weights(w_qkv[l], w_out[l], w_up[l], w_down[l]) for l in range(LAYERS))
-    )
+    direct = blocks == groups == 4
+    if direct:
+        firsts, rests, pair_all, up_all = gather_all(w_qkv, w_out, w_up, w_down, bias_qv, bias_up)
+    else:
+        firsts, rests = zip(
+            *(gather_weights(w_qkv[l], w_out[l], w_up[l], w_down[l]) for l in range(LAYERS))
+        )
+        pair_all = lax.all_gather(bias_qv, "tensor", axis=2, tiled=True)
+        pair_all = jnp.transpose(pair_all.reshape(LAYERS, 2, blocks, LANES), (2, 0, 1, 3))
+        up_all = lax.all_gather(bias_up, "tensor", axis=1, tiled=True)
+        up_all = jnp.transpose(up_all.reshape(LAYERS, blocks, -1), (1, 0, 2))
     sums_shape = (steps, per_tile, 2 * d)
     triple = [("t", (rows, d), bf16)] * 3 + [("s", sums_shape, f32)]
     back = [
@@ -527,7 +1154,7 @@
         ("t", (rows, d), bf16),
         ("t", (rows, d), f32),
         ("t", (rows, d), f32),
-        ("w", (all_blocks, 2 * d), f32),
+        ("w", (groups, own_blocks, 2 * d), f32),
         ("w", rests[0].shape, bf16),
         ("w", (4 + blocks, 8, d), f32),
     ]
@@ -535,59 +1162,68 @@
     acc = pltpu.VMEM(rests[0].shape, f32)
     first_acc = pltpu.VMEM(firsts[0].shape, f32)
     tile_bf16 = pltpu.VMEM((tile, d), bf16)
-
-    q0, k0, v0, sums0 = call(
-        start_kernel, "start", tile, steps,
-        [("t", inputs), ("w", firsts[0]), ("w", ln_gain[0]), ("w", ln_bias[0]), ("w", bias_qv_all[0])],
-        triple,
-    )
-    sums0 = share_sums(sums0)
-    att0, log0, middle0, act0, slope0, x1, q1, k1, v1, sums1 = call(
-        forward_kernel, "forward", tile, steps,
-        [("t", inputs), ("t", q0), ("t", k0), ("t", v0), ("w", sums0), ("w", rests[0]),
-         ("w", ln_gain[0]), ("w", ln_bias[0]), ("w", bias_up_all[0:1]), ("w", branch_bias[0]),
-         ("w", firsts[1]), ("w", ln_gain[1]), ("w", ln_bias[1]), ("w", bias_qv_all[1])],
+    flat = pltpu.VMEM((all_blocks, 2 * d), f32)
+    norm = [("w", ln_gain), ("w", ln_bias)]
+
+    def run(kernel, l, name, ins, outs, scratch):
+        return call(functools.partial(kernel, l), name, tile, steps, ins, outs, scratch)
+
+    q0, k0, v0, sums0 = run(
+        start_kernel, 0, "start",
+        [("t", inputs), ("w", firsts[0])] + norm + [("w", pair_all)],
+        triple, [],
+    )
+    sums0 = share_sums(sums0, 2)
+    att0, log0, middle0, act0, slope0, x1, q1, k1, v1, sums1 = run(
+        forward_kernel, 0, "forward",
+        [("t", inputs), ("t", q0), ("t", k0), ("t", v0), ("w", sums0), ("w", rests[0])]
+        + norm + [("w", up_all), ("w", branch_bias), ("w", firsts[1]), ("w", pair_all)],
         [("t", (rows, d), bf16), ("b", (own_blocks, blocks, 2 * SPAN), f32), ("t", (rows, d), f32),
          ("t", (rows, ff), bf16), ("t", (rows, ff), bf16), ("t", (rows, d), f32)] + triple,
-    )
-    sums1 = share_sums(sums1)
-    outputs, dmid1, dq1, dk1, dv1, dsum1, rest1, small1 = call(
-        turn_kernel, "turn", tile, steps,
-        [("t", x1), ("t", q1), ("t", k1), ("t", v1), ("w", sums1), ("w", rests[1]),
-         ("w", ln_gain[1]), ("w", ln_bias[1]), ("w", bias_up_all[1:2]), ("w", branch_bias[1]),
-         ("t", cotangent)],
+        [flat],
+    )
+    sums1 = share_sums(sums1, 2)
+    outputs, dmid1, dq1, dk1, dv1, dsum1, rest1, small1 = run(
+        turn_kernel, 1, "turn",
+        [("t", x1), ("t", q1), ("t", k1), ("t", v1), ("w", sums1), ("w", rests[1])]
+        + norm + [("w", up_all), ("w", branch_bias), ("t", cotangent)],
         [("t", (rows, d), bf16)] + back,
         [tile_bf16, pltpu.VMEM((per_tile, blocks, 2 * SPAN), f32), pltpu.VMEM((tile, ff), bf16),
-         pltpu.VMEM((tile, ff), bf16), tile_bf16, acc],
-    )
-    dsum1 = return_sums(dsum1, sums_shape)
-    first1, small1_first, dmid0, dq0, dk0, dv0, dsum0, rest0, small0 = call(
-        backward_kernel, "backward", tile, steps,
-        [("t", x1), ("t", dmid1), ("t", dq1), ("t", dk1), ("t", dv1), ("s", dsum1), ("w", firsts[1]),
-         ("w", ln_gain[1]), ("w", ln_bias[1]), ("w", rests[0]), ("w", ln_gain[0]), ("w", ln_bias[0]),
-         ("t", middle0), ("t", att0), ("b", log0), ("t", act0), ("t", slope0),
-         ("t", q0), ("t", k0), ("t", v0), ("w", sums0)],
+         pltpu.VMEM((tile, ff), bf16), tile_bf16, acc, flat, flat],
+    )
+    dsum1 = return_sums(dsum1, sums_shape, 3)
+    first1, small1_first, dmid0, dq0, dk0, dv0, dsum0, rest0, small0 = run(
+        backward_kernel, 0, "backward",
+        [("t", x1), ("t", dmid1), ("t", dq1), ("t", dk1), ("t", dv1), ("s", dsum1),
+         ("w", firsts[1]), ("w", rests[0])] + norm
+        + [("t", middle0), ("t", att0), ("b", log0), ("t", act0), ("t", slope0),
+           ("t", q0), ("t", k0), ("t", v0), ("w", sums0)],
         first_out + back,
-        [first_acc, acc, tile_bf16],
-    )
-    dsum0 = return_sums(dsum0, sums_shape)
-    dx, first0, small0_first = call(
-        finish_kernel, "finish", tile, steps,
+        [first_acc, acc, tile_bf16, flat, flat],
+    )
+    dsum0 = return_sums(dsum0, sums_shape, 3)
+    dx, first0, small0_first = run(
+        finish_kernel, 0, "finish",
         [("t", inputs), ("t", dmid0), ("t", dq0), ("t", dk0), ("t", dv0), ("s", dsum0),
-         ("w", firsts[0]), ("w", ln_gain[0]), ("w", ln_bias[0])],
+         ("w", firsts[0])] + norm,
         [("t", (rows, d), f32)] + first_out,
         [first_acc],
     )
+    smalls = (small0, small0_first, small1, small1_first)
+    like = (w_qkv.shape, w_out.shape, w_up.shape, w_down.shape, ln_gain.shape, ln_bias.shape,
+            bias_qv.shape, bias_up.shape, branch_bias.shape)
+    if direct:
+        return (outputs, dx, *reduce_all((first0, first1), (rest0, rest1), smalls, like))
     weight_grads = [scatter_grads(first0, rest0), scatter_grads(first1, rest1)]
     joined = [jnp.stack([grads[at] for grads in weight_grads]) for at in range(4)]
     late = jnp.sum(jnp.stack([small0, small1]), 2)
     early = jnp.sum(jnp.stack([small0_first, small1_first]), 2)
     late, early = lax.psum((late, early), ("dp", "tensor"))
-    place = lax.axis_index("tensor")
+    spot = lax.axis_index("tensor")
 
     def own(array):
         size = array.shape[-1] // groups
-        return lax.dynamic_slice_in_dim(array, place * size, size, array.ndim - 1)
+        return lax.dynamic_slice_in_dim(array, spot * size, size, array.ndim - 1)
 
     gain_grad = jnp.stack([early[:, 0], late[:, 0]], 1)
     shift_grad = jnp.stack([early[:, 1], late[:, 1]], 1)

time: 930 us -> 353 us (0.38)
  waiting for transfers between devices: 301 us -> 0 us
  blocking collectives: 269 us -> 0 us
  Pallas kernels: 159 us -> 335 us
  local copies, waits for them, and re-layouts: 159 us -> 16.5 us
  between operations: 16.7 us -> 0.72 us
  other arithmetic: 10.8 us -> 0 us
    all_gather x14 -> x0, blocking collectives: 182 us -> none  [the longest x8 122 us: both(): piece = lax.all_gather(piece, 'dp', axis=dp_axis, tiled=True)]
    pallas_call x0 -> x6, Pallas kernels: none -> 175 us  [the longest x1 73.5 us: gather_all(): pl.pallas_call(functools.partial(gather_kernel, lines), name='gather', in...]
    unnamed x32 -> x0, waiting for transfers between devices: 152 us -> none
    reduce_scatter x6 -> x0, waiting for transfers between devices: 149 us -> none  [both(): lax.psum_scatter(matrix, 'tensor', scatter_dimension=tensor_axis, tiled=T...]
    unnamed x78 -> x11, local copies, waits for them, and re-layouts: 106 us -> 16.5 us
    unnamed x2 -> x0, blocking collectives: 47.8 us -> none
    psum x1 -> x0, blocking collectives: 38.9 us -> none  [body(): late, early = lax.psum((late, early), ('dp', 'tensor'))]
    transpose x12 -> x0, local copies, waits for them, and re-layouts: 25.8 us -> none  [the longest x10 23.4 us: natural(): return jnp.transpose(part, (2, 0, 1, 3)).reshape(d, -1)]
  transfers between devices with their start and end apart: 23 -> 0, of which waited for: 12 -> 0; matrix products, arithmetic and copies ran while one was open for 22% -> 0% of each run, Pallas kernels for 11% -> 0%
where the time goes in v2:
time: 353 us; the launch traced here: 352 us
  Pallas kernels  335 us (95%)
  local copies, waits for them, and re-layouts  16.5 us (5%)
    pallas_call x5, Pallas kernels, call(): pl.pallas_call(kernel, name=name, grid=(steps,), in_specs=[spec(kind, arg...  160 us
    pallas_call x1, Pallas kernels, gather_all(): pl.pallas_call(functools.partial(gather_kernel, lines), name='gather', in...  73.5 us
    pallas_call x1, Pallas kernels, reduce_all(): pl.pallas_call(functools.partial(reduce_kernel, lines), name='reduce', in...  71.4 us
    unnamed x11, local copies, waits for them, and re-layouts  16.5 us
    pallas_call x2, Pallas kernels, return_sums(): pl.pallas_call(functools.partial(return_kernel, groups), name='return', i...  15.1 us
    pallas_call x2, Pallas kernels, share_sums(): pl.pallas_call(functools.partial(share_kernel, groups), name='share', in_...  15 us

profile of v2, /device:TPU:0, one launch (start us, length us, event | category | flops | bytes accessed | tf_op | source)
XLA Modules:
  0.0 351.8 jit_solution(9225226559006492859)
XLA Ops:
  0.6 1.5 copy.22.out_w_ref
  2.1 1.7 copy.23.down_ref
  3.9 73.5 %gather.1 = (bf16[4,3,512,128]{3,2,1,0:T(8,128)(2,1)}, bf16[4,3,512,128]{3,2,1,0:T(8,128)(2,1)}, bf16[4,9,512,128]{3,2,1,0:T(8,128)(2,1)}, bf16[4,9,512,128]{3,2...) custom-call(bf16[2,3,64,128]{3,2,1,0:T(8,128)(2,1)} %qkv_ref.1, bf16[2,128,64]{2,1,0:T(8,128)(2,1)} %copy.22.out_w_ref, ...), custom_call_target="tpu_custom_call" | custom-call | tf_op jit(solution)/shard_map/gather/pallas_call | solution.py:753
  77.4 7.8 %start.1 = (bf16[1536,512]{1,0:T(8,128)(2,1)}, bf16[1536,512]{1,0:T(8,128)(2,1)}, bf16[1536,512]{1,0:T(8,128)(2,1)}, f32[6,2,1024]{2,1,0:T(2,128)}) custom-call(bf16[1536,512]{1,0:T(8,128)(2,1)} %x_ref.5, bf16[4,3,512,128]{3,2,1,0:T(8,128)(2,1)} %get-tuple-element.60.w_ref, f32[2,2,512]{2,1,0:T(2,128)} %gain_ref.9, f32[2,2,512]{2,1,0:T(2,128)} %shift_ref.9, ...), custom_call_target="tpu_custom_call" | custom-call | tf_op jit(solution)/shard_map/start/pallas_call | solution.py:472
  85.2 7.8 %share.2.sums_all = f32[4,6,2,1024]{3,2,1,0:T(2,128)} custom-call(f32[6,2,1024]{2,1,0:T(2,128)} %get-tuple-element.65.sums_ref), custom_call_target="tpu_custom_call" | custom-call | tf_op jit(solution)/shard_map/share/pallas_call | solution.py:796
  93.0 31.2 %forward.1 = (bf16[1536,512]{1,0:T(8,128)(2,1)}, f32[12,4,256]{2,1,0:T(4,128)}, f32[1536,512]{1,0:T(8,128)}, bf16[1536,2048]{1,0:T(8,128)(2,1)}, bf16[1536,2048]...) custom-call(bf16[1536,512]{1,0:T(8,128)(2,1)} %x_ref.5, ...), custom_call_target="tpu_custom_call" | custom-call | tf_op jit(solution)/shard_map/forward/pallas_call | solution.py:472
  124.2 7.1 %share.3.sums_all = f32[4,6,2,1024]{3,2,1,0:T(2,128)} custom-call(f32[6,2,1024]{2,1,0:T(2,128)} %get-tuple-element.73.sums_ref), custom_call_target="tpu_custom_call" | custom-call | tf_op jit(solution)/shard_map/share/pallas_call | solution.py:796
  131.3 58.0 %turn.1 = (bf16[1536,512]{1,0:T(8,128)(2,1)}, f32[1536,512]{1,0:T(8,128)}, bf16[1536,512]{1,0:T(8,128)(2,1)}, f32[1536,512]{1,0:T(8,128)}, f32[1536,512]{1,0:T(8...) custom-call(f32[1536,512]{1,0:T(8,128)} %get-tuple-element.69.x_ref, ...), custom_call_target="tpu_custom_call" | custom-call | tf_op jit(solution)/shard_map/turn/pallas_call | solution.py:472
  189.3 7.5 %return.2.dsum_in = f32[6,2,1024]{2,1,0:T(2,128)} custom-call(f32[4,12,1024]{2,1,0:T(8,128)} %get-tuple-element.80.dsum_ref), custom_call_target="tpu_custom_call" | custom-call | tf_op jit(solution)/shard_map/return/pallas_call | solution.py:831
  196.9 49.3 %backward.1 = (bf16[4,3,512,128]{3,2,1,0:T(8,128)(2,1)}, f32[4,8,512]{2,1,0:T(8,128)}, f32[1536,512]{1,0:T(8,128)}, bf16[1536,512]{1,0:T(8,128)(2,1)}, f32[1536,...) custom-call(f32[1536,512]{1,0:T(8,128)} %get-tuple-element.69.x_ref,, ...), custom_call_target="tpu_custom_call" | custom-call | tf_op jit(solution)/shard_map/backward/pallas_call | solution.py:472
  246.2 7.5 %return.3.dsum_in = f32[6,2,1024]{2,1,0:T(2,128)} custom-call(f32[4,12,1024]{2,1,0:T(8,128)} %get-tuple-element.90.dsum_ref), custom_call_target="tpu_custom_call" | custom-call | tf_op jit(solution)/shard_map/return/pallas_call | solution.py:831
  253.8 13.3 %finish.1 = (f32[1536,512]{1,0:T(8,128)}, bf16[4,3,512,128]{3,2,1,0:T(8,128)(2,1)}, f32[4,8,512]{2,1,0:T(8,128)}) custom-call(bf16[1536,512]{1,0:T(8,128)(2,1)} %x_ref.5, f32[1536,512]{1,0:T(8,128)} %get-tuple-element.86.dmid_in, bf16[1536,512]{1,0:T(8,128)(2,1)} %get-tuple-element.87.dq_in, f32[1536,512]{1,0:T(8,128)} %get-tuple-element.88.dk_in, ...), custom_call_target="tpu_custom_call" | custom-call | tf_op jit(solution)/shard_map/finish/pallas_call | solution.py:472
  267.1 71.4 %reduce.1 = (f32[2,3,64,128]{3,2,1,0:T(8,128)}, f32[2,128,64]{2,1,0:T(8,128)}, f32[2,64,512]{2,1,0:T(8,128)}, f32[2,512,64]{2,1,0:T(8,128)}, f32[2,2,512]{2,1,0:...) custom-call(bf16[4,3,512,128]{3,2,1,0:T(8,128)(2,1)} %get-tuple-element.92.firs, ...), custom_call_target="tpu_custom_call" | custom-call | tf_op jit(solution)/shard_map/reduce/pallas_call | solution.py:1114
  338.5 1.6 copy.24
  340.2 1.9 copy.25
  342.1 1.6 copy.33
  343.7 1.7 copy.34
  345.4 1.3 copy.35
  346.7 1.3 copy.36
  348.0 1.3 copy.37
  349.2 1.3 copy.38
  350.5 1.3 copy.39

commit v3 on v2

--- a/solution.py
+++ b/solution.py
@@ -126,7 +126,11 @@
     return jnp.concatenate([rows, summaries[pl.ds(start, SEQ_BLOCKS), lanes].astype(bf16)], 0)
 
 
-def attend_tile(base, q_ref, k_ref, v_ref, sum_ref, att_ref, log_ref):
+def no_tick():
+    pass
+
+
+def attend_tile(base, q_ref, k_ref, v_ref, sum_ref, att_ref, log_ref, tick=no_tick):
     width = q_ref.shape[1]
     masks = pair_masks()
     for at in range(q_ref.shape[0] // SPAN):
@@ -141,6 +145,7 @@
             mixed, log_total = pair_forward(q_ref[rows, lanes], keys, values, before, masks)
             att_ref[rows, lanes] = mixed
             log_ref[at, pl.ds(pair, 1), :] = log_total
+        tick()
 
 
 def attend_back_tile(
@@ -187,10 +192,10 @@
     width = keys.shape[1]
     for at in range(keys.shape[0] // SPAN):
         part = slice(at * SPAN, (at + 1) * SPAN)
-        sum_ref[0, pl.ds(at, 1), pl.ds(0, width)] = jnp.mean(
+        sum_ref[pl.ds(at, 1), pl.ds(0, width)] = jnp.mean(
             keys[part].astype(f32), 0, keepdims=True
         )
-        sum_ref[0, pl.ds(at, 1), pl.ds(width, width)] = jnp.mean(
+        sum_ref[pl.ds(at, 1), pl.ds(width, width)] = jnp.mean(
             values[part].astype(f32), 0, keepdims=True
         )
 
@@ -204,7 +209,9 @@
     return jnp.concatenate([ref[j, first + at] for at in range(count)], 1)
 
 
-def mlp_tile(middle, w_ref, gain, shift, l, bias_up, branch_bias, act_ref, slope_ref):
+def mlp_tile(
+    middle, w_ref, gain, shift, l, bias_up, branch_bias, act_ref, slope_ref, tick=no_tick
+):
     blocks = w_ref.shape[0]
     count = (w_ref.shape[1] - 1) // 2
     unit, _ = normalized(middle)
@@ -218,6 +225,7 @@
         act_ref[:, j * span : (j + 1) * span] = act
         slope_ref[:, j * span : (j + 1) * span] = slope.astype(bf16)
         total = total + dot_nt(act, wide(w_ref, j, 1 + count, count))
+        tick()
     return total
 
 
@@ -304,6 +312,9 @@
 def lay_out(all_ref, flat_ref):
     @pl.when(pl.program_id(0) == 0)
     def _():
+        if len(all_ref.shape) == 2:
+            flat_ref[...] = all_ref[...]
+            return
         groups, steps, per_tile, _ = all_ref.shape
         for group in range(groups):
             for step in range(steps):
@@ -340,7 +351,7 @@
 def start_kernel(l, x_ref, w_ref, gain_ref, shift_ref, bias_ref, q_ref, k_ref, v_ref, sum_ref):
     project_tile(
         x_ref[...].astype(f32), w_ref, vector(gain_ref, l, 0), vector(shift_ref, l, 0),
-        pair_bias(bias_ref, l), q_ref, k_ref, v_ref, sum_ref,
+        pair_bias(bias_ref, l), q_ref, k_ref, v_ref, sum_ref.at[0],
     )
 
 
@@ -362,7 +373,7 @@
     y_ref[...] = result
     project_tile(
         result, next_w, vector(gain_ref, l + 1, 0), vector(shift_ref, l + 1, 0),
-        pair_bias(bias_ref, l + 1), q_ref, k_ref, v_ref, sum_ref,
+        pair_bias(bias_ref, l + 1), q_ref, k_ref, v_ref, sum_ref.at[0],
     )
 
 
@@ -566,17 +577,18 @@
             device_id_type=pl.DeviceIdType.MESH,
         )
 
-    def send(self, key, source, target, where):
-        copy = self.describe(key, source, target, where)
-        copy.start()
-        self.sent.append(copy)
+    def send(self, key, source, target, where, like=None):
+        self.describe(key, source, target, where).start()
+        self.sent.append((key, like or (lambda: target)))
 
     def receive(self, key, target, where):
         self.describe(key, target, target, where).wait_recv()
 
     def finish(self):
-        for copy in self.sent:
-            copy.wait_send()
+        line, core, j = place()
+        for key, like in self.sent:
+            view = like()
+            self.describe(key, view, view, device(line, 1 - core, j)).wait_send()
         self.sent = []
 
 
@@ -614,8 +626,12 @@
     def key(self, *parts):
         return (self.name,) + parts
 
-    def move(self, key, view, where):
-        self.copies.send(self.key(*key), view, view, where)
+    def move(self, key, view, where, half=False):
+        share = self.ref.shape[2] // (2 * self.lines)
+        size = share // 2 if half else share
+        self.copies.send(
+            self.key(*key), view, view, where, lambda: self.ref.at[0, :, pl.ds(0, size), :]
+        )
 
     def source_line(self, d):
         return lax.rem(self.line + self.lines - d, self.lines)
@@ -625,8 +641,8 @@
         self.move(("high", d), view, device(self.line, self.core, self.high))
         self.partner(("own", d), view)
 
-    def partner(self, key, view):
-        self.move(("partner",) + key, view, device(self.line, 1 - self.core, self.j))
+    def partner(self, key, view, half=False):
+        self.move(("partner",) + key, view, device(self.line, 1 - self.core, self.j), half)
 
     def view(self, column, d, half=None, core=None):
         core = self.core if core is None else core
@@ -641,29 +657,27 @@
             self.move(("line", d), own, device(lax.rem(self.line + d, self.lines), self.core, self.j))
         self.out(0, own)
 
-    def relay_line(self):
-        for d in range(1, self.lines):
-            view = self.view(self.j, d)
-            self.receive(("line", d), view)
-            self.out(d, view)
-
-    def relay_bits(self):
-        for d in range(self.lines):
-            for name, column, half, other, where in (
-                ("low", self.low, 0, "far_high", self.high),
-                ("high", self.high, 1, "far_low", self.low),
-            ):
-                view = self.view(column, d)
-                self.receive((name, d), view)
-                self.move((other, d), self.view(column, d, half), device(self.line, self.core, where))
-                self.partner((name, d), view)
-
-    def relay_far(self):
-        for d in range(self.lines):
-            for name, half in (("far_high", 0), ("far_low", 1)):
-                view = self.view(self.far, d, half)
-                self.receive((name, d), view)
-                self.partner((name, d), view)
+    def relay_line(self, d):
+        view = self.view(self.j, d)
+        self.receive(("line", d), view)
+        self.out(d, view)
+
+    def relay_bits(self, d):
+        for name, column, half, other, where in (
+            ("low", self.low, 0, "far_high", self.high),
+            ("high", self.high, 1, "far_low", self.low),
+        ):
+            view = self.view(column, d)
+            self.receive((name, d), view)
+            half_view = self.view(column, d, half)
+            self.move((other, d), half_view, device(self.line, self.core, where), True)
+            self.partner((name, d), view)
+
+    def relay_far(self, d):
+        for name, half in (("far_high", 0), ("far_low", 1)):
+            view = self.view(self.far, d, half)
+            self.receive((name, d), view)
+            self.partner((name, d), view, True)
 
     def collect(self):
         for d in range(self.lines):
@@ -674,100 +688,318 @@
                 self.receive(("partner", name, d), view)
 
 
-GATHER_COPIES = 200
-
-
-def gather_kernel(
-    lines, qkv_ref, out_w_ref, up_ref, down_ref, pair_ref, up_bias_ref,
-    first0, first1, rest0, rest1, pair_all, up_all,
-    own_first, own_rest, send_sem, recv_sem, local_sem,
+GATHER_COPIES = 170
+
+
+def when_step(step, act):
+    pl.when(pl.program_id(0) == step)(act)
+
+
+class Agenda:
+    def __init__(self, actions):
+        self.actions, self.at = actions, 0
+
+    def restart(self):
+        self.at = 0
+
+    def tick(self):
+        for (step, at), acts in sorted(self.actions.items()):
+            if at == self.at:
+
+                def run(acts=acts):
+                    for act in acts:
+                        act()
+
+                when_step(step, run)
+        self.at += 1
+
+
+class Sums:
+    def __init__(self, ref, send_sem, recv_sem, groups):
+        self.ref, self.send_sem, self.recv_sem, self.groups = ref, send_sem, recv_sem, groups
+        self.spot, self.j = lax.axis_index("dp"), lax.axis_index("tensor")
+
+    def copy(self, source, d, tile, to):
+        view = self.ref.at[source, tile]
+        return pltpu.make_async_remote_copy(
+            src_ref=view,
+            dst_ref=view,
+            send_sem=self.send_sem.at[tile, d - 1],
+            recv_sem=self.recv_sem.at[tile, d - 1],
+            device_id=(self.spot, to),
+            device_id_type=pl.DeviceIdType.MESH,
+        )
+
+    def own(self, tile):
+        return self.ref.at[self.j, tile]
+
+    def send(self, tile):
+        for d in range(1, self.groups):
+            self.copy(self.j, d, tile, lax.rem(self.j + d, self.groups)).start()
+
+    def receive(self):
+        for tile in range(self.ref.shape[1]):
+            for d in range(1, self.groups):
+                other = lax.rem(self.j + self.groups - d, self.groups)
+                self.copy(other, d, tile, other).wait_recv()
+
+    def finish(self):
+        for tile in range(self.ref.shape[1]):
+            for d in range(1, self.groups):
+                self.copy(self.j, d, tile, lax.rem(self.j + d, self.groups)).wait_send()
+
+    def flatten(self, flat_ref):
+        groups, steps, per_tile, _ = self.ref.shape
+        for group in range(groups):
+            for step in range(steps):
+                at = (group * steps + step) * per_tile
+                flat_ref[pl.ds(at, per_tile)] = self.ref[group, step]
+
+
+def ascend_kernel(
+    lines, groups, steps, x_ref, qkv_ref, out_w_ref, up_ref, down_ref, pair_ref, up_bias_ref,
+    gain_ref, shift_ref, branch_bias,
+    q_out, k_out, v_out, sums0, att_ref, log_ref, middle_ref, act_ref, slope_ref, y_ref,
+    q_ref, k_ref, v_ref, sums1, first0_out, rest0_out, first1_out, rest1_out, up_out,
+    first0, rest0, first1, rest1, own_first, own_rest, q_all, k_all, v_all, sums0_in, sums1_in,
+    pair_all, up_all, send_sem, recv_sem, local_sem, sum_send, sum_recv,
 ):
     line, core, j = place()
-    far = flip_high(flip_low(j))
-    greet(near_peers(lines) + [device(line, core, far)])
+    low, high = flip_low(j), flip_high(j)
+    far = flip_high(low)
+    others = (low, high, far)
+    step = pl.program_id(0)
+    tile = x_ref.shape[0]
+    count = up_ref.shape[2] // LANES
     copies = Copies(send_sem, recv_sem)
-    stores = []
-
-    def store(source, target):
-        copy = pltpu.make_async_copy(source, target, local_sem.at[len(stores)])
-        copy.start()
-        stores.append(copy)
-
     firsts, rests = (first0, first1), (rest0, rest1)
-    count = up_ref.shape[2] // LANES
-    for l in range(LAYERS):
-        own_first[l] = qkv_ref[l]
-        own_rest[l, 0] = out_w_ref[l].T
-        turned = down_ref[l].T
-        for at in range(count):
-            own_rest[l, 1 + at] = up_ref[l, :, at * LANES : (at + 1) * LANES]
-            own_rest[l, 1 + count + at] = turned[:, at * LANES : (at + 1) * LANES]
-    for l in range(LAYERS):
-        store(own_first.at[l], piece(firsts[l], j, line, core))
-        store(own_rest.at[l], piece(rests[l], j, line, core))
-    store(pair_ref, pair_all.at[j])
-    store(up_bias_ref, up_all.at[j])
-    sections = []
-    for l in range(LAYERS):
-        sections.append(Gather(("first", l), firsts[l], copies, lines))
-        sections.append(Gather(("rest", l), rests[l], copies, lines))
-    stores[0].wait()
-    sections[0].begin()
-    others = (flip_low(j), flip_high(j), far)
-    for at, other in enumerate(others):
-        where = device(line, core, other)
-        copies.send(("pair", at), pair_ref, pair_all.at[j], where)
-        copies.send(("up", at), up_bias_ref, up_all.at[j], where)
-    for at in range(1, len(sections)):
-        stores[at].wait()
-        sections[at].begin()
-        previous = sections[at - 1]
-        previous.relay_line()
-        previous.relay_bits()
-        previous.relay_far()
-    last = sections[-1]
-    last.relay_line()
-    last.relay_bits()
-    last.relay_far()
-    for section in sections:
-        section.collect()
-    for at, other in enumerate(others):
-        where = device(line, core, other)
-        copies.receive(("pair", at), pair_all.at[other], where)
-        copies.receive(("up", at), up_all.at[other], where)
-    for copy in stores[len(sections) :]:
-        copy.wait()
-    copies.finish()
-
-
-def gather_all(w_qkv, w_out, w_up, w_down, bias_qv, bias_up):
+    sections = [
+        Gather((name, l), refs[l], copies, lines)
+        for l in range(LAYERS)
+        for name, refs in (("first", firsts), ("rest", rests))
+    ]
+    first_a, rest_a, first_b, rest_b = sections
+    sum_copies = [
+        Sums(ref, sum_send.at[l], sum_recv.at[l], groups)
+        for l, ref in enumerate((sums0_in, sums1_in))
+    ]
+    relayed = range(1, lines), range(lines), range(lines)
+
+    def store(l, at):
+        source, target = ((own_first, firsts), (own_rest, rests))[at]
+        return pltpu.make_async_copy(
+            source.at[l], piece(target[l], j, line, core), local_sem.at[2 * l + at]
+        )
+
+    def keep(at):
+        source, target = (
+            (first0, first0_out), (rest0, rest0_out), (first1, first1_out), (rest1, rest1_out),
+            (q_all, q_out), (k_all, k_out), (v_all, v_out),
+        )[at]
+        return pltpu.make_async_copy(source, target, local_sem.at[2 * LAYERS + at])
+
+    def begin():
+        greet(near_peers(lines) + [device(line, core, far)])
+        for l in range(LAYERS):
+            own_first[l] = qkv_ref[l]
+            own_rest[l, 0] = out_w_ref[l].T
+            turned = down_ref[l].T
+            for at in range(count):
+                own_rest[l, 1 + at] = up_ref[l, :, at * LANES : (at + 1) * LANES]
+                own_rest[l, 1 + count + at] = turned[:, at * LANES : (at + 1) * LANES]
+        for l in range(LAYERS):
+            store(l, 0).start()
+            store(l, 1).start()
+        pair_all[j] = pair_ref[...]
+        up_all[j] = up_bias_ref[...]
+        store(0, 0).wait()
+        first_a.begin()
+        for at, other in enumerate(others):
+            where = device(line, core, other)
+            copies.send(("pair", at), pair_ref, pair_all.at[j], where, lambda: pair_ref)
+            copies.send(("up", at), up_bias_ref, up_all.at[j], where, lambda: up_bias_ref)
+        for d in relayed[0]:
+            first_a.relay_line(d)
+        store(0, 1).wait()
+        rest_a.begin()
+        for d in relayed[1]:
+            first_a.relay_bits(d)
+        for d in relayed[2]:
+            first_a.relay_far(d)
+        for at, other in enumerate(others):
+            where = device(line, core, other)
+            copies.receive(("pair", at), pair_all.at[other], where)
+            copies.receive(("up", at), up_all.at[other], where)
+        first_a.collect()
+        keep(0).start()
+
+    def start_second():
+        store(1, 0).wait()
+        first_b.begin()
+
+    def start_third():
+        store(1, 1).wait()
+        rest_b.begin()
+
+    def rest_ready():
+        rest_a.collect()
+        keep(1).start()
+
+    def first_ready():
+        first_b.collect()
+        keep(2).start()
+
+    def step_of(kind, section, d):
+        return functools.partial(getattr(section, "relay_" + kind), d)
+
+    actions = {}
+
+    def at(when, *acts):
+        actions.setdefault(when, []).extend(acts)
+
+    at((0, 0), begin)
+    at((1, 0), step_of("line", rest_a, 1))
+    at((2, 0), step_of("line", rest_a, 2), step_of("line", rest_a, 3))
+    at((3, 0), start_second)
+    at((4, 0), step_of("bits", rest_a, 0))
+    at((5, 0), step_of("bits", rest_a, 1))
+    last = 2 * steps - 1
+    one = steps
+    at((one, 0), step_of("bits", rest_a, 2), step_of("far", rest_a, 0))
+    at((one, 1), step_of("bits", rest_a, 3), step_of("far", rest_a, 1), step_of("line", first_b, 1),
+       step_of("line", first_b, 2), step_of("line", first_b, 3), start_third)
+    at((one, 2), step_of("far", rest_a, 2), step_of("far", rest_a, 3), rest_ready)
+    at((one, 3), step_of("bits", first_b, 0), step_of("bits", first_b, 1))
+    at((one, 4), step_of("bits", first_b, 2), step_of("bits", first_b, 3))
+    at((one, 5), step_of("far", first_b, 0), step_of("far", first_b, 1))
+    at((one, 6), step_of("far", first_b, 2), step_of("far", first_b, 3), first_ready,
+       step_of("line", rest_b, 1))
+    at((one + 1, 0), step_of("line", rest_b, 2))
+    at((one + 1, 1), step_of("line", rest_b, 3))
+    at((one + 1, 4), step_of("bits", rest_b, 0))
+    at((one + 2, 1), step_of("bits", rest_b, 1), step_of("far", rest_b, 0))
+    at((one + 2, 4), step_of("bits", rest_b, 2), step_of("far", rest_b, 1))
+    at((one + 3, 1), step_of("bits", rest_b, 3), step_of("far", rest_b, 2))
+    at((one + 3, 6), step_of("far", rest_b, 3))
+
+    @pl.when(step < steps)
+    def _():
+        agenda = Agenda({key: acts for key, acts in actions.items() if key[0] < steps})
+        agenda.tick()
+        rows = pl.ds(pl.multiple_of(step * tile, tile), tile)
+        project_tile(
+            x_ref[...].astype(f32), first0, vector(gain_ref, 0, 0), vector(shift_ref, 0, 0),
+            pair_bias(pair_all, 0), q_all.at[rows], k_all.at[rows], v_all.at[rows],
+            sum_copies[0].own(step),
+        )
+        sum_copies[0].send(step)
+
+    @pl.when(step >= steps)
+    def _():
+        agenda = Agenda({key: acts for key, acts in actions.items() if key[0] >= steps})
+        now = step - steps
+
+        def arrive():
+            for at in (4, 5, 6):
+                keep(at).start()
+            sum_copies[0].receive()
+            sum_copies[0].flatten(sums0)
+
+        when_step(steps, arrive)
+        agenda.tick()
+        rows = pl.ds(pl.multiple_of(now * tile, tile), tile)
+        base = j * (steps * (tile // SPAN)) + now * (tile // SPAN)
+        attend_tile(
+            base, q_all.at[rows], k_all.at[rows], v_all.at[rows], sums0, att_ref, log_ref,
+            agenda.tick,
+        )
+        middle = middle_of(x_ref[...].astype(f32), att_ref[...], rest0, vector(branch_bias, 0, 0))
+        middle_ref[...] = middle
+        result = mlp_tile(
+            middle, rest0, vector(gain_ref, 0, 1), vector(shift_ref, 0, 1), 0, up_all,
+            vector(branch_bias, 0, 1), act_ref, slope_ref, agenda.tick,
+        )
+        y_ref[...] = result
+        project_tile(
+            result, first1, vector(gain_ref, 1, 0), vector(shift_ref, 1, 0), pair_bias(pair_all, 1),
+            q_ref, k_ref, v_ref, sum_copies[1].own(now),
+        )
+        sum_copies[1].send(now)
+
+    def end():
+        up_out[...] = up_all[...]
+        rest_b.collect()
+        keep(3).start()
+        sum_copies[1].receive()
+        sum_copies[1].flatten(sums1)
+        for group in sum_copies:
+            group.finish()
+        for at in range(7):
+            keep(at).wait()
+        copies.finish()
+
+    when_step(last, end)
+
+
+def ascend(inputs, w_qkv, w_out, w_up, w_down, bias_qv, bias_up, ln_gain, ln_bias, branch_bias, tile):
     lines, groups = lax.axis_size("dp") // 2, lax.axis_size("tensor")
-    d = w_up.shape[1] * 2 * lines
+    rows, d = inputs.shape
+    steps = rows // tile
+    per_tile = tile // SPAN
     count = w_up.shape[2] // LANES
-    first = jax.ShapeDtypeStruct((groups, 3, d, LANES), bf16)
-    rest = jax.ShapeDtypeStruct((groups, 1 + 2 * count, d, LANES), bf16)
+    ff = w_down.shape[1] * groups
+    blocks = rows // SPAN
     share = d // (2 * lines)
-    pair_all = jax.ShapeDtypeStruct((groups,) + bias_qv.shape, f32)
-    up_all = jax.ShapeDtypeStruct((groups,) + bias_up.shape, f32)
     vmem = pl.BlockSpec(memory_space=pltpu.VMEM)
-    outs = pl.pallas_call(
-        functools.partial(gather_kernel, lines),
-        name="gather",
-        in_specs=[vmem] * 6,
-        out_specs=[pl.BlockSpec(memory_space=pl.ANY)] * 6,
-        out_shape=[first, first, rest, rest, pair_all, up_all],
+    hbm = pl.BlockSpec(memory_space=pl.ANY)
+    first = (groups, 3, d, LANES)
+    rest = (groups, 1 + 2 * count, d, LANES)
+
+    def late(shape):
+        return pl.BlockSpec(
+            shape, lambda i: (jnp.maximum(i - steps, 0),) + (0,) * (len(shape) - 1)
+        )
+
+    def struct(shape, dtype):
+        return jax.ShapeDtypeStruct(shape, dtype)
+
+    flat = struct((blocks * groups, 2 * d), f32)
+    out_specs = [hbm] * 3 + [vmem]
+    out_specs += [late((tile, d)), late((per_tile, groups, 2 * SPAN)), late((tile, d))]
+    out_specs += [late((tile, ff))] * 2 + [late((tile, d))] * 4 + [vmem] + [hbm] * 4 + [vmem]
+    rows_bf16, rows_f32 = struct((rows, d), bf16), struct((rows, d), f32)
+    outs = [rows_bf16] * 3 + [flat, rows_bf16, struct((blocks, groups, 2 * SPAN), f32), rows_f32]
+    outs += [struct((rows, ff), bf16)] * 2 + [rows_f32] + [rows_bf16] * 3 + [flat]
+    outs += [struct(first, bf16), struct(rest, bf16)] * 2
+    outs.append(struct((groups,) + bias_up.shape, f32))
+    return pl.pallas_call(
+        functools.partial(ascend_kernel, lines, groups, steps),
+        name="ascend",
+        grid=(2 * steps,),
+        in_specs=[pl.BlockSpec((tile, d), lambda i: (lax.rem(i, steps), 0))] + [vmem] * 9,
+        out_specs=out_specs,
+        out_shape=outs,
         scratch_shapes=[
+            pltpu.VMEM(first, bf16), pltpu.VMEM(rest, bf16),
+            pltpu.VMEM(first, bf16), pltpu.VMEM(rest, bf16),
             pltpu.VMEM((LAYERS, 3, share, LANES), bf16),
             pltpu.VMEM((LAYERS, 1 + 2 * count, share, LANES), bf16),
+            pltpu.VMEM((rows, d), bf16), pltpu.VMEM((rows, d), bf16), pltpu.VMEM((rows, d), bf16),
+            pltpu.VMEM((groups, steps, per_tile, 2 * d), f32),
+            pltpu.VMEM((groups, steps, per_tile, 2 * d), f32),
+            pltpu.VMEM((groups,) + bias_qv.shape, f32),
+            pltpu.VMEM((groups,) + bias_up.shape, f32),
             pltpu.SemaphoreType.DMA((GATHER_COPIES,)),
             pltpu.SemaphoreType.DMA((GATHER_COPIES,)),
-            pltpu.SemaphoreType.DMA((2 * LAYERS + 2,)),
+            pltpu.SemaphoreType.DMA((2 * LAYERS + 7,)),
+            pltpu.SemaphoreType.DMA((LAYERS, steps, groups - 1)),
+            pltpu.SemaphoreType.DMA((LAYERS, steps, groups - 1)),
         ],
         compiler_params=pltpu.CompilerParams(
-            collective_id=0, has_side_effects=True, vmem_limit_bytes=VMEM_LIMIT
+            dimension_semantics=("arbitrary",), collective_id=0, has_side_effects=True,
+            vmem_limit_bytes=VMEM_LIMIT,
         ),
-    )(w_qkv, w_out, w_up, w_down, bias_qv, bias_up)
-    return outs[0:2], outs[2:4], outs[4], outs[5]
+    )(inputs, w_qkv, w_out, w_up, w_down, bias_qv, bias_up, ln_gain, ln_bias, branch_bias)
 
 
 def group_peers(groups):
@@ -1138,7 +1370,11 @@
     all_blocks = own_blocks * groups
     direct = blocks == groups == 4
     if direct:
-        firsts, rests, pair_all, up_all = gather_all(w_qkv, w_out, w_up, w_down, bias_qv, bias_up)
+        (q0, k0, v0, sums0, att0, log0, middle0, act0, slope0, x1, q1, k1, v1, sums1,
+         first0, rest0, first1, rest1, up_all) = ascend(
+            inputs, w_qkv, w_out, w_up, w_down, bias_qv, bias_up, ln_gain, ln_bias, branch_bias, tile
+        )
+        firsts, rests = (first0, first1), (rest0, rest1)
     else:
         firsts, rests = zip(
             *(gather_weights(w_qkv[l], w_out[l], w_up[l], w_down[l]) for l in range(LAYERS))
@@ -1168,21 +1404,22 @@
     def run(kernel, l, name, ins, outs, scratch):
         return call(functools.partial(kernel, l), name, tile, steps, ins, outs, scratch)
 
-    q0, k0, v0, sums0 = run(
-        start_kernel, 0, "start",
-        [("t", inputs), ("w", firsts[0])] + norm + [("w", pair_all)],
-        triple, [],
-    )
-    sums0 = share_sums(sums0, 2)
-    att0, log0, middle0, act0, slope0, x1, q1, k1, v1, sums1 = run(
-        forward_kernel, 0, "forward",
-        [("t", inputs), ("t", q0), ("t", k0), ("t", v0), ("w", sums0), ("w", rests[0])]
-        + norm + [("w", up_all), ("w", branch_bias), ("w", firsts[1]), ("w", pair_all)],
-        [("t", (rows, d), bf16), ("b", (own_blocks, blocks, 2 * SPAN), f32), ("t", (rows, d), f32),
-         ("t", (rows, ff), bf16), ("t", (rows, ff), bf16), ("t", (rows, d), f32)] + triple,
-        [flat],
-    )
-    sums1 = share_sums(sums1, 2)
+    if not direct:
+        q0, k0, v0, sums0 = run(
+            start_kernel, 0, "start",
+            [("t", inputs), ("w", firsts[0])] + norm + [("w", pair_all)],
+            triple, [],
+        )
+        sums0 = share_sums(sums0, 2)
+        att0, log0, middle0, act0, slope0, x1, q1, k1, v1, sums1 = run(
+            forward_kernel, 0, "forward",
+            [("t", inputs), ("t", q0), ("t", k0), ("t", v0), ("w", sums0), ("w", rests[0])]
+            + norm + [("w", up_all), ("w", branch_bias), ("w", firsts[1]), ("w", pair_all)],
+            [("t", (rows, d), bf16), ("b", (own_blocks, blocks, 2 * SPAN), f32), ("t", (rows, d), f32),
+             ("t", (rows, ff), bf16), ("t", (rows, ff), bf16), ("t", (rows, d), f32)] + triple,
+            [flat],
+        )
+        sums1 = share_sums(sums1, 2)
     outputs, dmid1, dq1, dk1, dv1, dsum1, rest1, small1 = run(
         turn_kernel, 1, "turn",
         [("t", x1), ("t", q1), ("t", k1), ("t", v1), ("w", sums1), ("w", rests[1])]

time: 353 us -> 324 us (0.918)
  Pallas kernels: 335 us -> 307 us
    pallas_call x5 -> x3, Pallas kernels: 160 us -> 121 us  [call(): pl.pallas_call(kernel, name=name, grid=(steps,), in_specs=[spec(kind, arg...]
    pallas_call x3 -> x1, Pallas kernels: 88.4 us -> 99.7 us  [ascend(): pl.pallas_call(functools.partial(ascend_kernel, lines, groups, steps), na...]
where the time goes in v3:
time: 324 us
  Pallas kernels  307 us (95%)
  local copies, waits for them, and re-layouts  16.5 us (5%)
    pallas_call x3, Pallas kernels, call(): pl.pallas_call(kernel, name=name, grid=(steps,), in_specs=[spec(kind, arg...  121 us
    pallas_call x1, Pallas kernels, ascend(): pl.pallas_call(functools.partial(ascend_kernel, lines, groups, steps), na...  99.7 us
    pallas_call x1, Pallas kernels, reduce_all(): pl.pallas_call(functools.partial(reduce_kernel, lines), name='reduce', in...  72 us
    unnamed x11, local copies, waits for them, and re-layouts  16.5 us
    pallas_call x2, Pallas kernels, return_sums(): pl.pallas_call(functools.partial(return_kernel, groups), name='return', i...  14.2 us

profile of v3, /device:TPU:0, one launch (start us, length us, event | category | flops | bytes accessed | tf_op | source)
XLA Modules:
  0.0 323.7 jit_solution(11314306007499812955)
XLA Ops:
  0.6 1.5 copy.22.out_w_ref
  2.1 1.7 copy.23.down_ref
  3.9 99.7 %ascend.1 = (bf16[1536,512]{1,0:T(8,128)(2,1)}, bf16[1536,512]{1,0:T(8,128)(2,1)}, bf16[1536,512]{1,0:T(8,128)(2,1)}, f32[48,1024]{1,0:T(8,128)}, bf16[1536,512]...) custom-call(bf16[1536,512]{1,0:T(8,128)(2,1)} %x_ref.3, ...), custom_call_target="tpu_custom_call" | custom-call | tf_op jit(solution)/shard_map/ascend/pallas_call | solution.py:975
  103.6 58.0 %turn.1 = (bf16[1536,512]{1,0:T(8,128)(2,1)}, f32[1536,512]{1,0:T(8,128)}, bf16[1536,512]{1,0:T(8,128)(2,1)}, f32[1536,512]{1,0:T(8,128)}, f32[1536,512]{1,0:T(8...) custom-call(f32[1536,512]{1,0:T(8,128)} %get-tuple-element.59.x_ref, ...), custom_call_target="tpu_custom_call" | custom-call | tf_op jit(solution)/shard_map/turn/pallas_call | solution.py:483
  161.5 6.8 %return.2.dsum_in = f32[6,2,1024]{2,1,0:T(2,128)} custom-call(f32[4,12,1024]{2,1,0:T(8,128)} %get-tuple-element.71.dsum_ref), custom_call_target="tpu_custom_call" | custom-call | tf_op jit(solution)/shard_map/return/pallas_call | solution.py:1063
  168.4 49.3 %backward.1 = (bf16[4,3,512,128]{3,2,1,0:T(8,128)(2,1)}, f32[4,8,512]{2,1,0:T(8,128)}, f32[1536,512]{1,0:T(8,128)}, bf16[1536,512]{1,0:T(8,128)(2,1)}, f32[1536,...) custom-call(f32[1536,512]{1,0:T(8,128)} %get-tuple-element.59.x_ref,, ...), custom_call_target="tpu_custom_call" | custom-call | tf_op jit(solution)/shard_map/backward/pallas_call | solution.py:483
  217.7 7.4 %return.3.dsum_in = f32[6,2,1024]{2,1,0:T(2,128)} custom-call(f32[4,12,1024]{2,1,0:T(8,128)} %get-tuple-element.87.dsum_ref), custom_call_target="tpu_custom_call" | custom-call | tf_op jit(solution)/shard_map/return/pallas_call | solution.py:1063
  225.1 13.3 %finish.1 = (f32[1536,512]{1,0:T(8,128)}, bf16[4,3,512,128]{3,2,1,0:T(8,128)(2,1)}, f32[4,8,512]{2,1,0:T(8,128)}) custom-call(bf16[1536,512]{1,0:T(8,128)(2,1)} %x_ref.3, f32[1536,512]{1,0:T(8,128)} %get-tuple-element.83.dmid_in, bf16[1536,512]{1,0:T(8,128)(2,1)} %get-tuple-element.84.dq_in, f32[1536,512]{1,0:T(8,128)} %get-tuple-element.85.dk_in, ...), custom_call_target="tpu_custom_call" | custom-call | tf_op jit(solution)/shard_map/finish/pallas_call | solution.py:483
  238.5 72.0 %reduce.1 = (f32[2,3,64,128]{3,2,1,0:T(8,128)}, f32[2,128,64]{2,1,0:T(8,128)}, f32[2,64,512]{2,1,0:T(8,128)}, f32[2,512,64]{2,1,0:T(8,128)}, f32[2,2,512]{2,1,0:...) custom-call(bf16[4,3,512,128]{3,2,1,0:T(8,128)(2,1)} %get-tuple-element.90.firs, ...), custom_call_target="tpu_custom_call" | custom-call | tf_op jit(solution)/shard_map/reduce/pallas_call | solution.py:1346
  310.4 1.6 copy.24
  312.1 1.9 copy.25
  314.0 1.6 copy.33
  315.6 1.7 copy.34
  317.3 1.3 copy.35
  318.6 1.3 copy.36
  319.9 1.2 copy.37
  321.1 1.3 copy.38
  322.4 1.3 copy.39

commit v4 on v3

--- a/solution.py
+++ b/solution.py
@@ -53,8 +53,12 @@
     return jnp.sum(rows.reshape(-1, 8, rows.shape[1]), 0)
 
 
+def block(ref, j, at):
+    return ref[j, at].reshape(-1, LANES)
+
+
 def lane_blocks(ref, blocks, at):
-    return jnp.concatenate([ref[j, at] for j in range(blocks)], 1)
+    return jnp.concatenate([block(ref, j, at) for j in range(blocks)], 1)
 
 
 def gelu_pair(hidden):
@@ -149,7 +153,8 @@
 
 
 def attend_back_tile(
-    base, q_ref, k_ref, v_ref, sum_ref, datt_ref, att_ref, log_ref, dq_ref, dk_ref, dv_ref, dsum_ref
+    base, q_ref, k_ref, v_ref, sum_ref, datt_ref, att_ref, log_ref, dq_ref, dk_ref, dv_ref, dsum_ref,
+    tick=no_tick,
 ):
     width = q_ref.shape[1]
     masks = pair_masks()
@@ -177,6 +182,7 @@
             dv_ref[rows, lanes] = dv[:SPAN]
             dsum_ref[pl.ds(start, SEQ_BLOCKS), lanes] += dk[SPAN:]
             dsum_ref[pl.ds(start, SEQ_BLOCKS), value_lanes] += dv[SPAN:]
+        tick()
 
 
 def project_tile(rows, w_ref, gain, shift, bias, q_ref, k_ref, v_ref, sum_ref):
@@ -206,7 +212,7 @@
 
 
 def wide(ref, j, first, count):
-    return jnp.concatenate([ref[j, first + at] for at in range(count)], 1)
+    return jnp.concatenate([block(ref, j, first + at) for at in range(count)], 1)
 
 
 def mlp_tile(
@@ -234,7 +240,9 @@
         acc_ref[j, first + at] += value[:, at * LANES : (at + 1) * LANES]
 
 
-def mlp_back_tile(dy, middle, att, w_ref, gain, shift, act_ref, slope_ref, acc_ref, small_ref, datt_ref):
+def mlp_back_tile(
+    dy, middle, att, w_ref, gain, shift, act_ref, slope_ref, acc_ref, small_ref, datt_ref, tick=no_tick
+):
     blocks = w_ref.shape[0]
     count = (w_ref.shape[1] - 1) // 2
     span = count * LANES
@@ -253,6 +261,7 @@
         accumulate(acc_ref, j, 1, dot_nn(turned_in, grad_hidden))
         term = dot_nt(grad_hidden, wide(w_ref, j, 1, count))
         grad_in = term if grad_in is None else grad_in + term
+        tick()
     small_ref[0] += row_sums(grad_in * unit)
     small_ref[1] += row_sums(grad_in)
     grad_middle = dy + normalized_back(grad_in, gain, unit, rate)
@@ -266,35 +275,81 @@
     return grad_middle
 
 
-def project_back_tile(
-    rows, grad_middle, dq_ref, dk_ref, dv_ref, dsum_ref, w_ref, gain, shift, acc_ref, small_ref
-):
-    blocks = w_ref.shape[0]
-    width = rows.shape[1]
-    unit, rate = normalized(rows)
-    turned = (unit * gain + shift).astype(bf16).T
-    count = rows.shape[0] // SPAN
-
-    def spread(ref, first):
-        parts = []
-        for at in range(count):
-            share = dsum_ref[0, pl.ds(at, 1), pl.ds(first, width)] * (1.0 / SPAN)
-            parts.append(ref[pl.ds(at * SPAN, SPAN), :] + share)
-        return jnp.concatenate(parts, 0).astype(bf16)
-
-    grads = (dq_ref[...], spread(dk_ref, 0), spread(dv_ref, width))
+def spread_share(ref, share, first):
+    width = ref.shape[1]
+    parts = []
+    for at in range(ref.shape[0] // SPAN):
+        part = share[at : at + 1, first : first + width] * (1.0 / SPAN)
+        parts.append(ref[pl.ds(at * SPAN, SPAN), :] + part)
+    return jnp.concatenate(parts, 0).astype(bf16)
+
+
+def project_grads(turned, grads, acc_ref, small_ref):
+    for at, grad in enumerate(grads):
+        piece_grad = dot_nn(turned, grad)
+        for j in range(acc_ref.shape[0]):
+            acc_ref[j, at] += piece_grad[:, j * LANES : (j + 1) * LANES]
+    small_ref[2] += row_sums(grads[0].astype(f32))
+    small_ref[3] += row_sums(grads[2].astype(f32))
+
+
+def project_input(grads, unit, rate, grad_middle, w_ref, gain, small_ref):
     grad_in = None
     for at, grad in enumerate(grads):
-        piece = dot_nn(turned, grad)
-        for j in range(blocks):
-            acc_ref[j, at] += piece[:, j * LANES : (j + 1) * LANES]
-        term = dot_nt(grad, lane_blocks(w_ref, blocks, at))
+        term = dot_nt(grad, lane_blocks(w_ref, w_ref.shape[0], at))
         grad_in = term if grad_in is None else grad_in + term
     small_ref[0] += row_sums(grad_in * unit)
     small_ref[1] += row_sums(grad_in)
-    small_ref[2] += row_sums(grads[0].astype(f32))
-    small_ref[3] += row_sums(grads[2].astype(f32))
     return grad_middle + normalized_back(grad_in, gain, unit, rate)
+
+
+def project_back_tile(
+    rows, grad_middle, dq_ref, dk_ref, dv_ref, share, w_ref, gain, shift, acc_ref, small_ref
+):
+    unit, rate = normalized(rows)
+    turned = (unit * gain + shift).astype(bf16).T
+    grads = (dq_ref[...], spread_share(dk_ref, share, 0), spread_share(dv_ref, share, rows.shape[1]))
+    project_grads(turned, grads, acc_ref, small_ref)
+    return project_input(grads, unit, rate, grad_middle, w_ref, gain, small_ref)
+
+
+class Shares:
+    def __init__(self, slabs, landed, send_sem, recv_sem):
+        self.slabs, self.landed = slabs, landed
+        self.send_sem, self.recv_sem = send_sem, recv_sem
+        self.groups = slabs.shape[0]
+        self.spot, self.j = lax.axis_index("dp"), lax.axis_index("tensor")
+
+    def copy(self, d):
+        to = lax.rem(self.j + d, self.groups)
+        return pltpu.make_async_remote_copy(
+            src_ref=self.slabs.at[to],
+            dst_ref=self.landed.at[d - 1],
+            send_sem=self.send_sem.at[d - 1],
+            recv_sem=self.recv_sem.at[d - 1],
+            device_id=(self.spot, to),
+            device_id_type=pl.DeviceIdType.MESH,
+        )
+
+    def send(self):
+        for d in range(1, self.groups):
+            self.copy(d).start()
+
+    def receive(self):
+        total = self.slabs[self.j]
+        for d in range(1, self.groups):
+            self.copy(d).wait()
+            total = total + self.landed[d - 1]
+        return total
+
+    @staticmethod
+    def scratch(groups, blocks, width):
+        return [
+            pltpu.VMEM((groups, blocks, width), f32),
+            pltpu.VMEM((groups - 1, blocks, width), f32),
+            pltpu.SemaphoreType.DMA((groups - 1,)),
+            pltpu.SemaphoreType.DMA((groups - 1,)),
+        ]
 
 
 def first_block(tile):
@@ -380,11 +435,16 @@
 def turn_kernel(
     l, x_ref, q_in, k_in, v_in, sums_all, w_ref, gain_ref, shift_ref, bias_up, branch_bias, dy_ref,
     out_ref, dmid_ref, dq_ref, dk_ref, dv_ref, dsum_ref, grad_ref, small_ref,
-    att_ref, log_ref, act_ref, slope_ref, datt_ref, acc_ref, sums, dsums,
+    att_ref, log_ref, act_ref, slope_ref, datt_ref, acc_ref, sums, dsums, *exchange,
 ):
     lay_out(sums_all, sums)
     base = first_block(x_ref.shape[0])
     zero_first(acc_ref, dsums, small_ref)
+    if exchange:
+
+        @pl.when(pl.program_id(0) == 0)
+        def _():
+            greet(group_peers(lax.axis_size("tensor")))
     attend_tile(base, q_in, k_in, v_in, sums, att_ref, log_ref)
     middle = middle_of(x_ref[...], att_ref[...], w_ref, vector(branch_bias, l, 0))
     gain, shift = vector(gain_ref, l, 1), vector(shift_ref, l, 1)
@@ -402,8 +462,15 @@
 
     @on_last
     def _():
+        if not exchange:
+            store_sums(dsums, dsum_ref)
+        else:
+            traffic = Shares(*exchange)
+            store_sums(dsums, exchange[0])
+            traffic.send()
         store_grads((acc_ref, grad_ref))
-        store_sums(dsums, dsum_ref)
+        if exchange:
+            dsum_ref[...] = traffic.receive()
 
 
 def backward_kernel(
@@ -416,7 +483,7 @@
     base = first_block(x_ref.shape[0])
     zero_first(high_acc, acc_ref, dsums, small_ref, high_small)
     dy = project_back_tile(
-        x_ref[...], dmid_in[...], dq_in, dk_in, dv_in, dsum_in, w_ref, vector(gain_ref, l + 1, 0),
+        x_ref[...], dmid_in[...], dq_in, dk_in, dv_in, dsum_in[0], w_ref, vector(gain_ref, l + 1, 0),
         vector(shift_ref, l + 1, 0), high_acc, high_small,
     )
     dmid_ref[...] = mlp_back_tile(
@@ -439,7 +506,7 @@
 ):
     zero_first(acc_ref, small_ref)
     dx_ref[...] = project_back_tile(
-        x_ref[...].astype(f32), dmid_in[...], dq_in, dk_in, dv_in, dsum_in, w_ref,
+        x_ref[...].astype(f32), dmid_in[...], dq_in, dk_in, dv_in, dsum_in[0], w_ref,
         vector(gain_ref, l, 0), vector(shift_ref, l, 0), acc_ref, small_ref,
     )
 
@@ -476,7 +543,7 @@
     return stepped(array_like, tile // SPAN)
 
 
-def call(kernel, name, tile, steps, ins, outs, scratch=()):
+def call(kernel, name, tile, steps, ins, outs, scratch=(), number=None):
     kinds = [kind for kind, _ in ins]
     args = [arg for _, arg in ins]
     shapes = [jax.ShapeDtypeStruct(shape, dtype) for _, shape, dtype in outs]
@@ -489,7 +556,10 @@
         out_shape=shapes,
         scratch_shapes=list(scratch),
         compiler_params=pltpu.CompilerParams(
-            dimension_semantics=("arbitrary",), vmem_limit_bytes=VMEM_LIMIT
+            dimension_semantics=("arbitrary",),
+            vmem_limit_bytes=VMEM_LIMIT,
+            collective_id=number,
+            has_side_effects=number is not None,
         ),
     )(*args)
 
@@ -556,6 +626,13 @@
 
 def device(line, core, j):
     return (2 * line + core, j)
+
+
+def when_any(condition, act):
+    if condition is None:
+        act()
+    else:
+        pl.when(condition)(act)
 
 
 class Copies:
@@ -577,18 +654,23 @@
             device_id_type=pl.DeviceIdType.MESH,
         )
 
-    def send(self, key, source, target, where, like=None):
-        self.describe(key, source, target, where).start()
-        self.sent.append((key, like or (lambda: target)))
+    def send(self, key, source, target, where, like=None, condition=None):
+        view = target() if callable(target) else target
+        self.describe(key, source, view, where).start()
+        self.sent.append((key, like or target, condition))
 
     def receive(self, key, target, where):
         self.describe(key, target, target, where).wait_recv()
 
     def finish(self):
         line, core, j = place()
-        for key, like in self.sent:
-            view = like()
-            self.describe(key, view, view, device(line, 1 - core, j)).wait_send()
+        for key, like, condition in self.sent:
+
+            def wait(key=key, like=like):
+                view = like()
+                self.describe(key, view, view, device(line, 1 - core, j)).wait_send()
+
+            when_any(None if condition is None else condition(), wait)
         self.sent = []
 
 
@@ -607,85 +689,142 @@
     return peers
 
 
-def piece(ref, j, line, core, half=None):
-    share = ref.shape[2] // lax.axis_size("dp")
-    first = (2 * line + core) * share
-    if half is None:
-        return ref.at[j, :, pl.ds(pl.multiple_of(first, share), share), :]
-    small = share // 2
-    return ref.at[j, :, pl.ds(pl.multiple_of(first + half * small, small), small), :]
-
-
 class Gather:
-    def __init__(self, name, ref, copies, lines):
-        self.name, self.ref, self.copies, self.lines = name, ref, copies, lines
+    def __init__(self, name, ref, copies):
+        self.name, self.ref, self.copies = name, ref, copies
+        self.lines, self.half = ref.shape[2], ref.shape[4] // 2
         self.line, self.core, self.j = place()
         self.low, self.high = flip_low(self.j), flip_high(self.j)
         self.far = flip_high(self.low)
-
-    def key(self, *parts):
-        return (self.name,) + parts
-
-    def move(self, key, view, where, half=False):
-        share = self.ref.shape[2] // (2 * self.lines)
-        size = share // 2 if half else share
-        self.copies.send(
-            self.key(*key), view, view, where, lambda: self.ref.at[0, :, pl.ds(0, size), :]
-        )
-
-    def source_line(self, d):
-        return lax.rem(self.line + self.lines - d, self.lines)
-
-    def out(self, d, view):
-        self.move(("low", d), view, device(self.line, self.core, self.low))
-        self.move(("high", d), view, device(self.line, self.core, self.high))
-        self.partner(("own", d), view)
-
-    def partner(self, key, view, half=False):
-        self.move(("partner",) + key, view, device(self.line, 1 - self.core, self.j), half)
-
-    def view(self, column, d, half=None, core=None):
+        count = ref.shape[1]
+        self.ahead, self.behind = pl.ds(0, count - count // 3), pl.ds(count - count // 3, count // 3)
+        self.to_low = device(self.line, self.core, self.low)
+        self.to_high = device(self.line, self.core, self.high)
+        self.to_partner = device(self.line, 1 - self.core, self.j)
+        self.lines_at = [lax.rem(self.line + d, self.lines) for d in range(self.lines)]
+
+    def rows(self, upper):
+        return pl.ds(0 if upper else self.half, self.half)
+
+    def move(self, key, view, where, like):
+        self.copies.send((self.name,) + key, view, view, where, like)
+
+    def receive(self, key, view):
+        self.copies.receive((self.name,) + key, view, self.to_partner)
+
+    def own(self, d):
+        return self.ref.at[self.j, self.ahead, self.lines_at[d % self.lines], self.core]
+
+    def own_like(self):
+        return self.ref.at[0, self.ahead, 0, 0]
+
+    def slab(self, d, core=None):
         core = self.core if core is None else core
-        return piece(self.ref, column, self.source_line(d), core, half)
-
-    def receive(self, key, view):
-        self.copies.receive(self.key(*key), view, device(self.line, 1 - self.core, self.j))
+        return self.ref.at[:, self.behind, self.lines_at[d % self.lines], core]
+
+    def slab_like(self):
+        return self.ref.at[:, self.behind, 0, 0]
+
+    def half_slab(self, d, upper):
+        return self.ref.at[:, self.behind, self.lines_at[d % self.lines], self.core, self.rows(upper), :]
+
+    def half_slab_like(self):
+        return self.ref.at[:, self.behind, 0, 0, pl.ds(0, self.half), :]
+
+    def column(self, j, upper, core=None):
+        core = self.core if core is None else core
+        return self.ref.at[j, self.ahead, :, core, self.rows(upper), :]
+
+    def column_like(self):
+        return self.ref.at[0, self.ahead, :, 0, pl.ds(0, self.half), :]
+
+    def part(self, j, upper):
+        return self.ref.at[j, self.behind, self.line, self.core, self.rows(upper), :]
+
+    def part_like(self):
+        return self.ref.at[0, self.behind, 0, 0, pl.ds(0, self.half), :]
+
+    def along(self, d):
+        return device(self.lines_at[d % self.lines], self.core, self.j)
+
+    def share(self, number, j, upper):
+        self.move(("share", number), self.column(j, upper), self.to_partner, self.column_like)
+
+    def share_slab(self, d):
+        self.move(("share slab", d), self.slab(d), self.to_partner, self.slab_like)
 
     def begin(self):
-        own = self.view(self.j, 0)
+        for number, upper, where in (
+            (0, True, self.to_low), (1, False, self.to_high),
+            (2, True, self.to_high), (3, False, self.to_low),
+        ):
+            self.move(("bits", number), self.part(self.j, upper), where, self.part_like)
         for d in range(1, self.lines):
-            self.move(("line", d), own, device(lax.rem(self.line + d, self.lines), self.core, self.j))
-        self.out(0, own)
-
-    def relay_line(self, d):
-        view = self.view(self.j, d)
-        self.receive(("line", d), view)
-        self.out(d, view)
-
-    def relay_bits(self, d):
-        for name, column, half, other, where in (
-            ("low", self.low, 0, "far_high", self.high),
-            ("high", self.high, 1, "far_low", self.low),
+            self.move(("line", d), self.own(0), self.along(d), self.own_like)
+
+    def spread(self):
+        self.receive(("bits", 0), self.part(self.low, True))
+        self.move(("bits", 4), self.part(self.low, True), self.to_high, self.part_like)
+        self.receive(("bits", 1), self.part(self.high, False))
+        self.move(("bits", 5), self.part(self.high, False), self.to_low, self.part_like)
+        for d in range(1, self.lines):
+            self.receive(("line", d), self.own(self.lines - d))
+        self.move(("low", 0), self.column(self.j, True), self.to_low, self.column_like)
+        self.move(("high", 0), self.column(self.j, False), self.to_high, self.column_like)
+        self.share(0, self.j, True)
+        self.share(1, self.j, False)
+
+    def spread_more(self):
+        self.move(("high", 1), self.column(self.j, True), self.to_high, self.column_like)
+        self.move(("low", 1), self.column(self.j, False), self.to_low, self.column_like)
+
+    def slab_begin(self):
+        for number, j, upper in (
+            (2, self.high, True), (3, self.low, False), (4, self.far, True), (5, self.far, False)
         ):
-            view = self.view(column, d)
-            self.receive((name, d), view)
-            half_view = self.view(column, d, half)
-            self.move((other, d), half_view, device(self.line, self.core, where), True)
-            self.partner((name, d), view)
-
-    def relay_far(self, d):
-        for name, half in (("far_high", 0), ("far_low", 1)):
-            view = self.view(self.far, d, half)
-            self.receive((name, d), view)
-            self.partner((name, d), view, True)
+            self.receive(("bits", number), self.part(j, upper))
+        self.move(("slab", 1), self.slab(0), self.along(1), self.slab_like)
+        self.move(("slab", -1), self.slab(0), self.along(-1), self.slab_like)
+        self.share_slab(0)
+
+    def cross(self):
+        self.receive(("low", 0), self.column(self.low, True))
+        self.move(("high", 2), self.column(self.low, True), self.to_high, self.column_like)
+        self.receive(("high", 0), self.column(self.high, False))
+        self.move(("low", 2), self.column(self.high, False), self.to_low, self.column_like)
+        self.share(2, self.low, True)
+        self.share(3, self.high, False)
+
+    def slab_relay(self):
+        self.receive(("slab", 1), self.slab(-1))
+        self.move(("half", 1), self.half_slab(-1, True), self.along(1), self.half_slab_like)
+        self.receive(("slab", -1), self.slab(1))
+        self.move(("half", -1), self.half_slab(1, False), self.along(-1), self.half_slab_like)
+        self.share_slab(1)
+        self.share_slab(3)
+
+    def tail(self):
+        for number, key, j, upper in (
+            (4, ("high", 1), self.high, True), (5, ("low", 1), self.low, False),
+            (6, ("high", 2), self.far, True), (7, ("low", 2), self.far, False),
+        ):
+            self.receive(key, self.column(j, upper))
+            self.share(number, j, upper)
+
+    def close(self):
+        self.receive(("half", 1), self.half_slab(2, True))
+        self.receive(("half", -1), self.half_slab(2, False))
+        self.share_slab(2)
 
     def collect(self):
+        other = 1 - self.core
+        for number, (j, upper) in enumerate(
+            ((self.j, True), (self.j, False), (self.low, True), (self.high, False),
+             (self.high, True), (self.low, False), (self.far, True), (self.far, False))
+        ):
+            self.receive(("share", number), self.column(j, upper, other))
         for d in range(self.lines):
-            for name, column in (("own", self.j), ("low", self.low), ("high", self.high)):
-                self.receive(("partner", name, d), self.view(column, d, None, 1 - self.core))
-            for name, half in (("far_high", 0), ("far_low", 1)):
-                view = self.view(self.far, d, half, 1 - self.core)
-                self.receive(("partner", name, d), view)
+            self.receive(("share slab", d), self.slab(d, other))
 
 
 GATHER_COPIES = 170
@@ -762,7 +901,7 @@
     q_out, k_out, v_out, sums0, att_ref, log_ref, middle_ref, act_ref, slope_ref, y_ref,
     q_ref, k_ref, v_ref, sums1, first0_out, rest0_out, first1_out, rest1_out, up_out,
     first0, rest0, first1, rest1, own_first, own_rest, q_all, k_all, v_all, sums0_in, sums1_in,
-    pair_all, up_all, send_sem, recv_sem, local_sem, sum_send, sum_recv,
+    pair_all, up_all, att_all, y_all, send_sem, recv_sem, local_sem, sum_send, sum_recv,
 ):
     line, core, j = place()
     low, high = flip_low(j), flip_high(j)
@@ -774,7 +913,7 @@
     copies = Copies(send_sem, recv_sem)
     firsts, rests = (first0, first1), (rest0, rest1)
     sections = [
-        Gather((name, l), refs[l], copies, lines)
+        Gather((name, l), refs[l], copies)
         for l in range(LAYERS)
         for name, refs in (("first", firsts), ("rest", rests))
     ]
@@ -783,12 +922,11 @@
         Sums(ref, sum_send.at[l], sum_recv.at[l], groups)
         for l, ref in enumerate((sums0_in, sums1_in))
     ]
-    relayed = range(1, lines), range(lines), range(lines)
 
     def store(l, at):
         source, target = ((own_first, firsts), (own_rest, rests))[at]
         return pltpu.make_async_copy(
-            source.at[l], piece(target[l], j, line, core), local_sem.at[2 * l + at]
+            source.at[l], target[l].at[j, :, line, core], local_sem.at[2 * l + at]
         )
 
     def keep(at):
@@ -818,14 +956,15 @@
             where = device(line, core, other)
             copies.send(("pair", at), pair_ref, pair_all.at[j], where, lambda: pair_ref)
             copies.send(("up", at), up_bias_ref, up_all.at[j], where, lambda: up_bias_ref)
-        for d in relayed[0]:
-            first_a.relay_line(d)
+        first_a.spread()
+        first_a.spread_more()
+        first_a.slab_begin()
+        first_a.cross()
+        first_a.slab_relay()
         store(0, 1).wait()
         rest_a.begin()
-        for d in relayed[1]:
-            first_a.relay_bits(d)
-        for d in relayed[2]:
-            first_a.relay_far(d)
+        first_a.tail()
+        first_a.close()
         for at, other in enumerate(others):
             where = device(line, core, other)
             copies.receive(("pair", at), pair_all.at[other], where)
@@ -833,11 +972,11 @@
         first_a.collect()
         keep(0).start()
 
-    def start_second():
+    def start_third():
         store(1, 0).wait()
         first_b.begin()
 
-    def start_third():
+    def start_last():
         store(1, 1).wait()
         rest_b.begin()
 
@@ -849,38 +988,28 @@
         first_b.collect()
         keep(2).start()
 
-    def step_of(kind, section, d):
-        return functools.partial(getattr(section, "relay_" + kind), d)
-
     actions = {}
 
     def at(when, *acts):
         actions.setdefault(when, []).extend(acts)
 
+    one, two, three, last = steps, 2 * steps, 3 * steps, 4 * steps - 1
     at((0, 0), begin)
-    at((1, 0), step_of("line", rest_a, 1))
-    at((2, 0), step_of("line", rest_a, 2), step_of("line", rest_a, 3))
-    at((3, 0), start_second)
-    at((4, 0), step_of("bits", rest_a, 0))
-    at((5, 0), step_of("bits", rest_a, 1))
-    last = 2 * steps - 1
-    one = steps
-    at((one, 0), step_of("bits", rest_a, 2), step_of("far", rest_a, 0))
-    at((one, 1), step_of("bits", rest_a, 3), step_of("far", rest_a, 1), step_of("line", first_b, 1),
-       step_of("line", first_b, 2), step_of("line", first_b, 3), start_third)
-    at((one, 2), step_of("far", rest_a, 2), step_of("far", rest_a, 3), rest_ready)
-    at((one, 3), step_of("bits", first_b, 0), step_of("bits", first_b, 1))
-    at((one, 4), step_of("bits", first_b, 2), step_of("bits", first_b, 3))
-    at((one, 5), step_of("far", first_b, 0), step_of("far", first_b, 1))
-    at((one, 6), step_of("far", first_b, 2), step_of("far", first_b, 3), first_ready,
-       step_of("line", rest_b, 1))
-    at((one + 1, 0), step_of("line", rest_b, 2))
-    at((one + 1, 1), step_of("line", rest_b, 3))
-    at((one + 1, 4), step_of("bits", rest_b, 0))
-    at((one + 2, 1), step_of("bits", rest_b, 1), step_of("far", rest_b, 0))
-    at((one + 2, 4), step_of("bits", rest_b, 2), step_of("far", rest_b, 1))
-    at((one + 3, 1), step_of("bits", rest_b, 3), step_of("far", rest_b, 2))
-    at((one + 3, 6), step_of("far", rest_b, 3))
+    at((1, 0), rest_a.spread)
+    at((3, 0), start_third)
+    at((one, 0), rest_a.spread_more, rest_a.slab_begin)
+    at((one, 1), rest_a.cross)
+    at((one + 3, 0), rest_a.slab_relay, start_last)
+    at((one + 4, 0), first_b.spread, first_b.spread_more)
+    at((two, 0), rest_a.tail, rest_a.close, first_b.slab_begin, rest_ready)
+    at((two + 1, 0), first_b.cross, first_b.slab_relay, rest_b.spread)
+    at((two + 1, 2), rest_b.spread_more, rest_b.slab_begin)
+    at((two + 2, 2), first_b.tail)
+    at((two + 3, 2), first_b.close, rest_b.cross)
+    at((two + 4, 0), rest_b.slab_relay)
+    at((three, 0), first_ready)
+    at((three + 3, 0), rest_b.tail)
+    at((three + 4, 0), rest_b.close)
 
     @pl.when(step < steps)
     def _():
@@ -894,10 +1023,12 @@
         )
         sum_copies[0].send(step)
 
-    @pl.when(step >= steps)
+    rows = pl.ds(pl.multiple_of(lax.rem(step, steps) * tile, tile), tile)
+
+    @pl.when((step >= one) & (step < two))
     def _():
-        agenda = Agenda({key: acts for key, acts in actions.items() if key[0] >= steps})
-        now = step - steps
+        agenda = Agenda({key: acts for key, acts in actions.items() if one <= key[0] < two})
+        now = step - one
 
         def arrive():
             for at in (4, 5, 6):
@@ -905,23 +1036,35 @@
             sum_copies[0].receive()
             sum_copies[0].flatten(sums0)
 
-        when_step(steps, arrive)
         agenda.tick()
-        rows = pl.ds(pl.multiple_of(now * tile, tile), tile)
+        when_step(one, arrive)
         base = j * (steps * (tile // SPAN)) + now * (tile // SPAN)
         attend_tile(
             base, q_all.at[rows], k_all.at[rows], v_all.at[rows], sums0, att_ref, log_ref,
             agenda.tick,
         )
-        middle = middle_of(x_ref[...].astype(f32), att_ref[...], rest0, vector(branch_bias, 0, 0))
+        att_all[rows] = att_ref[...]
+
+    @pl.when((step >= two) & (step < three))
+    def _():
+        agenda = Agenda({key: acts for key, acts in actions.items() if two <= key[0] < three})
+        agenda.tick()
+        middle = middle_of(x_ref[...].astype(f32), att_all[rows], rest0, vector(branch_bias, 0, 0))
         middle_ref[...] = middle
         result = mlp_tile(
             middle, rest0, vector(gain_ref, 0, 1), vector(shift_ref, 0, 1), 0, up_all,
             vector(branch_bias, 0, 1), act_ref, slope_ref, agenda.tick,
         )
         y_ref[...] = result
+        y_all[rows] = result
+
+    @pl.when(step >= three)
+    def _():
+        agenda = Agenda({key: acts for key, acts in actions.items() if key[0] >= three})
+        now = step - three
+        agenda.tick()
         project_tile(
-            result, first1, vector(gain_ref, 1, 0), vector(shift_ref, 1, 0), pair_bias(pair_all, 1),
+            y_all[rows], first1, vector(gain_ref, 1, 0), vector(shift_ref, 1, 0), pair_bias(pair_all, 1),
             q_ref, k_ref, v_ref, sum_copies[1].own(now),
         )
         sum_copies[1].send(now)
@@ -952,21 +1095,26 @@
     share = d // (2 * lines)
     vmem = pl.BlockSpec(memory_space=pltpu.VMEM)
     hbm = pl.BlockSpec(memory_space=pl.ANY)
-    first = (groups, 3, d, LANES)
-    rest = (groups, 1 + 2 * count, d, LANES)
+    first = (groups, 3, lines, 2, share, LANES)
+    rest = (groups, 1 + 2 * count, lines, 2, share, LANES)
+
+    def attended(shape):
+        return clipped(steps, steps, shape)
 
     def late(shape):
-        return pl.BlockSpec(
-            shape, lambda i: (jnp.maximum(i - steps, 0),) + (0,) * (len(shape) - 1)
-        )
+        return clipped(steps, 2 * steps, shape)
+
+    def latest(shape):
+        return clipped(steps, 3 * steps, shape)
 
     def struct(shape, dtype):
         return jax.ShapeDtypeStruct(shape, dtype)
 
     flat = struct((blocks * groups, 2 * d), f32)
     out_specs = [hbm] * 3 + [vmem]
-    out_specs += [late((tile, d)), late((per_tile, groups, 2 * SPAN)), late((tile, d))]
-    out_specs += [late((tile, ff))] * 2 + [late((tile, d))] * 4 + [vmem] + [hbm] * 4 + [vmem]
+    out_specs += [attended((tile, d)), attended((per_tile, groups, 2 * SPAN)), late((tile, d))]
+    out_specs += [late((tile, ff))] * 2 + [late((tile, d))] + [latest((tile, d))] * 3
+    out_specs += [vmem] + [hbm] * 4 + [vmem]
     rows_bf16, rows_f32 = struct((rows, d), bf16), struct((rows, d), f32)
     outs = [rows_bf16] * 3 + [flat, rows_bf16, struct((blocks, groups, 2 * SPAN), f32), rows_f32]
     outs += [struct((rows, ff), bf16)] * 2 + [rows_f32] + [rows_bf16] * 3 + [flat]
@@ -975,7 +1123,7 @@
     return pl.pallas_call(
         functools.partial(ascend_kernel, lines, groups, steps),
         name="ascend",
-        grid=(2 * steps,),
+        grid=(4 * steps,),
         in_specs=[pl.BlockSpec((tile, d), lambda i: (lax.rem(i, steps), 0))] + [vmem] * 9,
         out_specs=out_specs,
         out_shape=outs,
@@ -989,6 +1137,8 @@
             pltpu.VMEM((groups, steps, per_tile, 2 * d), f32),
             pltpu.VMEM((groups,) + bias_qv.shape, f32),
             pltpu.VMEM((groups,) + bias_up.shape, f32),
+            pltpu.VMEM((rows, d), bf16),
+            pltpu.VMEM((rows, d), f32),
             pltpu.SemaphoreType.DMA((GATHER_COPIES,)),
             pltpu.SemaphoreType.DMA((GATHER_COPIES,)),
             pltpu.SemaphoreType.DMA((2 * LAYERS + 7,)),
@@ -1015,7 +1165,7 @@
     greet(peers)
     copies = Copies(send_sem, recv_sem)
     for d, peer in enumerate(peers):
-        copies.send(d, sums_ref, all_ref.at[j], peer)
+        copies.send(d, sums_ref, all_ref.at[j], peer, lambda: sums_ref)
     for d in range(1, groups):
         other = lax.rem(j + groups - d, groups)
         copies.receive(d - 1, all_ref.at[other], (spot, other))
@@ -1046,7 +1196,7 @@
     greet(peers)
     copies = Copies(send_sem, recv_sem)
     for d, peer in enumerate(peers):
-        copies.send(d, dsum_ref.at[peer[1]], landed.at[d], peer)
+        copies.send(d, dsum_ref.at[peer[1]], lambda d=d: landed.at[d], peer)
     for d in range(1, groups):
         copies.receive(d - 1, landed.at[d - 1], (spot, lax.rem(j + groups - d, groups)))
     total = dsum_ref[j]
@@ -1099,8 +1249,8 @@
     def begin(self):
         for line in range(self.lines):
             self.copies.send(
-                self.key("partner", line), self.rows_of(line, 1 - self.core), self.landed.at[line],
-                self.partner(),
+                self.key("partner", line), self.rows_of(line, 1 - self.core),
+                lambda line=line: self.landed.at[line], self.partner(),
             )
             self.fetch(line).start()
 
@@ -1127,13 +1277,13 @@
         upper, lower = pl.ds(0, half), pl.ds(half, half)
         for to, (column, rows) in enumerate(((self.low, upper), (self.far, upper))):
             self.copies.send(
-                self.key("low", to), self.own.at[:, column, :, rows, :], self.low_one.at[to],
-                device(self.line, self.core, self.low),
+                self.key("low", to), self.own.at[:, column, :, rows, :],
+                lambda to=to: self.low_one.at[to], device(self.line, self.core, self.low),
             )
         for to, (column, rows) in enumerate(((self.high, lower), (self.far, lower))):
             self.copies.send(
-                self.key("high", to), self.own.at[:, column, :, rows, :], self.high_one.at[to],
-                device(self.line, self.core, self.high),
+                self.key("high", to), self.own.at[:, column, :, rows, :],
+                lambda to=to: self.high_one.at[to], device(self.line, self.core, self.high),
             )
 
     def second_sum(self):
@@ -1157,11 +1307,11 @@
 
         lax.fori_loop(0, self.lines, add, 0)
         self.copies.send(
-            self.key("high_two"), self.low_one.at[1], self.high_two,
+            self.key("high_two"), self.low_one.at[1], lambda: self.high_two,
             device(self.line, self.core, self.high),
         )
         self.copies.send(
-            self.key("low_two"), self.high_one.at[1], self.low_two,
+            self.key("low_two"), self.high_one.at[1], lambda: self.low_two,
             device(self.line, self.core, self.low),
         )
 
@@ -1182,8 +1332,8 @@
         for d in range(1, self.lines):
             to = lax.rem(self.line + d, self.lines)
             self.copies.send(
-                self.key("line", d), self.line_sum.at[to], self.line_in.at[d - 1],
-                device(to, self.core, self.j),
+                self.key("line", d), self.line_sum.at[to],
+                lambda d=d: self.line_in.at[d - 1], device(to, self.core, self.j),
             )
 
     def result(self, at):
@@ -1230,17 +1380,19 @@
             for row in range(ref.shape[0]):
                 own[0, pl.ds(at, 1)] = jnp.sum(ref[row], 0, keepdims=True)
                 at += 1
-        copies.send(("small", 0), own.at[0], near.at[0], peers[0])
+        copies.send(("small", 0), own.at[0], lambda: near.at[0], peers[0])
     elif stage < 3:
         copies.receive(("small", stage - 1), near.at[stage - 1], peers[0])
         own[stage] = own[stage - 1] + near[stage - 1]
-        copies.send(("small", stage), own.at[stage], near.at[stage], peers[stage])
+        copies.send(("small", stage), own.at[stage], lambda: near.at[stage], peers[stage])
     elif stage == 3:
         copies.receive(("small", 2), near.at[2], peers[0])
         own[3] = own[2] + near[2]
         for d in range(1, lines):
             to = lax.rem(line + d, lines)
-            copies.send(("small", 2 + d), own.at[3], far.at[line], device(to, core, j))
+            copies.send(
+                ("small", 2 + d), own.at[3], far.at[line], device(to, core, j), lambda: own.at[3]
+            )
     else:
         for d in range(1, lines):
             source = lax.rem(line + lines - d, lines)
@@ -1252,108 +1404,399 @@
         return total
 
 
-def store_vectors(total, outs):
+def last_sums(small_ref, copies, lines, own, near, far, stage):
+    line, core, j = place()
+    groups = lax.axis_size("tensor")
+    me = core * groups + j
+    if stage == 0:
+        for row in range(small_ref.shape[0]):
+            own[0, pl.ds(row, 1)] = jnp.sum(small_ref[row], 0, keepdims=True)
+        near[me] = own[0]
+        for d in range(1, 2 * groups):
+            to = lax.rem(me + d, 2 * groups)
+            copies.send(
+                ("last", d), own.at[0], near.at[me], device(line, to // groups, lax.rem(to, groups)),
+                lambda: own.at[0],
+            )
+    elif stage == 1:
+        for d in range(1, 2 * groups):
+            source = lax.rem(me + 2 * groups - d, 2 * groups)
+            copies.receive(("last", d), near.at[source], device(line, 1 - core, j))
+        total = near[0]
+        for at in range(1, 2 * groups):
+            total = total + near[at]
+        own[1] = total
+        far[line] = total
+        for d in range(1, lines):
+            to = lax.rem(line + d, lines)
+            copies.send(
+                ("last line", d), own.at[1], far.at[line], device(to, core, j), lambda: own.at[1]
+            )
+    else:
+        for d in range(1, lines):
+            source = lax.rem(line + lines - d, lines)
+            copies.receive(("last line", d), far.at[source], device(line, 1 - core, j))
+        total = far[0]
+        for at in range(1, lines):
+            total = total + far[at]
+        return total
+
+
+def store_vectors(early, last, outs):
     gain_out, shift_out, pair_out, up_out, branch_out = outs
     j = lax.axis_index("tensor")
-    late = total.shape[0] // LAYERS - 4
     own = pl.ds(pl.multiple_of(j * LANES, LANES), LANES)
+    per_layer = (early.shape[0] - last.shape[0]) // LAYERS
     for l in range(LAYERS):
-        at = l * (total.shape[0] // LAYERS)
+        late = l * per_layer
+        first, base = (early, LAYERS * per_layer) if l else (last, 0)
+        gain_out[l, pl.ds(0, 1)] = first[pl.ds(base, 1)]
+        gain_out[l, pl.ds(1, 1)] = early[pl.ds(late, 1)]
+        shift_out[l, pl.ds(0, 1)] = first[pl.ds(base + 1, 1)]
+        shift_out[l, pl.ds(1, 1)] = early[pl.ds(late + 1, 1)]
         for row in range(2):
-            gain_out[l, pl.ds(row, 1)] = total[pl.ds(at + (1 - row) * late, 1)]
-            shift_out[l, pl.ds(row, 1)] = total[pl.ds(at + (1 - row) * late + 1, 1)]
-            branch_out[l, pl.ds(row, 1)] = total[pl.ds(at + 2 + row, 1)]
-            pair_out[l, pl.ds(row, 1)] = total[pl.ds(at + late + 2 + row, 1), own]
-        up_out[pl.ds(l, 1)] = total[pl.ds(at + 4 + j, 1)]
-
-
-def reduce_kernel(
-    lines, first0, first1, rest0, rest1, *refs,
+            branch_out[l, pl.ds(row, 1)] = early[pl.ds(late + 2 + row, 1)]
+            pair_out[l, pl.ds(row, 1)] = first[pl.ds(base + 2 + row, 1), own]
+        up_out[pl.ds(l, 1)] = early[pl.ds(late + 4 + j, 1)]
+
+
+def put_section(section, piece_ref):
+    section.end()
+    for at in range(section.blocks[1]):
+        piece_ref[at] = section.result(at)
+
+
+def make_sections(sources, copies, refs, lines):
+    sections = []
+    for name, source in sources:
+        for first in range(0, source.shape[1], SECTION):
+            at = BUFFERS * len(sections)
+            sections.append(
+                Reduce((name, first), source, (first, SECTION), copies, refs[at : at + BUFFERS], lines)
+            )
+    return sections
+
+
+def clipped(steps, first, shape):
+    zeros = (0,) * (len(shape) - 1)
+    return pl.BlockSpec(shape, lambda i: (jnp.clip(i - first, 0, steps - 1),) + zeros)
+
+
+def descend_kernel(
+    lines, steps, x_ref, dmid_in, dq_in, dk_in, dv_in, share_ref, high_w, low_w, gain_ref, shift_ref,
+    middle_ref, att_ref, act_ref, slope_ref, rest_in,
+    high_small, dmid_ref, datt_ref, grad_ref, small_ref, pieces,
+    dy_all, high_acc, acc_ref, high_grad, send_sem, recv_sem, *buffers,
 ):
-    smalls, refs = refs[:4], refs[4:]
-    (qkv_out, out_out, up_out, down_out), refs = refs[:4], refs[4:]
-    vector_outs, refs = refs[:5], refs[5:]
-    (small_own, small_near, small_far, small_total, send_sem, recv_sem), refs = refs[:6], refs[6:]
-    greet(near_peers(lines))
+    step = pl.program_id(0)
+    tile = x_ref.shape[0]
     copies = Copies(send_sem, recv_sem)
-    sections = []
-    for l, source in ((1, rest1), (1, first1), (0, rest0), (0, first0)):
-        for first in range(0, source.shape[1], SECTION):
-            at = len(sections)
-            sections.append(
-                (l, source.shape[1] == 3, first,
-                 Reduce((l, at), source, (first, SECTION), copies,
-                        refs[BUFFERS * at : BUFFERS * (at + 1)], lines))
-            )
-    count = up_out.shape[2] // LANES
-
-    def put(l, is_first, first, section):
-        section.end()
-        for at in range(SECTION):
-            value = section.result(at)
-            block = first + at
-            if is_first:
-                qkv_out[l, block] = value
-            elif block == 0:
-                out_out[l] = value.T
-            elif block <= count:
-                up_out[l, :, pl.ds((block - 1) * LANES, LANES)] = value
-            else:
-                down_out[l, pl.ds((block - 1 - count) * LANES, LANES), :] = value.T
+    sections = make_sections((("rest", rest_in), ("first", high_grad)), copies, buffers, lines)
+    high = sections[-1]
+    zero_first(high_acc, acc_ref, small_ref, high_small)
+
+    def begin():
+        greet(near_peers(lines))
+        for section in sections[:-1]:
+            section.begin()
+
+    def put(at):
+        return lambda: put_section(sections[at], pieces.at[at])
+
+    low = {}
+
+    def at(when, *acts):
+        low.setdefault(when, []).extend(acts)
+
+    one = steps
+    at((0, 0), begin)
+    at((1, 0), sections[0].first_sum)
+    at((2, 0), sections[1].first_sum)
+    at((3, 0), sections[2].first_sum)
+    at((5, 0), sections[0].second_sum)
+    at((one, 1), high.begin)
+    at((one, 2), sections[1].second_sum)
+    at((one, 4), high.first_sum, sections[0].third_sum)
+    at((one + 1, 2), sections[2].second_sum)
+    at((one + 2, 0), sections[1].third_sum)
+    at((one + 2, 2), high.second_sum)
+    at((one + 2, 4), put(0))
+    at((one + 3, 0), sections[2].third_sum)
+    at((one + 3, 2), put(1))
+    at((one + 3, 4), high.third_sum)
+    at((one + 4, 3), put(2))
+    at((one + 5, 2), put(3))
+
+    @pl.when(step < steps)
+    def _():
+        agenda = Agenda({key: acts for key, acts in low.items() if key[0] < one})
+        agenda.tick()
+        dy = project_back_tile(
+            x_ref[...], dmid_in[...], dq_in, dk_in, dv_in, share_ref[step], high_w,
+            vector(gain_ref, 1, 0), vector(shift_ref, 1, 0), high_acc, high_small,
+        )
+        dy_all[pl.ds(pl.multiple_of(step * tile, tile), tile)] = dy
+
+    @pl.when(step == steps - 1)
+    def _():
+        store_grads((high_acc, high_grad))
+
+    @pl.when(step >= steps)
+    def _():
+        agenda = Agenda({key: acts for key, acts in low.items() if key[0] >= one})
+        agenda.tick()
+        now = step - steps
+        dy = dy_all[pl.ds(pl.multiple_of(now * tile, tile), tile)]
+        dmid_ref[...] = mlp_back_tile(
+            dy, middle_ref[...], att_ref[...], low_w, vector(gain_ref, 0, 1),
+            vector(shift_ref, 0, 1), act_ref, slope_ref, acc_ref, small_ref, datt_ref, agenda.tick,
+        )
+
+    @pl.when(step == 2 * steps - 1)
+    def _():
+        store_grads((acc_ref, grad_ref))
+        copies.finish()
+
+
+def descend(x, back, share, high_w, low_w, ln_gain, ln_bias, saved, rest_grad, tile):
+    lines, groups = lax.axis_size("dp") // 2, lax.axis_size("tensor")
+    rows, d = x.shape
+    steps = rows // tile
+    width = d // (2 * lines)
+    vmem = pl.BlockSpec(memory_space=pltpu.VMEM)
+    hbm = pl.BlockSpec(memory_space=pl.ANY)
+    ff = saved[2].shape[1]
+
+    def early(columns):
+        return clipped(steps, 0, (tile, columns))
+
+    def late(columns):
+        return clipped(steps, steps, (tile, columns))
+
+    struct = jax.ShapeDtypeStruct
+    small = struct((4 + groups, 8, d), f32)
+    number = (rest_grad.shape[1] + high_w.shape[1]) // SECTION
+    scratch = [
+        pltpu.VMEM((rows, d), f32), pltpu.VMEM(high_w.shape, f32), pltpu.VMEM(low_w.shape, f32),
+        pltpu.VMEM(high_w.shape, bf16),
+        pltpu.SemaphoreType.DMA((REDUCE_COPIES,)), pltpu.SemaphoreType.DMA((REDUCE_COPIES,)),
+    ]
+    for _ in range(number):
+        scratch += Reduce.buffers(lines, groups, SECTION, width)
+    return pl.pallas_call(
+        functools.partial(descend_kernel, lines, steps),
+        name="descend",
+        grid=(2 * steps,),
+        in_specs=[early(d)] * 5 + [vmem] * 5 + [late(d)] * 2 + [late(ff)] * 2 + [hbm],
+        out_specs=[vmem, late(d), late(d), vmem, vmem, vmem],
+        out_shape=[
+            struct((4, 8, d), f32), struct((rows, d), f32), struct((rows, d), bf16),
+            struct(low_w.shape, bf16), small, struct((number, SECTION, width, LANES), f32),
+        ],
+        scratch_shapes=scratch,
+        compiler_params=pltpu.CompilerParams(
+            dimension_semantics=("arbitrary",), collective_id=1, has_side_effects=True,
+            vmem_limit_bytes=VMEM_LIMIT,
+        ),
+    )(x, *back, share, high_w, low_w, ln_gain, ln_bias, *saved, rest_grad)
+
+
+def land_kernel(
+    lines, steps, x_ref, q_in, k_in, v_in, datt_ref, att_ref, log_ref, sums, dmid_ref, w_ref,
+    gain_ref, shift_ref, rest_in, small0, small1, first_small1,
+    dx_ref, pieces, small_total, last_total,
+    dq_all, dk_all, dv_all, dk_done, dv_done, dsums, slabs, landed, share_send, share_recv, shares,
+    acc_ref, grad_ref, first_small0, small_own, small_near, small_far, last_own, last_near, last_far,
+    send_sem, recv_sem, *buffers,
+):
+    step = pl.program_id(0)
+    tile, d = x_ref.shape
+    per_tile = tile // SPAN
+    j = lax.axis_index("tensor")
+    copies = Copies(send_sem, recv_sem)
+    sections = make_sections((("rest", rest_in), ("first", grad_ref)), copies, buffers, lines)
+    last = sections[-1]
+    traffic = Shares(slabs, landed, share_send, share_recv)
+    smalls = (small0, small1, first_small1)
+    zero_first(acc_ref, first_small0, dsums)
+
+    def begin():
+        line, core, _ = place()
+        far = flip_high(flip_low(j))
+        others = [device(line, 1 - core, at) for at in (flip_low(j), flip_high(j), far)]
+        greet(near_peers(lines) + [device(line, core, far)] + others)
+        for section in sections[:-1]:
+            section.begin()
+
+    def put(at):
+        return lambda: put_section(sections[at], pieces.at[at])
 
     def small(stage):
         return small_sums(smalls, copies, lines, small_own, small_near, small_far, stage)
 
-    for section in sections:
-        section[3].begin()
-    total = len(sections)
-    for at in range(total + 3):
-        if at < 5:
-            done = small(at)
-            if at == 4:
-                small_total[...] = done
-                store_vectors(small_total, vector_outs)
-        if at < total:
-            sections[at][3].first_sum()
-        if 1 <= at < total + 1:
-            sections[at - 1][3].second_sum()
-        if 2 <= at < total + 2:
-            sections[at - 2][3].third_sum()
-        if 3 <= at:
-            put(*sections[at - 3])
-    copies.finish()
-
-
-def reduce_all(firsts, rests, smalls, shapes):
+    def final(stage):
+        return last_sums(first_small0, copies, lines, last_own, last_near, last_far, stage)
+
+    def small_step(stage):
+        return functools.partial(small, stage)
+
+    def small_end():
+        small_total[...] = small(4)
+
+    plan = {}
+
+    def at(when, *acts):
+        plan.setdefault(when, []).extend(acts)
+
+    one, two = steps, 2 * steps
+    at((0, 0), begin)
+    at((0, 1), small_step(0))
+    at((1, 0), sections[0].first_sum)
+    at((1, 1), small_step(1), sections[1].first_sum)
+    at((2, 0), sections[2].first_sum)
+    at((3, 2), sections[0].second_sum)
+    at((5, 1), sections[1].second_sum)
+    at((one + 1, 0), sections[0].third_sum, sections[2].second_sum)
+    at((one + 1, 0), small_step(2))
+    at((one + 3, 0), sections[1].third_sum)
+    at((one + 3, 0), small_step(3))
+    at((one + 4, 0), put(0))
+    at((one + 5, 0), sections[2].third_sum)
+    at((two, 0), last.begin)
+    at((two + 1, 0), put(1))
+    at((two + 2, 0), last.first_sum)
+    at((two + 3, 0), put(2))
+    at((two + 4, 0), small_end)
+    rows = pl.ds(pl.multiple_of(lax.rem(step, steps) * tile, tile), tile)
+
+    @pl.when(step < steps)
+    def _():
+        agenda = Agenda({key: acts for key, acts in plan.items() if key[0] < one})
+        agenda.tick()
+        attend_back_tile(
+            (j * steps + step) * per_tile, q_in, k_in, v_in, sums, datt_ref, att_ref, log_ref,
+            dq_all.at[rows], dk_all.at[rows], dv_all.at[rows], dsums, agenda.tick,
+        )
+
+    @pl.when(step == steps - 1)
+    def _():
+        store_sums(dsums, slabs)
+        traffic.send()
+
+    @pl.when((step >= steps) & (step < two))
+    def _():
+        agenda = Agenda({key: acts for key, acts in plan.items() if one <= key[0] < two})
+        agenda.tick()
+
+        @pl.when(step == steps)
+        def _():
+            total = traffic.receive()
+            for at in range(steps):
+                shares[at] = total[at * per_tile : (at + 1) * per_tile]
+
+        share = shares[step - steps]
+        unit, _ = normalized(x_ref[...].astype(f32))
+        turned = (unit * vector(gain_ref, 0, 0) + vector(shift_ref, 0, 0)).astype(bf16).T
+        grad_keys = spread_share(dk_all.at[rows], share, 0)
+        grad_values = spread_share(dv_all.at[rows], share, d)
+        dk_done[rows] = grad_keys
+        dv_done[rows] = grad_values
+        project_grads(turned, (dq_all[rows], grad_keys, grad_values), acc_ref, first_small0)
+
+    @pl.when(step == two - 1)
+    def _():
+        store_grads((acc_ref, grad_ref))
+
+    @pl.when(step >= two)
+    def _():
+        agenda = Agenda({key: acts for key, acts in plan.items() if key[0] >= two})
+        agenda.tick()
+        unit, rate = normalized(x_ref[...].astype(f32))
+        dx_ref[...] = project_input(
+            (dq_all[rows], dk_done[rows], dv_done[rows]), unit, rate, dmid_ref[...], w_ref,
+            vector(gain_ref, 0, 0), first_small0,
+        )
+
+    @pl.when(step == 3 * steps - 1)
+    def _():
+        final(0)
+        last.second_sum()
+        final(1)
+        last.third_sum()
+        last_total[...] = final(2)
+        put(3)()
+        copies.finish()
+
+
+def land(inputs, saved, sums, dmid, w, ln_gain, ln_bias, rest_grad, smalls, tile):
     lines, groups = lax.axis_size("dp") // 2, lax.axis_size("tensor")
-    d = firsts[0].shape[2]
-    share = d // (2 * lines)
-    number = 2 * (firsts[0].shape[1] + rests[0].shape[1]) // SECTION
-    rows = sum(small.shape[0] for small in smalls)
-    width = smalls[0].shape[2]
+    rows, d = inputs.shape
+    steps = rows // tile
+    per_tile = tile // SPAN
+    blocks = rows // SPAN
+    width = d // (2 * lines)
     vmem = pl.BlockSpec(memory_space=pltpu.VMEM)
     hbm = pl.BlockSpec(memory_space=pl.ANY)
+    struct = jax.ShapeDtypeStruct
+    number = (rest_grad.shape[1] + w.shape[1]) // SECTION
+    count = sum(small.shape[0] for small in smalls)
     scratch = [
-        pltpu.VMEM((4, rows, width), f32),
-        pltpu.VMEM((3, rows, width), f32),
-        pltpu.VMEM((lines, rows, width), f32),
-        pltpu.VMEM((rows, width), f32),
-        pltpu.SemaphoreType.DMA((REDUCE_COPIES,)),
-        pltpu.SemaphoreType.DMA((REDUCE_COPIES,)),
+        pltpu.VMEM((rows, d), bf16), pltpu.VMEM((rows, d), f32), pltpu.VMEM((rows, d), f32),
+        pltpu.VMEM((rows, d), bf16), pltpu.VMEM((rows, d), bf16),
+        pltpu.VMEM((blocks * groups, 2 * d), f32),
+        *Shares.scratch(groups, blocks, 2 * d),
+        pltpu.VMEM((steps, per_tile, 2 * d), f32),
+        pltpu.VMEM(w.shape, f32), pltpu.VMEM(w.shape, bf16), pltpu.VMEM((4, 8, d), f32),
+        pltpu.VMEM((4, count, d), f32), pltpu.VMEM((3, count, d), f32), pltpu.VMEM((lines, count, d), f32),
+        pltpu.VMEM((2, 4, d), f32), pltpu.VMEM((2 * groups, 4, d), f32), pltpu.VMEM((lines, 4, d), f32),
+        pltpu.SemaphoreType.DMA((REDUCE_COPIES,)), pltpu.SemaphoreType.DMA((REDUCE_COPIES,)),
     ]
     for _ in range(number):
-        scratch += Reduce.buffers(lines, groups, SECTION, share)
+        scratch += Reduce.buffers(lines, groups, SECTION, width)
+    walk = pl.BlockSpec((tile, d), lambda i: (lax.rem(i, steps), 0))
+    early = clipped(steps, 0, (tile, d))
+    late = clipped(steps, 2 * steps, (tile, d))
+    log_spec = clipped(steps, 0, (per_tile,) + saved[-1].shape[1:])
     return pl.pallas_call(
-        functools.partial(reduce_kernel, lines),
-        name="reduce",
-        in_specs=[hbm] * 4 + [vmem] * len(smalls),
+        functools.partial(land_kernel, lines, steps),
+        name="land",
+        grid=(3 * steps,),
+        in_specs=[walk] + [early] * 5 + [log_spec, vmem, late] + [vmem] * 3 + [hbm] + [vmem] * 3,
+        out_specs=[late, vmem, vmem, vmem],
+        out_shape=[
+            struct((rows, d), f32), struct((number, SECTION, width, LANES), f32),
+            struct((count, d), f32), struct((4, d), f32),
+        ],
+        scratch_shapes=scratch,
+        compiler_params=pltpu.CompilerParams(
+            dimension_semantics=("arbitrary",), collective_id=3, has_side_effects=True,
+            vmem_limit_bytes=VMEM_LIMIT,
+        ),
+    )(inputs, *saved, sums, dmid, w, ln_gain, ln_bias, rest_grad, *smalls)
+
+
+def settle_kernel(low_pieces, high_pieces, early, last, qkv_out, out_out, up_out, down_out, *vector_outs):
+    count = up_out.shape[2] // LANES
+    for l, pieces in enumerate((low_pieces, high_pieces)):
+        blocks = [pieces[at // SECTION, at % SECTION] for at in range(pieces.shape[0] * SECTION)]
+        out_out[l] = blocks[0].T
+        for at in range(count):
+            up_out[l, :, pl.ds(at * LANES, LANES)] = blocks[1 + at]
+            down_out[l, pl.ds(at * LANES, LANES), :] = blocks[1 + count + at].T
+        for at in range(3):
+            qkv_out[l, at] = blocks[1 + 2 * count + at]
+    store_vectors(early, last, vector_outs)
+
+
+def settle(low_pieces, high_pieces, early, last, shapes):
+    vmem = pl.BlockSpec(memory_space=pltpu.VMEM)
+    return pl.pallas_call(
+        settle_kernel,
+        name="settle",
+        in_specs=[vmem] * 4,
         out_specs=[vmem] * len(shapes),
         out_shape=[jax.ShapeDtypeStruct(shape, f32) for shape in shapes],
-        scratch_shapes=scratch,
-        compiler_params=pltpu.CompilerParams(
-            collective_id=1, has_side_effects=True, vmem_limit_bytes=VMEM_LIMIT
-        ),
-    )(*firsts, *rests, *smalls)
+    )(low_pieces, high_pieces, early, last)
 
 
 def body(
@@ -1368,13 +1811,14 @@
     blocks = d // LANES
     ff = w_down.shape[1] * groups
     all_blocks = own_blocks * groups
-    direct = blocks == groups == 4
+    direct = blocks == groups == 4 and lax.axis_size("dp") == 8
     if direct:
         (q0, k0, v0, sums0, att0, log0, middle0, act0, slope0, x1, q1, k1, v1, sums1,
          first0, rest0, first1, rest1, up_all) = ascend(
             inputs, w_qkv, w_out, w_up, w_down, bias_qv, bias_up, ln_gain, ln_bias, branch_bias, tile
         )
-        firsts, rests = (first0, first1), (rest0, rest1)
+        firsts = [first.reshape(groups, 3, d, LANES) for first in (first0, first1)]
+        rests = [rest.reshape(groups, rest.shape[1], d, LANES) for rest in (rest0, rest1)]
     else:
         firsts, rests = zip(
             *(gather_weights(w_qkv[l], w_out[l], w_up[l], w_down[l]) for l in range(LAYERS))
@@ -1401,8 +1845,8 @@
     flat = pltpu.VMEM((all_blocks, 2 * d), f32)
     norm = [("w", ln_gain), ("w", ln_bias)]
 
-    def run(kernel, l, name, ins, outs, scratch):
-        return call(functools.partial(kernel, l), name, tile, steps, ins, outs, scratch)
+    def run(kernel, l, name, ins, outs, scratch, number=None):
+        return call(functools.partial(kernel, l), name, tile, steps, ins, outs, scratch, number)
 
     if not direct:
         q0, k0, v0, sums0 = run(
@@ -1420,14 +1864,29 @@
             [flat],
         )
         sums1 = share_sums(sums1, 2)
+    slab = ("w", (own_blocks, 2 * d), f32) if direct else back[4]
     outputs, dmid1, dq1, dk1, dv1, dsum1, rest1, small1 = run(
         turn_kernel, 1, "turn",
         [("t", x1), ("t", q1), ("t", k1), ("t", v1), ("w", sums1), ("w", rests[1])]
         + norm + [("w", up_all), ("w", branch_bias), ("t", cotangent)],
-        [("t", (rows, d), bf16)] + back,
+        [("t", (rows, d), bf16)] + back[:4] + [slab] + back[5:],
         [tile_bf16, pltpu.VMEM((per_tile, blocks, 2 * SPAN), f32), pltpu.VMEM((tile, ff), bf16),
-         pltpu.VMEM((tile, ff), bf16), tile_bf16, acc, flat, flat],
+         pltpu.VMEM((tile, ff), bf16), tile_bf16, acc, flat, flat]
+        + (Shares.scratch(groups, own_blocks, 2 * d) if direct else []),
+        2 if direct else None,
     )
+    like = (w_qkv.shape, w_out.shape, w_up.shape, w_down.shape, ln_gain.shape, ln_bias.shape,
+            bias_qv.shape, bias_up.shape, branch_bias.shape)
+    if direct:
+        small1_first, dmid0, datt0, rest0, small0, high_pieces = descend(
+            x1, (dmid1, dq1, dk1, dv1), dsum1.reshape(sums_shape), firsts[1], rests[0], ln_gain,
+            ln_bias, (middle0, att0, act0, slope0), rest1, tile,
+        )
+        dx, low_pieces, early, last = land(
+            inputs, (q0, k0, v0, datt0, att0, log0), sums0, dmid0, firsts[0], ln_gain, ln_bias, rest0,
+            (small0, small1, small1_first), tile,
+        )
+        return (outputs, dx, *settle(low_pieces, high_pieces, early, last, like))
     dsum1 = return_sums(dsum1, sums_shape, 3)
     first1, small1_first, dmid0, dq0, dk0, dv0, dsum0, rest0, small0 = run(
         backward_kernel, 0, "backward",
@@ -1446,11 +1905,6 @@
         [("t", (rows, d), f32)] + first_out,
         [first_acc],
     )
-    smalls = (small0, small0_first, small1, small1_first)
-    like = (w_qkv.shape, w_out.shape, w_up.shape, w_down.shape, ln_gain.shape, ln_bias.shape,
-            bias_qv.shape, bias_up.shape, branch_bias.shape)
-    if direct:
-        return (outputs, dx, *reduce_all((first0, first1), (rest0, rest1), smalls, like))
     weight_grads = [scatter_grads(first0, rest0), scatter_grads(first1, rest1)]
     joined = [jnp.stack([grads[at] for grads in weight_grads]) for at in range(4)]
     late = jnp.sum(jnp.stack([small0, small1]), 2)

time: 324 us -> 291 us (0.90)
  Pallas kernels: 307 us -> 277 us
  local copies, waits for them, and re-layouts: 16.5 us -> 12.6 us
    pallas_call x3 -> x1, Pallas kernels: 121 us -> 63.1 us  [call(): pl.pallas_call(kernel, name=name, grid=(steps,), in_specs=[spec(kind, arg...]
    pallas_call x3, Pallas kernels: 86.2 us -> 124 us  [the longest x1 67 us: land(): pl.pallas_call(functools.partial(land_kernel, lines, steps), name='land',...]
    pallas_call x1, Pallas kernels: 99.7 us -> 89.8 us  [ascend(): pl.pallas_call(functools.partial(ascend_kernel, lines, groups, steps), na...]
    unnamed x11 -> x8, local copies, waits for them, and re-layouts: 16.5 us -> 11.1 us
where the time goes in v4:
time: 291 us; the launch traced here: 290 us
  Pallas kernels  277 us (95%)
  local copies, waits for them, and re-layouts  12.6 us (4%)
    pallas_call x1, Pallas kernels, ascend(): pl.pallas_call(functools.partial(ascend_kernel, lines, groups, steps), na...  89.8 us
    pallas_call x1, Pallas kernels, land(): pl.pallas_call(functools.partial(land_kernel, lines, steps), name='land',...  67 us
    pallas_call x1, Pallas kernels, call(): pl.pallas_call(kernel, name=name, grid=(steps,), in_specs=[spec(kind, arg...  63.1 us
    pallas_call x1, Pallas kernels, descend(): pl.pallas_call(functools.partial(descend_kernel, lines, steps), name='des...  54.5 us
    unnamed x8, local copies, waits for them, and re-layouts  11.1 us

profile of v4, /device:TPU:0, one launch (start us, length us, event | category | flops | bytes accessed | tf_op | source)
XLA Modules:
  0.0 290.2 jit_solution(1571413432181443943)
XLA Ops:
  0.6 1.5 copy.22.out_w_ref
  2.1 1.7 copy.23.down_ref
  3.9 89.8 %ascend.1 = (bf16[1536,512]{1,0:T(8,128)(2,1)}, bf16[1536,512]{1,0:T(8,128)(2,1)}, bf16[1536,512]{1,0:T(8,128)(2,1)}, f32[48,1024]{1,0:T(8,128)}, bf16[1536,512]...) custom-call(bf16[1536,512]{1,0:T(8,128)(2,1)} %x_ref.3, ...), custom_call_target="tpu_custom_call" | custom-call | tf_op jit(solution)/shard_map/ascend/pallas_call | solution.py:1123
  93.7 63.1 %turn.1 = (bf16[1536,512]{1,0:T(8,128)(2,1)}, f32[1536,512]{1,0:T(8,128)}, bf16[1536,512]{1,0:T(8,128)(2,1)}, f32[1536,512]{1,0:T(8,128)}, f32[1536,512]{1,0:T(8...) custom-call(f32[1536,512]{1,0:T(8,128)} %get-tuple-element.57.x_ref, ...), custom_call_target="tpu_custom_call" | custom-call | tf_op jit(solution)/shard_map/turn/pallas_call | solution.py:550
  156.8 1.5 reshape.38.share_ref
  158.3 54.5 %descend.1 = (f32[4,8,512]{2,1,0:T(8,128)}, f32[1536,512]{1,0:T(8,128)}, bf16[1536,512]{1,0:T(8,128)(2,1)}, bf16[4,9,512,128]{3,2,1,0:T(8,128)(2,1)}, f32[8,8,512]{2,1,0:T(8,128)}, /*index=5*/f32[4,3,64,128]{3,2,1,0:T(8,128)}) custom-call(f32[1536,512]{1,0:T(8,128)} %get-tuple-element.57.x_ref, f32[1536,512]{1,0:T(8,128)} %get-tuple-element.68.dmid_in, ...), custom_call_target="tpu_custom_call" | custom-call | tf_op jit(solution)/shard_map/descend/pallas_call | solution.py:1586
  212.8 67.0 %land.1 = (f32[1536,512]{1,0:T(8,128)}, f32[4,3,64,128]{3,2,1,0:T(8,128)}, f32[20,512]{1,0:T(8,128)}, f32[4,512]{1,0:T(4,128)}) custom-call(bf16[1536,512]{1,0:T(8,128)(2,1)} %x_ref.3, bf16[1536,512]{1,0:T(8,128)(2,1)} %get-tuple-element.65.q_in, bf16[1536,512]{1,0:T(8,128)(2,1)} %get-tuple-element.66.k_in, bf16[1536,512]{1,0:T(8,128)(2,1)} %get-tuple-element.67.v_in, ...), custom_call_target="tpu_custom_call" | custom-call | tf_op jit(solution)/shard_map/land/pallas_call | solution.py:1760
  279.9 0.0 copy-start
  279.9 2.5 settle.1
  282.3 1.6 copy.24
  283.9 1.9 copy.25
  285.9 2.7 copy.28
  288.5 0.0 copy-done
  288.5 1.7 copy.29
Async XLA Ops:
  279.9 8.7 %copy-start = (f32[1536,512]{1,0:T(8,128)S(1)}, f32[1536,512]{1,0:T(8,128)}, u32[]{:S(2)}) copy-start(f32[1536,512]{1,0:T(8,128)} %get-tuple-element.126) | copy-start | bytes 9437188

commit v5 on v4

--- a/solution.py
+++ b/solution.py
@@ -433,19 +433,17 @@
 
 
 def turn_kernel(
-    l, x_ref, q_in, k_in, v_in, sums_all, w_ref, gain_ref, shift_ref, bias_up, branch_bias, dy_ref,
+    l, x_ref, q_in, k_in, v_in, sums_all, w_in, gain_ref, shift_ref, bias_up, branch_bias, dy_ref,
     out_ref, dmid_ref, dq_ref, dk_ref, dv_ref, dsum_ref, grad_ref, small_ref,
-    att_ref, log_ref, act_ref, slope_ref, datt_ref, acc_ref, sums, dsums, *exchange,
+    att_ref, log_ref, act_ref, slope_ref, datt_ref, acc_ref, sums, dsums, w_ref, w_sem,
 ):
+    load = pltpu.make_async_copy(w_in, w_ref, w_sem)
+    when_step(0, load.start)
     lay_out(sums_all, sums)
     base = first_block(x_ref.shape[0])
     zero_first(acc_ref, dsums, small_ref)
-    if exchange:
-
-        @pl.when(pl.program_id(0) == 0)
-        def _():
-            greet(group_peers(lax.axis_size("tensor")))
     attend_tile(base, q_in, k_in, v_in, sums, att_ref, log_ref)
+    when_step(0, load.wait)
     middle = middle_of(x_ref[...], att_ref[...], w_ref, vector(branch_bias, l, 0))
     gain, shift = vector(gain_ref, l, 1), vector(shift_ref, l, 1)
     result = mlp_tile(
@@ -462,15 +460,8 @@
 
     @on_last
     def _():
-        if not exchange:
-            store_sums(dsums, dsum_ref)
-        else:
-            traffic = Shares(*exchange)
-            store_sums(dsums, exchange[0])
-            traffic.send()
         store_grads((acc_ref, grad_ref))
-        if exchange:
-            dsum_ref[...] = traffic.receive()
+        store_sums(dsums, dsum_ref)
 
 
 def backward_kernel(
@@ -538,6 +529,8 @@
         return tiled(array_like, tile)
     if kind == "w":
         return whole(array_like)
+    if kind == "h":
+        return pl.BlockSpec(memory_space=pl.ANY)
     if kind == "s":
         return stepped(array_like, 1)
     return stepped(array_like, tile // SPAN)
@@ -674,11 +667,19 @@
         self.sent = []
 
 
-def greet(peers):
+def greet_signal(peers):
     barrier = pltpu.get_barrier_semaphore()
     for peer in peers:
         pl.semaphore_signal(barrier, inc=1, device_id=peer, device_id_type=pl.DeviceIdType.MESH)
-    pl.semaphore_wait(barrier, len(peers))
+
+
+def greet_wait(peers):
+    pl.semaphore_wait(pltpu.get_barrier_semaphore(), len(peers))
+
+
+def greet(peers):
+    greet_signal(peers)
+    greet_wait(peers)
 
 
 def near_peers(lines):
@@ -900,7 +901,7 @@
     gain_ref, shift_ref, branch_bias,
     q_out, k_out, v_out, sums0, att_ref, log_ref, middle_ref, act_ref, slope_ref, y_ref,
     q_ref, k_ref, v_ref, sums1, first0_out, rest0_out, first1_out, rest1_out, up_out,
-    first0, rest0, first1, rest1, own_first, own_rest, q_all, k_all, v_all, sums0_in, sums1_in,
+    first0, rest0, first1, rest1, own_rest, q_all, k_all, v_all, sums0_in, sums1_in,
     pair_all, up_all, att_all, y_all, send_sem, recv_sem, local_sem, sum_send, sum_recv,
 ):
     line, core, j = place()
@@ -924,7 +925,7 @@
     ]
 
     def store(l, at):
-        source, target = ((own_first, firsts), (own_rest, rests))[at]
+        source, target = ((qkv_ref, firsts), (own_rest, rests))[at]
         return pltpu.make_async_copy(
             source.at[l], target[l].at[j, :, line, core], local_sem.at[2 * l + at]
         )
@@ -937,19 +938,21 @@
         return pltpu.make_async_copy(source, target, local_sem.at[2 * LAYERS + at])
 
     def begin():
-        greet(near_peers(lines) + [device(line, core, far)])
+        peers = near_peers(lines) + [device(line, core, far)]
+        greet_signal(peers)
+        store(0, 0).start()
         for l in range(LAYERS):
-            own_first[l] = qkv_ref[l]
-            own_rest[l, 0] = out_w_ref[l].T
-            turned = down_ref[l].T
+            own_rest[l, 0] = out_w_ref[l]
             for at in range(count):
-                own_rest[l, 1 + at] = up_ref[l, :, at * LANES : (at + 1) * LANES]
-                own_rest[l, 1 + count + at] = turned[:, at * LANES : (at + 1) * LANES]
-        for l in range(LAYERS):
-            store(l, 0).start()
-            store(l, 1).start()
+                part = slice(at * LANES, (at + 1) * LANES)
+                own_rest[l, 1 + at] = up_ref[l, :, part]
+                own_rest[l, 1 + count + at] = down_ref[l, :, part]
+        store(0, 1).start()
+        store(1, 0).start()
+        store(1, 1).start()
         pair_all[j] = pair_ref[...]
         up_all[j] = up_bias_ref[...]
+        greet_wait(peers)
         store(0, 0).wait()
         first_a.begin()
         for at, other in enumerate(others):
@@ -998,15 +1001,15 @@
     at((1, 0), rest_a.spread)
     at((3, 0), start_third)
     at((one, 0), rest_a.spread_more, rest_a.slab_begin)
-    at((one, 1), rest_a.cross)
+    at((one + 1, 0), rest_a.cross)
     at((one + 3, 0), rest_a.slab_relay, start_last)
     at((one + 4, 0), first_b.spread, first_b.spread_more)
     at((two, 0), rest_a.tail, rest_a.close, first_b.slab_begin, rest_ready)
-    at((two + 1, 0), first_b.cross, first_b.slab_relay, rest_b.spread)
-    at((two + 1, 2), rest_b.spread_more, rest_b.slab_begin)
-    at((two + 2, 2), first_b.tail)
-    at((two + 3, 2), first_b.close, rest_b.cross)
-    at((two + 4, 0), rest_b.slab_relay)
+    at((two + 1, 0), first_b.cross, rest_b.spread)
+    at((two + 1, 1), first_b.slab_relay, rest_b.spread_more, rest_b.slab_begin)
+    at((two + 2, 1), first_b.tail)
+    at((two + 3, 1), first_b.close, rest_b.cross)
+    at((two + 4, 1), rest_b.slab_relay)
     at((three, 0), first_ready)
     at((three + 3, 0), rest_b.tail)
     at((three + 4, 0), rest_b.close)
@@ -1040,10 +1043,10 @@
         when_step(one, arrive)
         base = j * (steps * (tile // SPAN)) + now * (tile // SPAN)
         attend_tile(
-            base, q_all.at[rows], k_all.at[rows], v_all.at[rows], sums0, att_ref, log_ref,
-            agenda.tick,
+            base, q_all.at[rows], k_all.at[rows], v_all.at[rows], sums0, att_ref, log_ref
         )
         att_all[rows] = att_ref[...]
+        agenda.tick()
 
     @pl.when((step >= two) & (step < three))
     def _():
@@ -1053,10 +1056,11 @@
         middle_ref[...] = middle
         result = mlp_tile(
             middle, rest0, vector(gain_ref, 0, 1), vector(shift_ref, 0, 1), 0, up_all,
-            vector(branch_bias, 0, 1), act_ref, slope_ref, agenda.tick,
+            vector(branch_bias, 0, 1), act_ref, slope_ref,
         )
         y_ref[...] = result
         y_all[rows] = result
+        agenda.tick()
 
     @pl.when(step >= three)
     def _():
@@ -1090,7 +1094,7 @@
     steps = rows // tile
     per_tile = tile // SPAN
     count = w_up.shape[2] // LANES
-    ff = w_down.shape[1] * groups
+    ff = w_down.shape[2] * groups
     blocks = rows // SPAN
     share = d // (2 * lines)
     vmem = pl.BlockSpec(memory_space=pltpu.VMEM)
@@ -1130,7 +1134,6 @@
         scratch_shapes=[
             pltpu.VMEM(first, bf16), pltpu.VMEM(rest, bf16),
             pltpu.VMEM(first, bf16), pltpu.VMEM(rest, bf16),
-            pltpu.VMEM((LAYERS, 3, share, LANES), bf16),
             pltpu.VMEM((LAYERS, 1 + 2 * count, share, LANES), bf16),
             pltpu.VMEM((rows, d), bf16), pltpu.VMEM((rows, d), bf16), pltpu.VMEM((rows, d), bf16),
             pltpu.VMEM((groups, steps, per_tile, 2 * d), f32),
@@ -1483,22 +1486,38 @@
 
 
 def descend_kernel(
-    lines, steps, x_ref, dmid_in, dq_in, dk_in, dv_in, share_ref, high_w, low_w, gain_ref, shift_ref,
+    lines, steps, x_ref, dmid_in, dq_in, dk_in, dv_in, slabs, high_in, low_in, gain_ref, shift_ref,
     middle_ref, att_ref, act_ref, slope_ref, rest_in,
     high_small, dmid_ref, datt_ref, grad_ref, small_ref, pieces,
-    dy_all, high_acc, acc_ref, high_grad, send_sem, recv_sem, *buffers,
+    dy_all, high_acc, acc_ref, high_grad, high_w, low_w, load_sem, shares, landed, share_send,
+    share_recv, send_sem, recv_sem, *buffers,
 ):
     step = pl.program_id(0)
     tile = x_ref.shape[0]
+    per_tile = tile // SPAN
+    traffic = Shares(slabs, landed, share_send, share_recv)
+    load_high = pltpu.make_async_copy(high_in, high_w, load_sem.at[0])
+    load_low = pltpu.make_async_copy(low_in, low_w, load_sem.at[1])
     copies = Copies(send_sem, recv_sem)
     sections = make_sections((("rest", rest_in), ("first", high_grad)), copies, buffers, lines)
     high = sections[-1]
-    zero_first(high_acc, acc_ref, small_ref, high_small)
 
     def begin():
-        greet(near_peers(lines))
+        line, core, j = place()
+        peers = near_peers(lines) + [device(line, core, flip_high(flip_low(j)))]
+        greet_signal(peers)
+        load_high.start()
+        load_low.start()
+        for ref in (high_acc, small_ref, high_small, acc_ref):
+            ref[...] = jnp.zeros_like(ref)
+        greet_wait(peers)
+        traffic.send()
         for section in sections[:-1]:
             section.begin()
+        load_high.wait()
+        total = traffic.receive()
+        for at in range(steps):
+            shares[at] = total[at * per_tile : (at + 1) * per_tile]
 
     def put(at):
         return lambda: put_section(sections[at], pieces.at[at])
@@ -1514,25 +1533,24 @@
     at((2, 0), sections[1].first_sum)
     at((3, 0), sections[2].first_sum)
     at((5, 0), sections[0].second_sum)
-    at((one, 1), high.begin)
-    at((one, 2), sections[1].second_sum)
-    at((one, 4), high.first_sum, sections[0].third_sum)
-    at((one + 1, 2), sections[2].second_sum)
+    at((one, 0), load_low.wait, high.begin)
+    at((one, 1), sections[1].second_sum)
+    at((one + 1, 0), high.first_sum, sections[0].third_sum)
+    at((one + 1, 1), sections[2].second_sum)
     at((one + 2, 0), sections[1].third_sum)
-    at((one + 2, 2), high.second_sum)
-    at((one + 2, 4), put(0))
+    at((one + 2, 1), high.second_sum, put(0))
     at((one + 3, 0), sections[2].third_sum)
-    at((one + 3, 2), put(1))
-    at((one + 3, 4), high.third_sum)
-    at((one + 4, 3), put(2))
-    at((one + 5, 2), put(3))
+    at((one + 3, 1), put(1))
+    at((one + 4, 0), high.third_sum)
+    at((one + 4, 1), put(2))
+    at((one + 5, 1), put(3))
 
     @pl.when(step < steps)
     def _():
         agenda = Agenda({key: acts for key, acts in low.items() if key[0] < one})
         agenda.tick()
         dy = project_back_tile(
-            x_ref[...], dmid_in[...], dq_in, dk_in, dv_in, share_ref[step], high_w,
+            x_ref[...], dmid_in[...], dq_in, dk_in, dv_in, shares[step], high_w,
             vector(gain_ref, 1, 0), vector(shift_ref, 1, 0), high_acc, high_small,
         )
         dy_all[pl.ds(pl.multiple_of(step * tile, tile), tile)] = dy
@@ -1549,8 +1567,9 @@
         dy = dy_all[pl.ds(pl.multiple_of(now * tile, tile), tile)]
         dmid_ref[...] = mlp_back_tile(
             dy, middle_ref[...], att_ref[...], low_w, vector(gain_ref, 0, 1),
-            vector(shift_ref, 0, 1), act_ref, slope_ref, acc_ref, small_ref, datt_ref, agenda.tick,
-        )
+            vector(shift_ref, 0, 1), act_ref, slope_ref, acc_ref, small_ref, datt_ref,
+        )
+        agenda.tick()
 
     @pl.when(step == 2 * steps - 1)
     def _():
@@ -1558,7 +1577,7 @@
         copies.finish()
 
 
-def descend(x, back, share, high_w, low_w, ln_gain, ln_bias, saved, rest_grad, tile):
+def descend(x, back, slabs, high_w, low_w, ln_gain, ln_bias, saved, rest_grad, tile):
     lines, groups = lax.axis_size("dp") // 2, lax.axis_size("tensor")
     rows, d = x.shape
     steps = rows // tile
@@ -1578,7 +1597,9 @@
     number = (rest_grad.shape[1] + high_w.shape[1]) // SECTION
     scratch = [
         pltpu.VMEM((rows, d), f32), pltpu.VMEM(high_w.shape, f32), pltpu.VMEM(low_w.shape, f32),
-        pltpu.VMEM(high_w.shape, bf16),
+        pltpu.VMEM(high_w.shape, bf16), pltpu.VMEM(high_w.shape, bf16), pltpu.VMEM(low_w.shape, bf16),
+        pltpu.SemaphoreType.DMA((2,)), pltpu.VMEM((steps, tile // SPAN, 2 * d), f32),
+        *Shares.scratch(groups, slabs.shape[1], 2 * d)[1:],
         pltpu.SemaphoreType.DMA((REDUCE_COPIES,)), pltpu.SemaphoreType.DMA((REDUCE_COPIES,)),
     ]
     for _ in range(number):
@@ -1587,7 +1608,7 @@
         functools.partial(descend_kernel, lines, steps),
         name="descend",
         grid=(2 * steps,),
-        in_specs=[early(d)] * 5 + [vmem] * 5 + [late(d)] * 2 + [late(ff)] * 2 + [hbm],
+        in_specs=[early(d)] * 5 + [vmem] + [hbm] * 2 + [vmem] * 2 + [late(d)] * 2 + [late(ff)] * 2 + [hbm],
         out_specs=[vmem, late(d), late(d), vmem, vmem, vmem],
         out_shape=[
             struct((4, 8, d), f32), struct((rows, d), f32), struct((rows, d), bf16),
@@ -1598,19 +1619,20 @@
             dimension_semantics=("arbitrary",), collective_id=1, has_side_effects=True,
             vmem_limit_bytes=VMEM_LIMIT,
         ),
-    )(x, *back, share, high_w, low_w, ln_gain, ln_bias, *saved, rest_grad)
+    )(x, *back, slabs, high_w, low_w, ln_gain, ln_bias, *saved, rest_grad)
 
 
 def land_kernel(
-    lines, steps, x_ref, q_in, k_in, v_in, datt_ref, att_ref, log_ref, sums, dmid_ref, w_ref,
+    lines, steps, x_ref, q_in, k_in, v_in, datt_ref, att_ref, log_ref, sums, dmid_ref, w_in,
     gain_ref, shift_ref, rest_in, small0, small1, first_small1,
     dx_ref, pieces, small_total, last_total,
     dq_all, dk_all, dv_all, dk_done, dv_done, dsums, slabs, landed, share_send, share_recv, shares,
     acc_ref, grad_ref, first_small0, small_own, small_near, small_far, last_own, last_near, last_far,
-    send_sem, recv_sem, *buffers,
+    w_ref, w_sem, send_sem, recv_sem, *buffers,
 ):
     step = pl.program_id(0)
     tile, d = x_ref.shape
+    load = pltpu.make_async_copy(w_in, w_ref, w_sem)
     per_tile = tile // SPAN
     j = lax.axis_index("tensor")
     copies = Copies(send_sem, recv_sem)
@@ -1618,13 +1640,17 @@
     last = sections[-1]
     traffic = Shares(slabs, landed, share_send, share_recv)
     smalls = (small0, small1, first_small1)
-    zero_first(acc_ref, first_small0, dsums)
 
     def begin():
         line, core, _ = place()
         far = flip_high(flip_low(j))
         others = [device(line, 1 - core, at) for at in (flip_low(j), flip_high(j), far)]
-        greet(near_peers(lines) + [device(line, core, far)] + others)
+        peers = near_peers(lines) + [device(line, core, far)] + others
+        greet_signal(peers)
+        load.start()
+        for ref in (acc_ref, first_small0, dsums):
+            ref[...] = jnp.zeros_like(ref)
+        greet_wait(peers)
         for section in sections[:-1]:
             section.begin()
 
@@ -1653,20 +1679,18 @@
     at((0, 1), small_step(0))
     at((1, 0), sections[0].first_sum)
     at((1, 1), small_step(1), sections[1].first_sum)
-    at((2, 0), sections[2].first_sum)
-    at((3, 2), sections[0].second_sum)
-    at((5, 1), sections[1].second_sum)
-    at((one + 1, 0), sections[0].third_sum, sections[2].second_sum)
-    at((one + 1, 0), small_step(2))
-    at((one + 3, 0), sections[1].third_sum)
-    at((one + 3, 0), small_step(3))
-    at((one + 4, 0), put(0))
-    at((one + 5, 0), sections[2].third_sum)
-    at((two, 0), last.begin)
-    at((two + 1, 0), put(1))
+    at((3, 1), sections[0].second_sum)
+    at((one, 0), sections[2].first_sum)
+    at((one + 1, 0), sections[1].second_sum, small_step(2))
+    at((one + 2, 0), sections[0].third_sum)
+    at((one + 4, 0), sections[2].second_sum, sections[1].third_sum)
+    at((one + 5, 0), small_step(3), put(0))
+    at((two, 0), last.begin, load.wait)
+    at((two + 1, 0), sections[2].third_sum)
     at((two + 2, 0), last.first_sum)
-    at((two + 3, 0), put(2))
+    at((two + 3, 0), put(1))
     at((two + 4, 0), small_end)
+    at((two + 5, 0), put(2))
     rows = pl.ds(pl.multiple_of(lax.rem(step, steps) * tile, tile), tile)
 
     @pl.when(step < steps)
@@ -1675,8 +1699,9 @@
         agenda.tick()
         attend_back_tile(
             (j * steps + step) * per_tile, q_in, k_in, v_in, sums, datt_ref, att_ref, log_ref,
-            dq_all.at[rows], dk_all.at[rows], dv_all.at[rows], dsums, agenda.tick,
-        )
+            dq_all.at[rows], dk_all.at[rows], dv_all.at[rows], dsums,
+        )
+        agenda.tick()
 
     @pl.when(step == steps - 1)
     def _():
@@ -1686,7 +1711,6 @@
     @pl.when((step >= steps) & (step < two))
     def _():
         agenda = Agenda({key: acts for key, acts in plan.items() if one <= key[0] < two})
-        agenda.tick()
 
         @pl.when(step == steps)
         def _():
@@ -1694,6 +1718,7 @@
             for at in range(steps):
                 shares[at] = total[at * per_tile : (at + 1) * per_tile]
 
+        agenda.tick()
         share = shares[step - steps]
         unit, _ = normalized(x_ref[...].astype(f32))
         turned = (unit * vector(gain_ref, 0, 0) + vector(shift_ref, 0, 0)).astype(bf16).T
@@ -1749,6 +1774,7 @@
         pltpu.VMEM(w.shape, f32), pltpu.VMEM(w.shape, bf16), pltpu.VMEM((4, 8, d), f32),
         pltpu.VMEM((4, count, d), f32), pltpu.VMEM((3, count, d), f32), pltpu.VMEM((lines, count, d), f32),
         pltpu.VMEM((2, 4, d), f32), pltpu.VMEM((2 * groups, 4, d), f32), pltpu.VMEM((lines, 4, d), f32),
+        pltpu.VMEM(w.shape, bf16), pltpu.SemaphoreType.DMA,
         pltpu.SemaphoreType.DMA((REDUCE_COPIES,)), pltpu.SemaphoreType.DMA((REDUCE_COPIES,)),
     ]
     for _ in range(number):
@@ -1761,7 +1787,7 @@
         functools.partial(land_kernel, lines, steps),
         name="land",
         grid=(3 * steps,),
-        in_specs=[walk] + [early] * 5 + [log_spec, vmem, late] + [vmem] * 3 + [hbm] + [vmem] * 3,
+        in_specs=[walk] + [early] * 5 + [log_spec, vmem, late, hbm] + [vmem] * 2 + [hbm] + [vmem] * 3,
         out_specs=[late, vmem, vmem, vmem],
         out_shape=[
             struct((rows, d), f32), struct((number, SECTION, width, LANES), f32),
@@ -1779,10 +1805,10 @@
     count = up_out.shape[2] // LANES
     for l, pieces in enumerate((low_pieces, high_pieces)):
         blocks = [pieces[at // SECTION, at % SECTION] for at in range(pieces.shape[0] * SECTION)]
-        out_out[l] = blocks[0].T
+        out_out[l] = blocks[0]
         for at in range(count):
             up_out[l, :, pl.ds(at * LANES, LANES)] = blocks[1 + at]
-            down_out[l, pl.ds(at * LANES, LANES), :] = blocks[1 + count + at].T
+            down_out[l, :, pl.ds(at * LANES, LANES)] = blocks[1 + count + at]
         for at in range(3):
             qkv_out[l, at] = blocks[1 + 2 * count + at]
     store_vectors(early, last, vector_outs)
@@ -1797,6 +1823,10 @@
         out_specs=[vmem] * len(shapes),
         out_shape=[jax.ShapeDtypeStruct(shape, f32) for shape in shapes],
     )(low_pieces, high_pieces, early, last)
+
+
+def turned(array):
+    return jnp.transpose(array, (0, 2, 1))
 
 
 def body(
@@ -1815,7 +1845,8 @@
     if direct:
         (q0, k0, v0, sums0, att0, log0, middle0, act0, slope0, x1, q1, k1, v1, sums1,
          first0, rest0, first1, rest1, up_all) = ascend(
-            inputs, w_qkv, w_out, w_up, w_down, bias_qv, bias_up, ln_gain, ln_bias, branch_bias, tile
+            inputs, w_qkv, turned(w_out), w_up, turned(w_down), bias_qv, bias_up, ln_gain, ln_bias,
+            branch_bias, tile,
         )
         firsts = [first.reshape(groups, 3, d, LANES) for first in (first0, first1)]
         rests = [rest.reshape(groups, rest.shape[1], d, LANES) for rest in (rest0, rest1)]
@@ -1864,29 +1895,29 @@
             [flat],
         )
         sums1 = share_sums(sums1, 2)
-    slab = ("w", (own_blocks, 2 * d), f32) if direct else back[4]
     outputs, dmid1, dq1, dk1, dv1, dsum1, rest1, small1 = run(
         turn_kernel, 1, "turn",
-        [("t", x1), ("t", q1), ("t", k1), ("t", v1), ("w", sums1), ("w", rests[1])]
+        [("t", x1), ("t", q1), ("t", k1), ("t", v1), ("w", sums1), ("h", rests[1])]
         + norm + [("w", up_all), ("w", branch_bias), ("t", cotangent)],
-        [("t", (rows, d), bf16)] + back[:4] + [slab] + back[5:],
+        [("t", (rows, d), bf16)] + back,
         [tile_bf16, pltpu.VMEM((per_tile, blocks, 2 * SPAN), f32), pltpu.VMEM((tile, ff), bf16),
-         pltpu.VMEM((tile, ff), bf16), tile_bf16, acc, flat, flat]
-        + (Shares.scratch(groups, own_blocks, 2 * d) if direct else []),
-        2 if direct else None,
+         pltpu.VMEM((tile, ff), bf16), tile_bf16, acc, flat, flat,
+         pltpu.VMEM(rests[1].shape, bf16), pltpu.SemaphoreType.DMA],
     )
     like = (w_qkv.shape, w_out.shape, w_up.shape, w_down.shape, ln_gain.shape, ln_bias.shape,
             bias_qv.shape, bias_up.shape, branch_bias.shape)
     if direct:
         small1_first, dmid0, datt0, rest0, small0, high_pieces = descend(
-            x1, (dmid1, dq1, dk1, dv1), dsum1.reshape(sums_shape), firsts[1], rests[0], ln_gain,
+            x1, (dmid1, dq1, dk1, dv1), dsum1, firsts[1], rests[0], ln_gain,
             ln_bias, (middle0, att0, act0, slope0), rest1, tile,
         )
         dx, low_pieces, early, last = land(
             inputs, (q0, k0, v0, datt0, att0, log0), sums0, dmid0, firsts[0], ln_gain, ln_bias, rest0,
             (small0, small1, small1_first), tile,
         )
-        return (outputs, dx, *settle(low_pieces, high_pieces, early, last, like))
+        like = [shape if at not in (1, 3) else (shape[0], shape[2], shape[1]) for at, shape in enumerate(like)]
+        done = settle(low_pieces, high_pieces, early, last, like)
+        return (outputs, dx, done[0], turned(done[1]), done[2], turned(done[3]), *done[4:])
     dsum1 = return_sums(dsum1, sums_shape, 3)
     first1, small1_first, dmid0, dq0, dk0, dv0, dsum0, rest0, small0 = run(
         backward_kernel, 0, "backward",

time: 291 us -> 266 us (0.914)
  Pallas kernels: 277 us -> 261 us
  local copies, waits for them, and re-layouts: 12.6 us -> 3.86 us
    unnamed x8 -> x1, local copies, waits for them, and re-layouts: 11.1 us -> 3.86 us
    pallas_call x1, Pallas kernels: 67 us -> 60.5 us  [land(): pl.pallas_call(functools.partial(land_kernel, lines, steps), name='land',...]
    pallas_call x1, Pallas kernels: 63.1 us -> 57.8 us  [call(): pl.pallas_call(kernel, name=name, grid=(steps,), in_specs=[spec(kind, arg...]
where the time goes in v5:
time: 266 us
  Pallas kernels  261 us (98%)
  local copies, waits for them, and re-layouts  3.86 us (1%)
    pallas_call x1, Pallas kernels, ascend(): pl.pallas_call(functools.partial(ascend_kernel, lines, groups, steps), na...  89.2 us
    pallas_call x1, Pallas kernels, land(): pl.pallas_call(functools.partial(land_kernel, lines, steps), name='land',...  60.5 us
    pallas_call x1, Pallas kernels, call(): pl.pallas_call(kernel, name=name, grid=(steps,), in_specs=[spec(kind, arg...  57.8 us
    pallas_call x1, Pallas kernels, descend(): pl.pallas_call(functools.partial(descend_kernel, lines, steps), name='des...  51.8 us

profile of v5, /device:TPU:0, one launch (start us, length us, event | category | flops | bytes accessed | tf_op | source)
XLA Modules:
  0.0 265.9 jit_solution(5595507895308671351)
XLA Ops:
  0.6 89.2 %ascend.1 = (bf16[1536,512]{1,0:T(8,128)(2,1)}, bf16[1536,512]{1,0:T(8,128)(2,1)}, bf16[1536,512]{1,0:T(8,128)(2,1)}, f32[48,1024]{1,0:T(8,128)}, bf16[1536,512]...) custom-call(bf16[1536,512]{1,0:T(8,128)(2,1)} %x_ref.3, ...), custom_call_target="tpu_custom_call" | custom-call | tf_op jit(solution)/shard_map/ascend/pallas_call | solution.py:1127
  89.9 57.8 %turn.1 = (bf16[1536,512]{1,0:T(8,128)(2,1)}, f32[1536,512]{1,0:T(8,128)}, bf16[1536,512]{1,0:T(8,128)(2,1)}, f32[1536,512]{1,0:T(8,128)}, f32[1536,512]{1,0:T(8...) custom-call(f32[1536,512]{1,0:T(8,128)} %get-tuple-element.57.x_ref, ...), custom_call_target="tpu_custom_call" | custom-call | tf_op jit(solution)/shard_map/turn/pallas_call | solution.py:543
  147.7 51.8 %descend.1 = (f32[4,8,512]{2,1,0:T(8,128)}, f32[1536,512]{1,0:T(8,128)}, bf16[1536,512]{1,0:T(8,128)(2,1)}, bf16[4,9,512,128]{3,2,1,0:T(8,128)(2,1)}, f32[8,8,512]{2,1,0:T(8,128)}, /*index=5*/f32[4,3,64,128]{3,2,1,0:T(8,128)}) custom-call(f32[1536,512]{1,0:T(8,128)} %get-tuple-element.57.x_ref, f32[1536,512]{1,0:T(8,128)} %get-tuple-element.68.dmid_in, ...), custom_call_target="tpu_custom_call" | custom-call | tf_op jit(solution)/shard_map/descend/pallas_call | solution.py:1607
  199.5 60.5 %land.1 = (f32[1536,512]{1,0:T(8,128)}, f32[4,3,64,128]{3,2,1,0:T(8,128)}, f32[20,512]{1,0:T(8,128)}, f32[4,512]{1,0:T(4,128)}) custom-call(bf16[1536,512]{1,0:T(8,128)(2,1)} %x_ref.3, bf16[1536,512]{1,0:T(8,128)(2,1)} %get-tuple-element.65.q_in, bf16[1536,512]{1,0:T(8,128)(2,1)} %get-tuple-element.66.k_in, bf16[1536,512]{1,0:T(8,128)(2,1)} %get-tuple-element.67.v_in, ...), custom_call_target="tpu_custom_call" | custom-call | tf_op jit(solution)/shard_map/land/pallas_call | solution.py:1786
  260.0 2.0 settle.1
  262.0 3.9 %copy.23 = f32[1536,512]{1,0:T(8,128)} copy(f32[1536,512]{1,0:T(8,128)} %get-tuple-element.115) | data formatting | bytes 6291456

commit v6 on v5

--- a/solution.py
+++ b/solution.py
@@ -224,13 +224,19 @@
     mlp_in = (unit * gain + shift).astype(bf16)
     total = middle + branch_bias
     span = count * LANES
+
+    def raised(j):
+        return dot_nn(mlp_in, wide(w_ref, j, 1, count)) + bias_up[j, pl.ds(l, 1)]
+
+    hidden = raised(0)
     for j in range(blocks):
-        hidden = dot_nn(mlp_in, wide(w_ref, j, 1, count)) + bias_up[j, pl.ds(l, 1)]
+        following = raised(j + 1) if j + 1 < blocks else None
         act, slope = gelu_pair(hidden)
         act = act.astype(bf16)
         act_ref[:, j * span : (j + 1) * span] = act
         slope_ref[:, j * span : (j + 1) * span] = slope.astype(bf16)
         total = total + dot_nt(act, wide(w_ref, j, 1 + count, count))
+        hidden = following
         tick()
     return total
 
@@ -691,14 +697,14 @@
 
 
 class Gather:
-    def __init__(self, name, ref, copies):
-        self.name, self.ref, self.copies = name, ref, copies
+    def __init__(self, name, ref, copies, late):
+        self.name, self.ref, self.copies, self.late = name, ref, copies, late
         self.lines, self.half = ref.shape[2], ref.shape[4] // 2
         self.line, self.core, self.j = place()
         self.low, self.high = flip_low(self.j), flip_high(self.j)
         self.far = flip_high(self.low)
         count = ref.shape[1]
-        self.ahead, self.behind = pl.ds(0, count - count // 3), pl.ds(count - count // 3, count // 3)
+        self.ahead, self.behind = pl.ds(0, count - late), pl.ds(count - late, late)
         self.to_low = device(self.line, self.core, self.low)
         self.to_high = device(self.line, self.core, self.high)
         self.to_partner = device(self.line, 1 - self.core, self.j)
@@ -755,19 +761,25 @@
         self.move(("share slab", d), self.slab(d), self.to_partner, self.slab_like)
 
     def begin(self):
-        for number, upper, where in (
-            (0, True, self.to_low), (1, False, self.to_high),
-            (2, True, self.to_high), (3, False, self.to_low),
-        ):
-            self.move(("bits", number), self.part(self.j, upper), where, self.part_like)
-        for d in range(1, self.lines):
+        if self.late:
+            for number, upper, where in (
+                (0, True, self.to_low), (1, False, self.to_high),
+                (2, True, self.to_high), (3, False, self.to_low),
+            ):
+                self.move(("bits", number), self.part(self.j, upper), where, self.part_like)
+        for d in (1, self.lines - 1):
             self.move(("line", d), self.own(0), self.along(d), self.own_like)
 
+    def begin_more(self):
+        for d in range(2, self.lines - 1):
+            self.move(("line", d), self.own(0), self.along(d), self.own_like)
+
     def spread(self):
-        self.receive(("bits", 0), self.part(self.low, True))
-        self.move(("bits", 4), self.part(self.low, True), self.to_high, self.part_like)
-        self.receive(("bits", 1), self.part(self.high, False))
-        self.move(("bits", 5), self.part(self.high, False), self.to_low, self.part_like)
+        if self.late:
+            self.receive(("bits", 0), self.part(self.low, True))
+            self.move(("bits", 4), self.part(self.low, True), self.to_high, self.part_like)
+            self.receive(("bits", 1), self.part(self.high, False))
+            self.move(("bits", 5), self.part(self.high, False), self.to_low, self.part_like)
         for d in range(1, self.lines):
             self.receive(("line", d), self.own(self.lines - d))
         self.move(("low", 0), self.column(self.j, True), self.to_low, self.column_like)
@@ -824,7 +836,7 @@
              (self.high, True), (self.low, False), (self.far, True), (self.far, False))
         ):
             self.receive(("share", number), self.column(j, upper, other))
-        for d in range(self.lines):
+        for d in range(self.lines if self.late else 0):
             self.receive(("share slab", d), self.slab(d, other))
 
 
@@ -914,7 +926,7 @@
     copies = Copies(send_sem, recv_sem)
     firsts, rests = (first0, first1), (rest0, rest1)
     sections = [
-        Gather((name, l), refs[l], copies)
+        Gather((name, l), refs[l], copies, (l or name == "rest") * (refs[l].shape[1] // 3))
         for l in range(LAYERS)
         for name, refs in (("first", firsts), ("rest", rests))
     ]
@@ -955,19 +967,18 @@
         greet_wait(peers)
         store(0, 0).wait()
         first_a.begin()
+        first_a.begin_more()
         for at, other in enumerate(others):
             where = device(line, core, other)
             copies.send(("pair", at), pair_ref, pair_all.at[j], where, lambda: pair_ref)
             copies.send(("up", at), up_bias_ref, up_all.at[j], where, lambda: up_bias_ref)
+        store(0, 1).wait()
         first_a.spread()
         first_a.spread_more()
-        first_a.slab_begin()
+        rest_a.begin()
+        rest_a.begin_more()
         first_a.cross()
-        first_a.slab_relay()
-        store(0, 1).wait()
-        rest_a.begin()
         first_a.tail()
-        first_a.close()
         for at, other in enumerate(others):
             where = device(line, core, other)
             copies.receive(("pair", at), pair_all.at[other], where)
@@ -978,6 +989,7 @@
     def start_third():
         store(1, 0).wait()
         first_b.begin()
+        first_b.begin_more()
 
     def start_last():
         store(1, 1).wait()
@@ -991,6 +1003,12 @@
         first_b.collect()
         keep(2).start()
 
+    def arrive():
+        for at in (4, 5, 6):
+            keep(at).start()
+        sum_copies[0].receive()
+        sum_copies[0].flatten(sums0)
+
     actions = {}
 
     def at(when, *acts):
@@ -998,20 +1016,21 @@
 
     one, two, three, last = steps, 2 * steps, 3 * steps, 4 * steps - 1
     at((0, 0), begin)
-    at((1, 0), rest_a.spread)
-    at((3, 0), start_third)
-    at((one, 0), rest_a.spread_more, rest_a.slab_begin)
+    at((1, 0), rest_a.spread, start_third, start_last)
+    at((one, 0), rest_a.slab_begin, arrive, rest_a.spread_more)
     at((one + 1, 0), rest_a.cross)
-    at((one + 3, 0), rest_a.slab_relay, start_last)
+    at((one + 2, 0), rest_a.slab_relay, rest_b.begin_more)
     at((one + 4, 0), first_b.spread, first_b.spread_more)
     at((two, 0), rest_a.tail, rest_a.close, first_b.slab_begin, rest_ready)
-    at((two + 1, 0), first_b.cross, rest_b.spread)
+    at((two, 1), rest_b.spread)
+    at((two + 1, 0), first_b.cross)
     at((two + 1, 1), first_b.slab_relay, rest_b.spread_more, rest_b.slab_begin)
     at((two + 2, 1), first_b.tail)
-    at((two + 3, 1), first_b.close, rest_b.cross)
+    at((two + 3, 0), rest_b.cross)
+    at((two + 3, 1), first_b.close)
     at((two + 4, 1), rest_b.slab_relay)
     at((three, 0), first_ready)
-    at((three + 3, 0), rest_b.tail)
+    at((three + 2, 0), rest_b.tail)
     at((three + 4, 0), rest_b.close)
 
     @pl.when(step < steps)
@@ -1033,14 +1052,7 @@
         agenda = Agenda({key: acts for key, acts in actions.items() if one <= key[0] < two})
         now = step - one
 
-        def arrive():
-            for at in (4, 5, 6):
-                keep(at).start()
-            sum_copies[0].receive()
-            sum_copies[0].flatten(sums0)
-
         agenda.tick()
-        when_step(one, arrive)
         base = j * (steps * (tile // SPAN)) + now * (tile // SPAN)
         attend_tile(
             base, q_all.at[rows], k_all.at[rows], v_all.at[rows], sums0, att_ref, log_ref
@@ -1463,19 +1475,19 @@
         up_out[pl.ds(l, 1)] = early[pl.ds(late + 4 + j, 1)]
 
 
-def put_section(section, piece_ref):
+def put_section(section, pieces, first):
     section.end()
     for at in range(section.blocks[1]):
-        piece_ref[at] = section.result(at)
+        pieces[first + at] = section.result(at)
 
 
 def make_sections(sources, copies, refs, lines):
     sections = []
-    for name, source in sources:
-        for first in range(0, source.shape[1], SECTION):
+    for name, source, size in sources:
+        for first in range(0, source.shape[1], size):
             at = BUFFERS * len(sections)
             sections.append(
-                Reduce((name, first), source, (first, SECTION), copies, refs[at : at + BUFFERS], lines)
+                Reduce((name, first), source, (first, size), copies, refs[at : at + BUFFERS], lines)
             )
     return sections
 
@@ -1499,7 +1511,9 @@
     load_high = pltpu.make_async_copy(high_in, high_w, load_sem.at[0])
     load_low = pltpu.make_async_copy(low_in, low_w, load_sem.at[1])
     copies = Copies(send_sem, recv_sem)
-    sections = make_sections((("rest", rest_in), ("first", high_grad)), copies, buffers, lines)
+    sections = make_sections(
+        (("rest", rest_in, SECTION), ("first", high_grad, SECTION)), copies, buffers, lines
+    )
     high = sections[-1]
 
     def begin():
@@ -1520,7 +1534,7 @@
             shares[at] = total[at * per_tile : (at + 1) * per_tile]
 
     def put(at):
-        return lambda: put_section(sections[at], pieces.at[at])
+        return lambda: put_section(sections[at], pieces, SECTION * at)
 
     low = {}
 
@@ -1612,7 +1626,7 @@
         out_specs=[vmem, late(d), late(d), vmem, vmem, vmem],
         out_shape=[
             struct((4, 8, d), f32), struct((rows, d), f32), struct((rows, d), bf16),
-            struct(low_w.shape, bf16), small, struct((number, SECTION, width, LANES), f32),
+            struct(low_w.shape, bf16), small, struct((number * SECTION, width, LANES), f32),
         ],
         scratch_shapes=scratch,
         compiler_params=pltpu.CompilerParams(
@@ -1626,8 +1640,8 @@
     lines, steps, x_ref, q_in, k_in, v_in, datt_ref, att_ref, log_ref, sums, dmid_ref, w_in,
     gain_ref, shift_ref, rest_in, small0, small1, first_small1,
     dx_ref, pieces, small_total, last_total,
-    dq_all, dk_all, dv_all, dk_done, dv_done, dsums, slabs, landed, share_send, share_recv, shares,
-    acc_ref, grad_ref, first_small0, small_own, small_near, small_far, last_own, last_near, last_far,
+    dq_all, dk_all, dv_all, dk_done, dv_done, turned_all, dsums, slabs, landed, share_send, share_recv,
+    grad_ref, first_small0, small_own, small_near, small_far, last_own, last_near, last_far,
     w_ref, w_sem, send_sem, recv_sem, *buffers,
 ):
     step = pl.program_id(0)
@@ -1636,8 +1650,10 @@
     per_tile = tile // SPAN
     j = lax.axis_index("tensor")
     copies = Copies(send_sem, recv_sem)
-    sections = make_sections((("rest", rest_in), ("first", grad_ref)), copies, buffers, lines)
-    last = sections[-1]
+    sections = make_sections(
+        (("rest", rest_in, SECTION), ("first", grad_ref, 1)), copies, buffers, lines
+    )
+    lasts = sections[-3:]
     traffic = Shares(slabs, landed, share_send, share_recv)
     smalls = (small0, small1, first_small1)
 
@@ -1648,14 +1664,14 @@
         peers = near_peers(lines) + [device(line, core, far)] + others
         greet_signal(peers)
         load.start()
-        for ref in (acc_ref, first_small0, dsums):
+        for ref in (first_small0, dsums):
             ref[...] = jnp.zeros_like(ref)
         greet_wait(peers)
-        for section in sections[:-1]:
+        for section in sections[:-3]:
             section.begin()
 
     def put(at):
-        return lambda: put_section(sections[at], pieces.at[at])
+        return lambda: put_section(sections[at], pieces, SECTION * at)
 
     def small(stage):
         return small_sums(smalls, copies, lines, small_own, small_near, small_far, stage)
@@ -1674,24 +1690,20 @@
     def at(when, *acts):
         plan.setdefault(when, []).extend(acts)
 
-    one, two = steps, 2 * steps
+    one, two, last = steps, steps + 1, 2 * steps
     at((0, 0), begin)
     at((0, 1), small_step(0))
     at((1, 0), sections[0].first_sum)
     at((1, 1), small_step(1), sections[1].first_sum)
     at((3, 1), sections[0].second_sum)
-    at((one, 0), sections[2].first_sum)
-    at((one + 1, 0), sections[1].second_sum, small_step(2))
-    at((one + 2, 0), sections[0].third_sum)
-    at((one + 4, 0), sections[2].second_sum, sections[1].third_sum)
-    at((one + 5, 0), small_step(3), put(0))
-    at((two, 0), last.begin, load.wait)
-    at((two + 1, 0), sections[2].third_sum)
-    at((two + 2, 0), last.first_sum)
-    at((two + 3, 0), put(1))
-    at((two + 4, 0), small_end)
-    at((two + 5, 0), put(2))
+    at((two, 0), lasts[0].first_sum, sections[1].second_sum, load.wait)
+    at((two + 1, 0), lasts[1].first_sum, lasts[2].first_sum)
+    at((two + 2, 0), sections[0].third_sum, small_step(2))
+    at((two + 3, 0), sections[2].second_sum)
+    at((two + 4, 0), sections[1].third_sum, small_step(3))
     rows = pl.ds(pl.multiple_of(lax.rem(step, steps) * tile, tile), tile)
+    walked = pl.ds(pl.multiple_of(lax.rem(step + steps - 1, steps) * tile, tile), tile)
+    gain, shift = vector(gain_ref, 0, 0), vector(shift_ref, 0, 0)
 
     @pl.when(step < steps)
     def _():
@@ -1701,6 +1713,8 @@
             (j * steps + step) * per_tile, q_in, k_in, v_in, sums, datt_ref, att_ref, log_ref,
             dq_all.at[rows], dk_all.at[rows], dv_all.at[rows], dsums,
         )
+        unit, _ = normalized(x_ref[...].astype(f32))
+        turned_all[:, rows] = (unit * gain + shift).astype(bf16).T
         agenda.tick()
 
     @pl.when(step == steps - 1)
@@ -1708,29 +1722,26 @@
         store_sums(dsums, slabs)
         traffic.send()
 
-    @pl.when((step >= steps) & (step < two))
+    @pl.when(step == one)
     def _():
-        agenda = Agenda({key: acts for key, acts in plan.items() if one <= key[0] < two})
-
-        @pl.when(step == steps)
-        def _():
-            total = traffic.receive()
-            for at in range(steps):
-                shares[at] = total[at * per_tile : (at + 1) * per_tile]
-
-        agenda.tick()
-        share = shares[step - steps]
-        unit, _ = normalized(x_ref[...].astype(f32))
-        turned = (unit * vector(gain_ref, 0, 0) + vector(shift_ref, 0, 0)).astype(bf16).T
-        grad_keys = spread_share(dk_all.at[rows], share, 0)
-        grad_values = spread_share(dv_all.at[rows], share, d)
-        dk_done[rows] = grad_keys
-        dv_done[rows] = grad_values
-        project_grads(turned, (dq_all[rows], grad_keys, grad_values), acc_ref, first_small0)
-
-    @pl.when(step == two - 1)
-    def _():
-        store_grads((acc_ref, grad_ref))
+        def weight_grad(at, grads):
+            value = dot_nn(turned_all[...], grads)
+            for column in range(grad_ref.shape[0]):
+                part = value[:, column * LANES : (column + 1) * LANES]
+                grad_ref[column, at] = part.astype(bf16)
+
+        weight_grad(0, dq_all[...])
+        first_small0[2] = row_sums(dq_all[...].astype(f32))
+        total = traffic.receive()
+        sections[2].first_sum()
+        lasts[0].begin()
+        dk_done[...] = spread_share(dk_all, total, 0)
+        dv_done[...] = spread_share(dv_all, total, d)
+        weight_grad(1, dk_done[...])
+        weight_grad(2, dv_done[...])
+        lasts[1].begin()
+        first_small0[3] = row_sums(dv_done[...].astype(f32))
+        lasts[2].begin()
 
     @pl.when(step >= two)
     def _():
@@ -1738,18 +1749,25 @@
         agenda.tick()
         unit, rate = normalized(x_ref[...].astype(f32))
         dx_ref[...] = project_input(
-            (dq_all[rows], dk_done[rows], dv_done[rows]), unit, rate, dmid_ref[...], w_ref,
-            vector(gain_ref, 0, 0), first_small0,
-        )
-
-    @pl.when(step == 3 * steps - 1)
+            (dq_all[walked], dk_done[walked], dv_done[walked]), unit, rate, dmid_ref[...], w_ref,
+            gain, first_small0,
+        )
+
+    @pl.when(step == last)
     def _():
         final(0)
-        last.second_sum()
+        for section in lasts:
+            section.second_sum()
         final(1)
-        last.third_sum()
+        sections[2].third_sum()
+        for section in lasts:
+            section.third_sum()
+        for at in range(3):
+            put(at)()
+        small_end()
         last_total[...] = final(2)
-        put(3)()
+        for at, section in enumerate(lasts):
+            put_section(section, pieces, 3 * SECTION + at)
         copies.finish()
 
 
@@ -1763,34 +1781,35 @@
     vmem = pl.BlockSpec(memory_space=pltpu.VMEM)
     hbm = pl.BlockSpec(memory_space=pl.ANY)
     struct = jax.ShapeDtypeStruct
-    number = (rest_grad.shape[1] + w.shape[1]) // SECTION
+    sizes = [SECTION] * (rest_grad.shape[1] // SECTION) + [1] * w.shape[1]
     count = sum(small.shape[0] for small in smalls)
     scratch = [
         pltpu.VMEM((rows, d), bf16), pltpu.VMEM((rows, d), f32), pltpu.VMEM((rows, d), f32),
-        pltpu.VMEM((rows, d), bf16), pltpu.VMEM((rows, d), bf16),
+        pltpu.VMEM((rows, d), bf16), pltpu.VMEM((rows, d), bf16), pltpu.VMEM((d, rows), bf16),
         pltpu.VMEM((blocks * groups, 2 * d), f32),
         *Shares.scratch(groups, blocks, 2 * d),
-        pltpu.VMEM((steps, per_tile, 2 * d), f32),
-        pltpu.VMEM(w.shape, f32), pltpu.VMEM(w.shape, bf16), pltpu.VMEM((4, 8, d), f32),
+        pltpu.VMEM(w.shape, bf16), pltpu.VMEM((4, 8, d), f32),
         pltpu.VMEM((4, count, d), f32), pltpu.VMEM((3, count, d), f32), pltpu.VMEM((lines, count, d), f32),
         pltpu.VMEM((2, 4, d), f32), pltpu.VMEM((2 * groups, 4, d), f32), pltpu.VMEM((lines, 4, d), f32),
         pltpu.VMEM(w.shape, bf16), pltpu.SemaphoreType.DMA,
         pltpu.SemaphoreType.DMA((REDUCE_COPIES,)), pltpu.SemaphoreType.DMA((REDUCE_COPIES,)),
     ]
-    for _ in range(number):
-        scratch += Reduce.buffers(lines, groups, SECTION, width)
-    walk = pl.BlockSpec((tile, d), lambda i: (lax.rem(i, steps), 0))
+    for size in sizes:
+        scratch += Reduce.buffers(lines, groups, size, width)
+    walk = pl.BlockSpec(
+        (tile, d), lambda i: (jnp.where(i < steps, i, jnp.maximum(i - steps - 1, 0)), 0)
+    )
     early = clipped(steps, 0, (tile, d))
-    late = clipped(steps, 2 * steps, (tile, d))
+    late = clipped(steps, steps + 1, (tile, d))
     log_spec = clipped(steps, 0, (per_tile,) + saved[-1].shape[1:])
     return pl.pallas_call(
         functools.partial(land_kernel, lines, steps),
         name="land",
-        grid=(3 * steps,),
+        grid=(2 * steps + 1,),
         in_specs=[walk] + [early] * 5 + [log_spec, vmem, late, hbm] + [vmem] * 2 + [hbm] + [vmem] * 3,
         out_specs=[late, vmem, vmem, vmem],
         out_shape=[
-            struct((rows, d), f32), struct((number, SECTION, width, LANES), f32),
+            struct((rows, d), f32), struct((sum(sizes), width, LANES), f32),
             struct((count, d), f32), struct((4, d), f32),
         ],
         scratch_shapes=scratch,
@@ -1804,7 +1823,7 @@
 def settle_kernel(low_pieces, high_pieces, early, last, qkv_out, out_out, up_out, down_out, *vector_outs):
     count = up_out.shape[2] // LANES
     for l, pieces in enumerate((low_pieces, high_pieces)):
-        blocks = [pieces[at // SECTION, at % SECTION] for at in range(pieces.shape[0] * SECTION)]
+        blocks = [pieces[at] for at in range(pieces.shape[0])]
         out_out[l] = blocks[0]
         for at in range(count):
             up_out[l, :, pl.ds(at * LANES, LANES)] = blocks[1 + at]

time: 266 us -> 256 us (0.962)
  Pallas kernels: 261 us -> 251 us
    pallas_call x1, Pallas kernels: 89.2 us -> 83.2 us  [ascend(): pl.pallas_call(functools.partial(ascend_kernel, lines, groups, steps), na...]
    pallas_call x1, Pallas kernels: 57.8 us -> 55 us  [call(): pl.pallas_call(kernel, name=name, grid=(steps,), in_specs=[spec(kind, arg...]
where the time goes in v6:
time: 256 us
  Pallas kernels  251 us (98%)
  local copies, waits for them, and re-layouts  3.86 us (2%)
    pallas_call x1, Pallas kernels, ascend(): pl.pallas_call(functools.partial(ascend_kernel, lines, groups, steps), na...  83.2 us
    pallas_call x1, Pallas kernels, land(): pl.pallas_call(functools.partial(land_kernel, lines, steps), name='land',...  59.2 us
    pallas_call x1, Pallas kernels, call(): pl.pallas_call(kernel, name=name, grid=(steps,), in_specs=[spec(kind, arg...  55 us
    pallas_call x1, Pallas kernels, descend(): pl.pallas_call(functools.partial(descend_kernel, lines, steps), name='des...  51.9 us

profile of v6, /device:TPU:0, one launch (start us, length us, event | category | flops | bytes accessed | tf_op | source)
XLA Modules:
  0.0 255.8 jit_solution(6127041708924880611)
XLA Ops:
  0.6 83.2 %ascend.1 = (bf16[1536,512]{1,0:T(8,128)(2,1)}, bf16[1536,512]{1,0:T(8,128)(2,1)}, bf16[1536,512]{1,0:T(8,128)(2,1)}, f32[48,1024]{1,0:T(8,128)}, bf16[1536,512]...) custom-call(bf16[1536,512]{1,0:T(8,128)(2,1)} %x_ref.3, ...), custom_call_target="tpu_custom_call" | custom-call | tf_op jit(solution)/shard_map/ascend/pallas_call | solution.py:1139
  83.8 55.0 %turn.1 = (bf16[1536,512]{1,0:T(8,128)(2,1)}, f32[1536,512]{1,0:T(8,128)}, bf16[1536,512]{1,0:T(8,128)(2,1)}, f32[1536,512]{1,0:T(8,128)}, f32[1536,512]{1,0:T(8...) custom-call(f32[1536,512]{1,0:T(8,128)} %get-tuple-element.57.x_ref, ...), custom_call_target="tpu_custom_call" | custom-call | tf_op jit(solution)/shard_map/turn/pallas_call | solution.py:549
  138.8 51.9 %descend.1 = (f32[4,8,512]{2,1,0:T(8,128)}, f32[1536,512]{1,0:T(8,128)}, bf16[1536,512]{1,0:T(8,128)(2,1)}, bf16[4,9,512,128]{3,2,1,0:T(8,128)(2,1)}, f32[8,8,512]{2,1,0:T(8,128)}, /*index=5*/f32[12,64,128]{2,1,0:T(8,128)}) custom-call(f32[1536,512]{1,0:T(8,128)} %get-tuple-element.57.x_ref, f32[1536,512]{1,0:T(8,128)} %get-tuple-element.68.dmid_in, ...), custom_call_target="tpu_custom_call" | custom-call | tf_op jit(solution)/shard_map/descend/pallas_call | solution.py:1621
  190.7 59.2 %land.1 = (f32[1536,512]{1,0:T(8,128)}, f32[12,64,128]{2,1,0:T(8,128)}, f32[20,512]{1,0:T(8,128)}, f32[4,512]{1,0:T(4,128)}) custom-call(bf16[1536,512]{1,0:T(8,128)(2,1)} %x_ref.3, bf16[1536,512]{1,0:T(8,128)(2,1)} %get-tuple-element.65.q_in, bf16[1536,512]{1,0:T(8,128)(2,1)} %get-tuple-element.66.k_in, bf16[1536,512]{1,0:T(8,128)(2,1)} %get-tuple-element.67.v_in, ...), custom_call_target="tpu_custom_call" | custom-call | tf_op jit(solution)/shard_map/land/pallas_call | solution.py:1805
  249.9 2.0 settle.1
  251.9 3.9 %copy.23 = f32[1536,512]{1,0:T(8,128)} copy(f32[1536,512]{1,0:T(8,128)} %get-tuple-element.115) | data formatting | bytes 6291456

commit v7 on v6

--- a/solution.py
+++ b/solution.py
@@ -256,16 +256,24 @@
     mlp_in = (unit * gain + shift).astype(bf16)
     turned_in = mlp_in.T
     dyb = dy.astype(bf16)
-    turned_dy = dyb.T
+    with_down = acc_ref.shape[1] == w_ref.shape[1]
+    turned_dy = dyb.T if with_down else None
     grad_in = None
+
+    def lowered(j):
+        return dot_nn(dyb, wide(w_ref, j, 1 + count, count))
+
+    grad_act = lowered(0)
     for j in range(blocks):
         part = slice(j * span, (j + 1) * span)
-        grad_act = dot_nn(dyb, wide(w_ref, j, 1 + count, count))
+        following = lowered(j + 1) if j + 1 < blocks else None
         grad_hidden = (grad_act * slope_ref[:, part].astype(f32)).astype(bf16)
         small_ref[4 + j] += row_sums(grad_hidden.astype(f32))
-        accumulate(acc_ref, j, 1 + count, dot_nn(turned_dy, act_ref[:, part]))
+        if with_down:
+            accumulate(acc_ref, j, 1 + count, dot_nn(turned_dy, act_ref[:, part]))
         accumulate(acc_ref, j, 1, dot_nn(turned_in, grad_hidden))
         term = dot_nt(grad_hidden, wide(w_ref, j, 1, count))
+        grad_act = following
         grad_in = term if grad_in is None else grad_in + term
         tick()
     small_ref[0] += row_sums(grad_in * unit)
@@ -1481,13 +1489,18 @@
         pieces[first + at] = section.result(at)
 
 
+def section_sizes(blocks, size):
+    return [min(size, blocks - first) for first in range(0, blocks, size)]
+
+
 def make_sections(sources, copies, refs, lines):
     sections = []
     for name, source, size in sources:
         for first in range(0, source.shape[1], size):
             at = BUFFERS * len(sections)
+            blocks = (first, min(size, source.shape[1] - first))
             sections.append(
-                Reduce((name, first), source, (first, size), copies, refs[at : at + BUFFERS], lines)
+                Reduce((name, first), source, blocks, copies, refs[at : at + BUFFERS], lines)
             )
     return sections
 
@@ -1501,7 +1514,7 @@
     lines, steps, x_ref, dmid_in, dq_in, dk_in, dv_in, slabs, high_in, low_in, gain_ref, shift_ref,
     middle_ref, att_ref, act_ref, slope_ref, rest_in,
     high_small, dmid_ref, datt_ref, grad_ref, small_ref, pieces,
-    dy_all, high_acc, acc_ref, high_grad, high_w, low_w, load_sem, shares, landed, share_send,
+    dy_all, high_acc, acc_ref, down_acc, high_grad, down_grad, high_w, low_w, load_sem, shares, landed, share_send,
     share_recv, send_sem, recv_sem, *buffers,
 ):
     step = pl.program_id(0)
@@ -1512,9 +1525,10 @@
     load_low = pltpu.make_async_copy(low_in, low_w, load_sem.at[1])
     copies = Copies(send_sem, recv_sem)
     sections = make_sections(
-        (("rest", rest_in, SECTION), ("first", high_grad, SECTION)), copies, buffers, lines
+        (("rest", rest_in, SECTION), ("first", high_grad, SECTION), ("down", down_grad, 2)),
+        copies, buffers, lines,
     )
-    high = sections[-1]
+    high, downs = sections[3], sections[4:]
 
     def begin():
         line, core, j = place()
@@ -1522,14 +1536,15 @@
         greet_signal(peers)
         load_high.start()
         load_low.start()
-        for ref in (high_acc, small_ref, high_small, acc_ref):
+        for ref in (high_acc, small_ref, high_small, acc_ref, down_acc):
             ref[...] = jnp.zeros_like(ref)
         greet_wait(peers)
         traffic.send()
-        for section in sections[:-1]:
+        for section in sections[:3]:
             section.begin()
         load_high.wait()
         total = traffic.receive()
+        sections[0].first_sum()
         for at in range(steps):
             shares[at] = total[at * per_tile : (at + 1) * per_tile]
 
@@ -1543,21 +1558,22 @@
 
     one = steps
     at((0, 0), begin)
-    at((1, 0), sections[0].first_sum)
-    at((2, 0), sections[1].first_sum)
-    at((3, 0), sections[2].first_sum)
-    at((5, 0), sections[0].second_sum)
-    at((one, 0), load_low.wait, high.begin)
-    at((one, 1), sections[1].second_sum)
-    at((one + 1, 0), high.first_sum, sections[0].third_sum)
-    at((one + 1, 1), sections[2].second_sum)
-    at((one + 2, 0), sections[1].third_sum)
-    at((one + 2, 1), high.second_sum, put(0))
-    at((one + 3, 0), sections[2].third_sum)
-    at((one + 3, 1), put(1))
-    at((one + 4, 0), high.third_sum)
-    at((one + 4, 1), put(2))
-    at((one + 5, 1), put(3))
+    def put_down(at):
+        return lambda: put_section(downs[at], pieces, 4 * SECTION + 2 * at)
+
+    at((1, 0), sections[1].first_sum)
+    at((2, 0), sections[2].first_sum)
+    at((3, 0), sections[0].second_sum)
+    at((5, 0), sections[1].second_sum)
+    at((one, 0), load_low.wait, high.begin, downs[0].begin, downs[1].begin, sections[2].second_sum)
+    at((one, 1), high.first_sum, sections[0].third_sum)
+    at((one + 1, 0), downs[0].first_sum)
+    at((one + 1, 1), downs[1].first_sum, sections[1].third_sum)
+    at((one + 2, 1), sections[2].third_sum, high.second_sum)
+    at((one + 3, 0), put(0))
+    at((one + 4, 0), downs[0].second_sum, put(1))
+    at((one + 4, 1), high.third_sum, put(2))
+    at((one + 5, 1), downs[1].second_sum, downs[0].third_sum, put(3))
 
     @pl.when(step < steps)
     def _():
@@ -1568,10 +1584,15 @@
             vector(gain_ref, 1, 0), vector(shift_ref, 1, 0), high_acc, high_small,
         )
         dy_all[pl.ds(pl.multiple_of(step * tile, tile), tile)] = dy
+        turned_dy = dy.astype(bf16).T
+        span = down_acc.shape[1] * LANES
+        for at_block in range(down_acc.shape[0]):
+            part = slice(at_block * span, (at_block + 1) * span)
+            accumulate(down_acc, at_block, 0, dot_nn(turned_dy, act_ref[:, part]))
 
     @pl.when(step == steps - 1)
     def _():
-        store_grads((high_acc, high_grad))
+        store_grads((high_acc, high_grad), (down_acc, down_grad))
 
     @pl.when(step >= steps)
     def _():
@@ -1588,6 +1609,9 @@
     @pl.when(step == 2 * steps - 1)
     def _():
         store_grads((acc_ref, grad_ref))
+        downs[1].third_sum()
+        for at_down in range(2):
+            put_down(at_down)()
         copies.finish()
 
 
@@ -1608,25 +1632,30 @@
 
     struct = jax.ShapeDtypeStruct
     small = struct((4 + groups, 8, d), f32)
-    number = (rest_grad.shape[1] + high_w.shape[1]) // SECTION
+    count = (low_w.shape[1] - 1) // 2
+    sizes = section_sizes(rest_grad.shape[1], SECTION) + section_sizes(high_w.shape[1], SECTION)
+    sizes += section_sizes(count, 2)
+    upper = (groups, 1 + count) + low_w.shape[2:]
+    lower = (groups, count) + low_w.shape[2:]
     scratch = [
-        pltpu.VMEM((rows, d), f32), pltpu.VMEM(high_w.shape, f32), pltpu.VMEM(low_w.shape, f32),
-        pltpu.VMEM(high_w.shape, bf16), pltpu.VMEM(high_w.shape, bf16), pltpu.VMEM(low_w.shape, bf16),
+        pltpu.VMEM((rows, d), f32), pltpu.VMEM(high_w.shape, f32), pltpu.VMEM(upper, f32),
+        pltpu.VMEM(lower, f32), pltpu.VMEM(high_w.shape, bf16), pltpu.VMEM(lower, bf16), pltpu.VMEM(high_w.shape, bf16), pltpu.VMEM(low_w.shape, bf16),
         pltpu.SemaphoreType.DMA((2,)), pltpu.VMEM((steps, tile // SPAN, 2 * d), f32),
         *Shares.scratch(groups, slabs.shape[1], 2 * d)[1:],
         pltpu.SemaphoreType.DMA((REDUCE_COPIES,)), pltpu.SemaphoreType.DMA((REDUCE_COPIES,)),
     ]
-    for _ in range(number):
-        scratch += Reduce.buffers(lines, groups, SECTION, width)
+    for size in sizes:
+        scratch += Reduce.buffers(lines, groups, size, width)
     return pl.pallas_call(
         functools.partial(descend_kernel, lines, steps),
         name="descend",
         grid=(2 * steps,),
-        in_specs=[early(d)] * 5 + [vmem] + [hbm] * 2 + [vmem] * 2 + [late(d)] * 2 + [late(ff)] * 2 + [hbm],
+        in_specs=[early(d)] * 5 + [vmem] + [hbm] * 2 + [vmem] * 2 + [late(d)] * 2
+        + [pl.BlockSpec((tile, ff), lambda i: (lax.rem(i, steps), 0)), late(ff), hbm],
         out_specs=[vmem, late(d), late(d), vmem, vmem, vmem],
         out_shape=[
             struct((4, 8, d), f32), struct((rows, d), f32), struct((rows, d), bf16),
-            struct(low_w.shape, bf16), small, struct((number * SECTION, width, LANES), f32),
+            struct(upper, bf16), small, struct((sum(sizes), width, LANES), f32),
         ],
         scratch_shapes=scratch,
         compiler_params=pltpu.CompilerParams(
@@ -1699,7 +1728,6 @@
     at((two, 0), lasts[0].first_sum, sections[1].second_sum, load.wait)
     at((two + 1, 0), lasts[1].first_sum, lasts[2].first_sum)
     at((two + 2, 0), sections[0].third_sum, small_step(2))
-    at((two + 3, 0), sections[2].second_sum)
     at((two + 4, 0), sections[1].third_sum, small_step(3))
     rows = pl.ds(pl.multiple_of(lax.rem(step, steps) * tile, tile), tile)
     walked = pl.ds(pl.multiple_of(lax.rem(step + steps - 1, steps) * tile, tile), tile)
@@ -1733,7 +1761,6 @@
         weight_grad(0, dq_all[...])
         first_small0[2] = row_sums(dq_all[...].astype(f32))
         total = traffic.receive()
-        sections[2].first_sum()
         lasts[0].begin()
         dk_done[...] = spread_share(dk_all, total, 0)
         dv_done[...] = spread_share(dv_all, total, d)
@@ -1759,15 +1786,14 @@
         for section in lasts:
             section.second_sum()
         final(1)
-        sections[2].third_sum()
         for section in lasts:
             section.third_sum()
-        for at in range(3):
+        for at in range(2):
             put(at)()
         small_end()
         last_total[...] = final(2)
         for at, section in enumerate(lasts):
-            put_section(section, pieces, 3 * SECTION + at)
+            put_section(section, pieces, rest_in.shape[1] + at)
         copies.finish()
 
 
@@ -1781,7 +1807,7 @@
     vmem = pl.BlockSpec(memory_space=pltpu.VMEM)
     hbm = pl.BlockSpec(memory_space=pl.ANY)
     struct = jax.ShapeDtypeStruct
-    sizes = [SECTION] * (rest_grad.shape[1] // SECTION) + [1] * w.shape[1]
+    sizes = section_sizes(rest_grad.shape[1], SECTION) + [1] * w.shape[1]
     count = sum(small.shape[0] for small in smalls)
     scratch = [
         pltpu.VMEM((rows, d), bf16), pltpu.VMEM((rows, d), f32), pltpu.VMEM((rows, d), f32),
@@ -1822,8 +1848,11 @@
 
 def settle_kernel(low_pieces, high_pieces, early, last, qkv_out, out_out, up_out, down_out, *vector_outs):
     count = up_out.shape[2] // LANES
-    for l, pieces in enumerate((low_pieces, high_pieces)):
-        blocks = [pieces[at] for at in range(pieces.shape[0])]
+    low = [low_pieces[at] for at in range(low_pieces.shape[0])]
+    high = [high_pieces[at] for at in range(high_pieces.shape[0])]
+    whole_layer = 4 + 2 * count
+    low = low[: 1 + count] + high[whole_layer:] + low[1 + count :]
+    for l, blocks in enumerate((low, high[:whole_layer])):
         out_out[l] = blocks[0]
         for at in range(count):
             up_out[l, :, pl.ds(at * LANES, LANES)] = blocks[1 + at]

time: 256 us -> 255 us (level)
    pallas_call x1, Pallas kernels: 59.2 us -> 50.3 us  [land(): pl.pallas_call(functools.partial(land_kernel, lines, steps), name='land',...]
    pallas_call x1, Pallas kernels: 51.9 us -> 59.2 us  [descend(): pl.pallas_call(functools.partial(descend_kernel, lines, steps), name='des...]
where the time goes in v7:
time: 255 us
  Pallas kernels  250 us (98%)
  local copies, waits for them, and re-layouts  3.86 us (2%)
    pallas_call x1, Pallas kernels, ascend(): pl.pallas_call(functools.partial(ascend_kernel, lines, groups, steps), na...  83.3 us
    pallas_call x1, Pallas kernels, descend(): pl.pallas_call(functools.partial(descend_kernel, lines, steps), name='des...  59.2 us
    pallas_call x1, Pallas kernels, call(): pl.pallas_call(kernel, name=name, grid=(steps,), in_specs=[spec(kind, arg...  55.4 us
    pallas_call x1, Pallas kernels, land(): pl.pallas_call(functools.partial(land_kernel, lines, steps), name='land',...  50.3 us

profile of v7, /device:TPU:0, one launch (start us, length us, event | category | flops | bytes accessed | tf_op | source)
XLA Modules:
  0.0 254.7 jit_solution(8432217103412181001)
XLA Ops:
  0.6 83.3 %ascend.1 = (bf16[1536,512]{1,0:T(8,128)(2,1)}, bf16[1536,512]{1,0:T(8,128)(2,1)}, bf16[1536,512]{1,0:T(8,128)(2,1)}, f32[48,1024]{1,0:T(8,128)}, bf16[1536,512]...) custom-call(bf16[1536,512]{1,0:T(8,128)(2,1)} %x_ref.3, ...), custom_call_target="tpu_custom_call" | custom-call | tf_op jit(solution)/shard_map/ascend/pallas_call | solution.py:1147
  83.9 55.4 %turn.1 = (bf16[1536,512]{1,0:T(8,128)(2,1)}, f32[1536,512]{1,0:T(8,128)}, bf16[1536,512]{1,0:T(8,128)(2,1)}, f32[1536,512]{1,0:T(8,128)}, f32[1536,512]{1,0:T(8...) custom-call(f32[1536,512]{1,0:T(8,128)} %get-tuple-element.57.x_ref, ...), custom_call_target="tpu_custom_call" | custom-call | tf_op jit(solution)/shard_map/turn/pallas_call | solution.py:557
  139.3 59.2 %descend.1 = (f32[4,8,512]{2,1,0:T(8,128)}, f32[1536,512]{1,0:T(8,128)}, bf16[1536,512]{1,0:T(8,128)(2,1)}, bf16[4,5,512,128]{3,2,1,0:T(8,128)(2,1)}, f32[8,8,512]{2,1,0:T(8,128)}, /*index=5*/f32[16,64,128]{2,1,0:T(8,128)}) custom-call(f32[1536,512]{1,0:T(8,128)} %get-tuple-element.57.x_ref, f32[1536,512]{1,0:T(8,128)} %get-tuple-element.68.dmid_in, ...), custom_call_target="tpu_custom_call" | custom-call | tf_op jit(solution)/shard_map/descend/pallas_call | solution.py:1649
  198.5 50.3 %land.1 = (f32[1536,512]{1,0:T(8,128)}, f32[8,64,128]{2,1,0:T(8,128)}, f32[20,512]{1,0:T(8,128)}, f32[4,512]{1,0:T(4,128)}) custom-call(bf16[1536,512]{1,0:T(8,128)(2,1)} %x_ref.3, bf16[1536,512]{1,0:T(8,128)(2,1)} %get-tuple-element.65.q_in, bf16[1536,512]{1,0:T(8,128)(2,1)} %get-tuple-element.66.k_in, bf16[1536,512]{1,0:T(8,128)(2,1)} %get-tuple-element.67.v_in, ...), custom_call_target="tpu_custom_call" | custom-call | tf_op jit(solution)/shard_map/land/pallas_call | solution.py:1831
  248.8 2.0 settle.1
  250.8 3.9 %copy.23 = f32[1536,512]{1,0:T(8,128)} copy(f32[1536,512]{1,0:T(8,128)} %get-tuple-element.115) | data formatting | bytes 6291456

commit v8 on v7

--- a/solution.py
+++ b/solution.py
@@ -1033,13 +1033,13 @@
     at((two, 1), rest_b.spread)
     at((two + 1, 0), first_b.cross)
     at((two + 1, 1), first_b.slab_relay, rest_b.spread_more, rest_b.slab_begin)
-    at((two + 2, 1), first_b.tail)
     at((two + 3, 0), rest_b.cross)
-    at((two + 3, 1), first_b.close)
-    at((two + 4, 1), rest_b.slab_relay)
+    at((two + 3, 1), first_b.tail)
+    at((two + 4, 1), first_b.close)
+    at((two + 5, 0), rest_b.slab_relay)
     at((three, 0), first_ready)
     at((three + 2, 0), rest_b.tail)
-    at((three + 4, 0), rest_b.close)
+    at((three + 5, 0), rest_b.close)
 
     @pl.when(step < steps)
     def _():

time: 255 us -> 256 us (level)
  no operation moved by 1% of the time
where the time goes in v8:
time: 256 us; the launch traced here: 255 us
  Pallas kernels  251 us (98%)
  local copies, waits for them, and re-layouts  3.86 us (2%)
    pallas_call x1, Pallas kernels, ascend(): pl.pallas_call(functools.partial(ascend_kernel, lines, groups, steps), na...  83 us
    pallas_call x1, Pallas kernels, descend(): pl.pallas_call(functools.partial(descend_kernel, lines, steps), name='des...  59.9 us
    pallas_call x1, Pallas kernels, call(): pl.pallas_call(kernel, name=name, grid=(steps,), in_specs=[spec(kind, arg...  55.4 us
    pallas_call x1, Pallas kernels, land(): pl.pallas_call(functools.partial(land_kernel, lines, steps), name='land',...  50.4 us

profile of v8, /device:TPU:0, one launch (start us, length us, event | category | flops | bytes accessed | tf_op | source)
XLA Modules:
  0.0 255.3 jit_solution(12920564783901344113)
XLA Ops:
  0.6 83.0 %ascend.1 = (bf16[1536,512]{1,0:T(8,128)(2,1)}, bf16[1536,512]{1,0:T(8,128)(2,1)}, bf16[1536,512]{1,0:T(8,128)(2,1)}, f32[48,1024]{1,0:T(8,128)}, bf16[1536,512]...) custom-call(bf16[1536,512]{1,0:T(8,128)(2,1)} %x_ref.3, ...), custom_call_target="tpu_custom_call" | custom-call | tf_op jit(solution)/shard_map/ascend/pallas_call | solution.py:1147
  83.6 55.4 %turn.1 = (bf16[1536,512]{1,0:T(8,128)(2,1)}, f32[1536,512]{1,0:T(8,128)}, bf16[1536,512]{1,0:T(8,128)(2,1)}, f32[1536,512]{1,0:T(8,128)}, f32[1536,512]{1,0:T(8...) custom-call(f32[1536,512]{1,0:T(8,128)} %get-tuple-element.57.x_ref, ...), custom_call_target="tpu_custom_call" | custom-call | tf_op jit(solution)/shard_map/turn/pallas_call | solution.py:557
  139.0 59.9 %descend.1 = (f32[4,8,512]{2,1,0:T(8,128)}, f32[1536,512]{1,0:T(8,128)}, bf16[1536,512]{1,0:T(8,128)(2,1)}, bf16[4,5,512,128]{3,2,1,0:T(8,128)(2,1)}, f32[8,8,512]{2,1,0:T(8,128)}, /*index=5*/f32[16,64,128]{2,1,0:T(8,128)}) custom-call(f32[1536,512]{1,0:T(8,128)} %get-tuple-element.57.x_ref, f32[1536,512]{1,0:T(8,128)} %get-tuple-element.68.dmid_in, ...), custom_call_target="tpu_custom_call" | custom-call | tf_op jit(solution)/shard_map/descend/pallas_call | solution.py:1649
  199.0 50.4 %land.1 = (f32[1536,512]{1,0:T(8,128)}, f32[8,64,128]{2,1,0:T(8,128)}, f32[20,512]{1,0:T(8,128)}, f32[4,512]{1,0:T(4,128)}) custom-call(bf16[1536,512]{1,0:T(8,128)(2,1)} %x_ref.3, bf16[1536,512]{1,0:T(8,128)(2,1)} %get-tuple-element.65.q_in, bf16[1536,512]{1,0:T(8,128)(2,1)} %get-tuple-element.66.k_in, bf16[1536,512]{1,0:T(8,128)(2,1)} %get-tuple-element.67.v_in, ...), custom_call_target="tpu_custom_call" | custom-call | tf_op jit(solution)/shard_map/land/pallas_call | solution.py:1831
  249.4 2.0 settle.1
  251.4 3.9 %copy.23 = f32[1536,512]{1,0:T(8,128)} copy(f32[1536,512]{1,0:T(8,128)} %get-tuple-element.115) | data formatting | bytes 6291456
